TPU v7x, 1024 devices: a whole 4x8x16 slice. The times are simulated.
1024 devices in a mesh: row: 64 (over z, x), col: 16 (over y, core).
Axes of the slice: x: 4, y: 8, z: 16, core: 2. Of those that a mesh axis runs over, the one named last changes fastest.
Arguments:
- upper_tiles: float32 [1024, 3, 256, 256], P(('row', 'col')), as said below
- listed_mask: int32 [1024, 3], P(('row', 'col')), may hold values from 0 to 1, as said below
Outputs:
- purified: float32 [1024, 3, 256, 256], P(('row', 'col'))
- square_traces: float32 [2], replicated
Inputs may be any that keep to these rules, and one draw needn't show every extreme that they name: `upper_tiles`: slot 0 of every tile row holds a symmetric tile. `listed_mask`: slot 0 of every tile row is listed.
All inputs are finite; a program needn't handle non-finite values.
Results may differ from a plain program's by a relative error of at most 0.0003.
Values sent between devices are 32-bit elements; how exact they have to be, the bound alone decides.
No kernel may reach another device: no remote copies, remote signals or barrier semaphores. Data moves between devices by JAX's collectives and lax.ppermute only.
A program may use at most 32 MiB of HBM per device.

v0:
```python
import jax
import jax.numpy as jnp
from jax import lax
from jax.sharding import PartitionSpec as P

STEPS = 2


def from_behind(value, axis, steps):
    count = lax.axis_size(axis)
    leading, last = (max(0, -steps), min(count, count - steps))
    return lax.ppermute(value, axis, [(source, source + steps) for source in range(leading, last)])


def fetch(position, target, own_tiles, behind_rows, ahead_rows):
    if target < position:
        found, flipped = fetch(target, position, own_tiles, behind_rows, ahead_rows)
        return (found, True)
    if position == 0:
        return (own_tiles[target], False)
    if position < 0:
        return (behind_rows[-position][target], False)
    return (ahead_rows[position][target - position], False)


def multiply(left_tile, left_flip, right_tile, right_flip):
    left_dim = 0 if left_flip else 1
    right_dim = 1 if right_flip else 0
    return lax.dot_general(
        left_tile,
        right_tile,
        (((left_dim,), (right_dim,)), ((), ())),
        precision=lax.Precision.HIGHEST,
        preferred_element_type=jnp.float32,
    )


def body(upper_tiles, listed_mask):
    rows_total = lax.axis_size(("row", "col"))
    here = lax.axis_index(("row", "col"))
    slot_count = upper_tiles.shape[1]
    tile_order = upper_tiles.shape[-1]
    span = slot_count - 1
    slots = jnp.arange(slot_count, dtype=jnp.int32)
    valid = listed_mask[0] * (here + slots < rows_total).astype(jnp.int32)
    weights = valid.astype(jnp.float32)[:, None, None]
    current = upper_tiles[0] * weights
    collected = []
    for step in range(STEPS):
        behind_rows = {}
        ahead_rows = {}
        for distance in range(1, slot_count):
            behind_rows[distance] = from_behind(current[distance:], ("row", "col"), distance)
        for distance in range(1, slot_count):
            ahead_rows[distance] = from_behind(
                current[: slot_count - distance], ("row", "col"), -distance
            )
        results = []
        for offset in range(slot_count):
            total = jnp.zeros((tile_order, tile_order), jnp.float32)
            for middle in range(offset - span, span + 1):
                left_tile, left_flip = fetch(0, middle, current, behind_rows, ahead_rows)
                right_tile, right_flip = fetch(middle, offset, current, behind_rows, ahead_rows)
                total = total + multiply(left_tile, left_flip, right_tile, right_flip)
            results.append(total)
        square = jnp.stack(results)
        local_trace = jnp.trace(results[0])
        collected.append(lax.psum(local_trace, ("row", "col")))
        if step % 2 == 0:
            current = (2.0 * current - square) * weights
        else:
            current = square * weights
    traces = jnp.stack(collected)
    return (current[None], traces / tile_order)


def solution(mesh):
    return jax.shard_map(
        body,
        mesh=mesh,
        in_specs=(P(("row", "col"), None, None, None), P(("row", "col"), None)),
        out_specs=(P(("row", "col"), None, None, None), P()),
        check_vma=False,
    )
```

profile of v0, /device:TPU:1, one launch (start us, length us, event | category | flops | bytes accessed | tf_op | source)
XLA Modules:
  0.0 194.2 jit_solution(5336767724270165523)
XLA Ops:
  0.6 0.6 copy-done.1
  1.3 1.3 bitcast_multiply_fusion
  2.6 0.1 fusion.59
  2.7 16.1 %collective-permute-start.2 = (f32[2,256,256]{2,1,0:T(8,128)S(1)}, f32[2,256,256]{2,1,0:T(8,128)S(1)}, u32[]{:S(2)}, u32[]{:S(2)}) collective-permute-start(f32[2,256,256]{2,1,0:T(8,128)S(1)} %get-tuple-element.11), channel_id=1, source_target_pairs={{1,0},{2,1},{3,2},{4,3},{5,4},{6,5},{7,6},{8,7},{9,8},{10,9},{11,1... | collective-permute-start | bytes 1572872 | tf_op jit(solution)/shard_map/ppermute | solution.py:12
  18.7 1.9 collective-permute-start.1
  20.7 1.3 collective-permute-start
  22.0 1.3 collective-permute-start.3
  23.3 0.4 fusion.34
  23.7 0.4 fusion.28
  24.1 0.4 fusion.36
  24.5 5.1 %collective-permute-done.1 = f32[2,256,256]{2,1,0:T(8,128)S(1)} collective-permute-done((f32[2,256,256]{2,1,0:T(8,128)S(1)}, f32[2,256,256]{2,1,0:T(8,128)S(1)}, u32[]{:S(2)}, u32[]{:S(2)}) %collective-permute-start.1) | collective-permute-done | bytes 524320 | tf_op jit(solution)/shard_map/ppermute | solution.py:12
  29.6 0.6 fusion.39
  30.2 2.2 %collective-permute-done = f32[1,256,256]{2,1,0:T(8,128)S(1)} collective-permute-done((f32[1,256,256]{2,1,0:T(8,128)S(1)}, f32[1,256,256]{2,1,0:T(8,128)S(1)}, u32[]{:S(2)}, u32[]{:S(2)}) %collective-permute-start) | collective-permute-done | bytes 262176 | tf_op jit(solution)/shard_map/ppermute | solution.py:12
  32.4 0.6 fusion.5
  33.0 0.4 convolution_add_fusion.10
  33.4 1.0 select_reduce_fusion.1
  34.4 0.0 collective-permute-done.2
  34.4 0.4 fusion.12
  34.8 0.4 fusion.30
  35.2 0.4 convolution_add_fusion.7
  35.6 0.0 collective-permute-done.3
  35.6 0.4 fusion.3
  36.0 0.0 copy-start
  36.0 0.6 fusion.7
  36.6 0.5 copy-done
  37.1 0.2 fusion.10
  37.3 0.1 fusion.57
  37.5 2.2 %collective-permute-start.5 = (f32[2,256,256]{2,1,0:T(8,128)S(1)}, f32[2,256,256]{2,1,0:T(8,128)S(1)}, u32[]{:S(2)}, u32[]{:S(2)}) collective-permute-start(f32[2,256,256]{2,1,0:T(8,128)S(1)} %get-tuple-element.6), channel_id=1, source_target_pairs={{0,1},{1,2},{2,3},{3,4},{4,5},{5,6},{6,7},{7,8},{8,9},{9,10},{10,1... | collective-permute-start | bytes 1572872 | tf_op jit(solution)/shard_map/ppermute | solution.py:12
  39.7 0.4 fusion.21
  40.1 3.6 %collective-permute-start.4 = (f32[1,256,256]{2,1,0:T(8,128)S(1)}, f32[1,256,256]{2,1,0:T(8,128)S(1)}, u32[]{:S(2)}, u32[]{:S(2)}) collective-permute-start(f32[1,256,256]{2,1,0:T(8,128)S(1)} %get-tuple-element.4), channel_id=1, source_target_pairs={{0,2},{1,3},{2,4},{3,5},{4,6},{5,7},{6,8},{7,9},{8,10},{9,11},{10,... | collective-permute-start | bytes 786440 | tf_op jit(solution)/shard_map/ppermute | solution.py:12
  43.6 0.4 fusion.15
  44.0 0.4 fusion.23
  44.4 2.7 %collective-permute-start.6 = (f32[2,256,256]{2,1,0:T(8,128)S(1)}, f32[2,256,256]{2,1,0:T(8,128)S(1)}, u32[]{:S(2)}, u32[]{:S(2)}) collective-permute-start(f32[2,256,256]{2,1,0:T(8,128)S(1)} %get-tuple-element.7), channel_id=1, source_target_pairs={{1,0},{2,1},{3,2},{4,3},{5,4},{6,5},{7,6},{8,7},{9,8},{10,9},{11,1... | collective-permute-start | bytes 1572872 | tf_op jit(solution)/shard_map/ppermute | solution.py:12
  47.1 1.3 collective-permute-start.7
  48.4 0.0 collective-permute-done.5
  48.4 0.6 fusion.40
  49.0 2.4 %collective-permute-done.4 = f32[1,256,256]{2,1,0:T(8,128)S(1)} collective-permute-done((f32[1,256,256]{2,1,0:T(8,128)S(1)}, f32[1,256,256]{2,1,0:T(8,128)S(1)}, u32[]{:S(2)}, u32[]{:S(2)}) %collective-permute-start.4) | collective-permute-done | bytes 262176 | tf_op jit(solution)/shard_map/ppermute | solution.py:12
  51.4 0.6 fusion.2
  52.0 0.4 convolution_add_fusion.4
  52.4 1.0 select_reduce_fusion
  53.4 134.7 %all-reduce = (f32[1]{0:T(128)}, f32[1]{0:T(128)}) all-reduce(f32[1]{0:T(128)} %bitcast.27, f32[1]{0:T(128)} %bitcast.26), channel_id=1, replica_groups=mesh['row'=64,'col'=16] {'row','col'}, use_global_device_ids=true, to_apply=%region_3.4 | all-reduce | flops 2 | bytes 16 | tf_op jit(solution)/shard_map/psum | solution.py:68
  188.1 0.4 fusion.11
  188.5 0.4 fusion.17
  188.9 1.9 maximum_multiply_fusion.1
  190.8 0.4 convolution_add_fusion.1
  191.2 1.3 fusion
  192.5 0.6 fusion.9
  193.2 1.0 maximum_multiply_fusion
  (6 shorter events, 0.1 us)
Async XLA Ops:
  0.6 0.7 copy-start.1
  2.7 31.8 %collective-permute-start.2 = (f32[2,256,256]{2,1,0:T(8,128)S(1)}, f32[2,256,256]{2,1,0:T(8,128)S(1)}, u32[]{:S(2)}, u32[]{:S(2)}) collective-permute-start(f32[2,256,256]{2,1,0:T(8,128)S(1)} %get-tuple-element.11), channel_id=1, source_target_pairs={{1,0},{2,1},{3,2},{4,3},{5,4},{6,5},{7,6},{8,7},{9,8},{10,9},{11,1... | collective-permute-start | bytes 1572872 | tf_op jit(solution)/shard_map/ppermute | solution.py:12
  18.7 10.8 %collective-permute-start.1 = (f32[2,256,256]{2,1,0:T(8,128)S(1)}, f32[2,256,256]{2,1,0:T(8,128)S(1)}, u32[]{:S(2)}, u32[]{:S(2)}) collective-permute-start(f32[2,256,256]{2,1,0:T(8,128)S(1)} %get-tuple-element.10), channel_id=1, source_target_pairs={{0,1},{1,2},{2,3},{3,4},{4,5},{5,6},{6,7},{7,8},{8,9},{9,10},{10,1... | collective-permute-start | bytes 1572872 | tf_op jit(solution)/shard_map/ppermute | solution.py:12
  20.7 11.7 %collective-permute-start = (f32[1,256,256]{2,1,0:T(8,128)S(1)}, f32[1,256,256]{2,1,0:T(8,128)S(1)}, u32[]{:S(2)}, u32[]{:S(2)}) collective-permute-start(f32[1,256,256]{2,1,0:T(8,128)S(1)} %get-tuple-element.8), channel_id=1, source_target_pairs={{0,2},{1,3},{2,4},{3,5},{4,6},{5,7},{6,8},{7,9},{8,10},{9,11},{10,... | collective-permute-start | bytes 786440 | tf_op jit(solution)/shard_map/ppermute | solution.py:12
  22.0 13.6 %collective-permute-start.3 = (f32[1,256,256]{2,1,0:T(8,128)S(1)}, f32[1,256,256]{2,1,0:T(8,128)S(1)}, u32[]{:S(2)}, u32[]{:S(2)}) collective-permute-start(f32[1,256,256]{2,1,0:T(8,128)S(1)} %get-tuple-element.9), channel_id=1, source_target_pairs={{2,0},{3,1},{4,2},{5,3},{6,4},{7,5},{8,6},{9,7},{10,8},{11,9},{12,... | collective-permute-start | bytes 786440 | tf_op jit(solution)/shard_map/ppermute | solution.py:12
  36.0 1.1 copy-start
  37.5 10.9 %collective-permute-start.5 = (f32[2,256,256]{2,1,0:T(8,128)S(1)}, f32[2,256,256]{2,1,0:T(8,128)S(1)}, u32[]{:S(2)}, u32[]{:S(2)}) collective-permute-start(f32[2,256,256]{2,1,0:T(8,128)S(1)} %get-tuple-element.6), channel_id=1, source_target_pairs={{0,1},{1,2},{2,3},{3,4},{4,5},{5,6},{6,7},{7,8},{8,9},{9,10},{10,1... | collective-permute-start | bytes 1572872 | tf_op jit(solution)/shard_map/ppermute | solution.py:12
  40.1 11.3 %collective-permute-start.4 = (f32[1,256,256]{2,1,0:T(8,128)S(1)}, f32[1,256,256]{2,1,0:T(8,128)S(1)}, u32[]{:S(2)}, u32[]{:S(2)}) collective-permute-start(f32[1,256,256]{2,1,0:T(8,128)S(1)} %get-tuple-element.4), channel_id=1, source_target_pairs={{0,2},{1,3},{2,4},{3,5},{4,6},{5,7},{6,8},{7,9},{8,10},{9,11},{10,... | collective-permute-start | bytes 786440 | tf_op jit(solution)/shard_map/ppermute | solution.py:12
  44.4 143.8 %collective-permute-start.6 = (f32[2,256,256]{2,1,0:T(8,128)S(1)}, f32[2,256,256]{2,1,0:T(8,128)S(1)}, u32[]{:S(2)}, u32[]{:S(2)}) collective-permute-start(f32[2,256,256]{2,1,0:T(8,128)S(1)} %get-tuple-element.7), channel_id=1, source_target_pairs={{1,0},{2,1},{3,2},{4,3},{5,4},{6,5},{7,6},{8,7},{9,8},{10,9},{11,1... | collective-permute-start | bytes 1572872 | tf_op jit(solution)/shard_map/ppermute | solution.py:12
  47.1 144.1 %collective-permute-start.7 = (f32[1,256,256]{2,1,0:T(8,128)S(1)}, f32[1,256,256]{2,1,0:T(8,128)}, u32[]{:S(2)}, u32[]{:S(2)}) collective-permute-start(f32[1,256,256]{2,1,0:T(8,128)S(1)} %get-tuple-element.5), channel_id=1, source_target_pairs={{2,0},{3,1},{4,2},{5,3},{6,4},{7,5},{8,6},{9,7},{10,8},{11,9},{12,... | collective-permute-start | bytes 786440 | tf_op jit(solution)/shard_map/ppermute | solution.py:12
where the time goes:
time: 195 us; the launch traced here: 194 us
  blocking collectives  135 us (69%)
  starting transfers between devices  30.3 us (16%)
  matrix products  12.8 us (7%)
  waiting for transfers between devices  9.71 us (5%)
  other arithmetic  4.31 us (2%)
    psum x1, blocking collectives, body(): collected.append(lax.psum(local_trace, ('row', 'col')))  135 us
    ppermute x8, starting transfers between devices, from_behind(): lax.ppermute(value, axis, [(source, source + steps) for source in range(l...  30.3 us
    dot_general x24, matrix products, multiply(): lax.dot_general(left_tile, right_tile, (((left_dim,), (right_dim,)), ((),...  12.8 us
    ppermute x8, waiting for transfers between devices, from_behind(): lax.ppermute(value, axis, [(source, source + steps) for source in range(l...  9.71 us
  transfers between devices with their start and end apart: 8, of which 3 were waited for; matrix products, arithmetic and copies ran while one was open for 6% of the time, Pallas kernels for 0%

commit v1 on v0

v1 whole, which is shorter than its diff:
```python
import functools

import jax
import jax.numpy as jnp
from jax import lax
from jax.experimental import pallas as pl
from jax.experimental.pallas import tpu as pltpu
from jax.sharding import PartitionSpec as P

STEPS = 2
AXES = ("row", "col")
LANES = 128


def shift(value, steps):
    count = lax.axis_size(AXES)
    first, last = (max(0, -steps), min(count, count - steps))
    return lax.ppermute(value, AXES, [(source, source + steps) for source in range(first, last)])


def split(tile):
    high = tile.astype(jnp.bfloat16)
    return (high, (tile - high.astype(jnp.float32)).astype(jnp.bfloat16))


def product(left, right, left_dim, right_dim):
    def one(a, b):
        return lax.dot_general(
            a, b, (((left_dim,), (right_dim,)), ((), ())), preferred_element_type=jnp.float32
        )

    return one(left[0], right[0]) + (one(left[0], right[1]) + one(left[1], right[0]))


def squared_norm(tiles):
    total = tiles[0] * tiles[0] + 2.0 * (tiles[1] * tiles[1] + tiles[2] * tiles[2])
    return jnp.sum(total)


def step_kernel(even, weights, own, behind1, behind2, ahead1, ahead2, out, *norms):
    own_f = [own[slot] for slot in range(3)]
    c0, c1, c2 = (split(tile) for tile in own_f)
    b10, b11 = (split(behind1[0]), split(behind1[1]))
    b22 = split(behind2[0])
    a10, a11 = (split(ahead1[0]), split(ahead1[1]))
    a20 = split(ahead2[0])
    squares = (
        product(c0, c0, 1, 0)
        + product(c1, c1, 1, 1)
        + product(c2, c2, 1, 1)
        + product(b10, b10, 0, 0)
        + product(b22, b22, 0, 0),
        product(c0, c1, 1, 0)
        + product(c1, a10, 1, 0)
        + product(c2, a11, 1, 1)
        + product(b10, b11, 0, 0),
        product(c0, c2, 1, 0) + product(c1, a11, 1, 0) + product(c2, a20, 1, 0),
    )
    fresh = []
    for slot in range(3):
        value = 2.0 * own_f[slot] - squares[slot] if even else squares[slot]
        fresh.append(value * weights[slot])
        out[slot] = fresh[slot]
    if norms:
        (pay,) = norms
        lane = lax.broadcasted_iota(jnp.int32, pay.shape, 1)
        pay[...] = jnp.where(lane == 0, squared_norm(own_f), squared_norm(fresh))


def step(even, weights, own, behind1, behind2, ahead1, ahead2, pay_rows):
    vmem = pl.BlockSpec(memory_space=pltpu.VMEM)
    shapes = [jax.ShapeDtypeStruct(own.shape, jnp.float32)]
    if pay_rows:
        shapes.append(jax.ShapeDtypeStruct((pay_rows, LANES), jnp.float32))
    order = own.shape[-1]
    return pl.pallas_call(
        functools.partial(step_kernel, even),
        out_shape=shapes,
        in_specs=[pl.BlockSpec(memory_space=pltpu.SMEM)] + [vmem] * 5,
        out_specs=[vmem] * len(shapes),
        compiler_params=pltpu.CompilerParams(vmem_limit_bytes=24 * 1024 * 1024),
        cost_estimate=pl.CostEstimate(
            flops=36 * 2 * order**3, bytes_accessed=12 * 4 * order**2, transcendentals=0
        ),
    )(weights, own, behind1, behind2, ahead1, ahead2)


def exchange(current):
    return (shift(current[1:], 1), shift(current[2:], 2), shift(current[:2], -1), shift(current[:1], -2))


def total_over(pay, axis):
    return jnp.sum(lax.all_to_all(pay, axis, 0, 0, tiled=True), axis=0, keepdims=True)


def body(upper_tiles, listed_mask):
    rows_total = lax.axis_size(AXES)
    here = lax.axis_index(AXES)
    slot_count = upper_tiles.shape[1]
    tile_order = upper_tiles.shape[-1]
    slots = jnp.arange(slot_count, dtype=jnp.int32)
    valid = listed_mask[0] * (here + slots < rows_total).astype(jnp.int32)
    weights = valid.astype(jnp.float32)
    current = upper_tiles[0] * weights[:, None, None]
    current, pay = step(True, weights, current, *exchange(current), lax.axis_size("col"))
    part = total_over(pay, "col")
    part = jnp.broadcast_to(part, (lax.axis_size("row"), LANES))
    traces = total_over(part, "row")[0, :STEPS]
    (purified,) = step(False, weights, current, *exchange(current), 0)
    return (purified[None], traces / tile_order)


def solution(mesh):
    return jax.shard_map(
        body,
        mesh=mesh,
        in_specs=(P(("row", "col"), None, None, None), P(("row", "col"), None)),
        out_specs=(P(("row", "col"), None, None, None), P()),
        check_vma=False,
    )
```

time: 195 us -> 96.7 us (0.50)
  the two profiles are of different devices: /device:TPU:1 before, /device:TPU:64 now
where the time goes in v1:
time: 96.7 us; the launch traced here: 96.3 us
  starting transfers between devices  54.9 us (57%)
  waiting for transfers between devices  21 us (22%)
  blocking collectives  10.5 us (11%)
  Pallas kernels  5 us (5%)
  local copies, waits for them, and re-layouts  2.31 us (2%)
  other arithmetic  1.84 us (2%)
    ppermute x8, starting transfers between devices, shift(): lax.ppermute(value, AXES, [(source, source + steps) for source in range(f...  27.7 us
    all_to_all x1, starting transfers between devices, total_over(): lax.all_to_all(pay, axis, 0, 0, tiled=True)  27.2 us
    ppermute x8, waiting for transfers between devices, shift(): lax.ppermute(value, AXES, [(source, source + steps) for source in range(f...  14.6 us
    all_to_all x1, blocking collectives, total_over(): lax.all_to_all(pay, axis, 0, 0, tiled=True)  10.5 us
    all_to_all x1, waiting for transfers between devices, total_over(): lax.all_to_all(pay, axis, 0, 0, tiled=True)  6.36 us
    pallas_call x2, Pallas kernels, step(): pl.pallas_call(functools.partial(step_kernel, even), out_shape=shapes, in...  5 us
  transfers between devices with their start and end apart: 9, of which 4 were waited for; matrix products, arithmetic and copies ran while one was open for 2% of the time, Pallas kernels for 0%

profile of v1, /device:TPU:64, one launch (start us, length us, event | category | flops | bytes accessed | tf_op | source)
XLA Modules:
  0.0 96.3 jit_solution(3806383119403494475)
XLA Ops:
  0.6 0.0 copy-start
  0.6 0.6 copy-done
  1.3 1.3 %bitcast_multiply_fusion.own = f32[3,256,256]{2,1,0:T(8,128)S(1)} fusion(f32[1,3,256,256]{3,2,1,0:T(8,128)} %param.2, f32[3]{0:T(128)S(1)} %fusion.weights), kind=kLoop, calls=%fused_computation | loop fusion | flops 196608 | bytes 1572876 | tf_op jit(solution)/shard_map/mul | solution.py:104
  2.6 0.1 fusion.4
  2.7 6.1 %collective-permute-start.2 = (f32[2,256,256]{2,1,0:T(8,128)S(1)}, f32[2,256,256]{2,1,0:T(8,128)S(1)}, u32[]{:S(2)}, u32[]{:S(2)}) collective-permute-start(f32[2,256,256]{2,1,0:T(8,128)S(1)} %get-tuple-element.12), channel_id=1, source_target_pairs={{1,0},{2,1},{3,2},{4,3},{5,4},{6,5},{7,6},{8,7},{9,8},{10,9},{11,1... | collective-permute-start | bytes 1572872 | tf_op jit(solution)/shard_map/ppermute | solution.py:18
  8.8 1.9 %collective-permute-start = (f32[2,256,256]{2,1,0:T(8,128)S(1)}, f32[2,256,256]{2,1,0:T(8,128)S(1)}, u32[]{:S(2)}, u32[]{:S(2)}) collective-permute-start(f32[2,256,256]{2,1,0:T(8,128)S(1)} %get-tuple-element.13), channel_id=1, source_target_pairs={{0,1},{1,2},{2,3},{3,4},{4,5},{5,6},{6,7},{7,8},{8,9},{9,10},{10,1... | collective-permute-start | bytes 1572872 | tf_op jit(solution)/shard_map/ppermute | solution.py:18
  10.7 3.3 %collective-permute-start.3 = (f32[1,256,256]{2,1,0:T(8,128)S(1)}, f32[1,256,256]{2,1,0:T(8,128)S(1)}, u32[]{:S(2)}, u32[]{:S(2)}) collective-permute-start(f32[1,256,256]{2,1,0:T(8,128)S(1)} %get-tuple-element.10), channel_id=1, source_target_pairs={{2,0},{3,1},{4,2},{5,3},{6,4},{7,5},{8,6},{9,7},{10,8},{11,9},{12,... | collective-permute-start | bytes 786440 | tf_op jit(solution)/shard_map/ppermute | solution.py:18
  14.0 2.6 %collective-permute-start.1 = (f32[1,256,256]{2,1,0:T(8,128)S(1)}, f32[1,256,256]{2,1,0:T(8,128)S(1)}, u32[]{:S(2)}, u32[]{:S(2)}) collective-permute-start(f32[1,256,256]{2,1,0:T(8,128)S(1)} %get-tuple-element.11), channel_id=1, source_target_pairs={{0,2},{1,3},{2,4},{3,5},{4,6},{5,7},{6,8},{7,9},{8,10},{9,11},{10,... | collective-permute-start | bytes 786440 | tf_op jit(solution)/shard_map/ppermute | solution.py:18
  16.6 2.4 %collective-permute-done.3.ahead2 = f32[1,256,256]{2,1,0:T(8,128)S(1)} collective-permute-done((f32[1,256,256]{2,1,0:T(8,128)S(1)}, f32[1,256,256]{2,1,0:T(8,128)S(1)}, u32[]{:S(2)}, u32[]{:S(2)}) %collective-permute-start.3) | collective-permute-done | bytes 262176 | tf_op jit(solution)/shard_map/ppermute | solution.py:18
  19.0 7.5 %collective-permute-done.1.behind2 = f32[1,256,256]{2,1,0:T(8,128)S(1)} collective-permute-done((f32[1,256,256]{2,1,0:T(8,128)S(1)}, f32[1,256,256]{2,1,0:T(8,128)S(1)}, u32[]{:S(2)}, u32[]{:S(2)}) %collective-permute-start.1) | collective-permute-done | bytes 262176 | tf_op jit(solution)/shard_map/ppermute | solution.py:18
  26.5 0.0 collective-permute-done.2.ahead1
  26.5 0.0 collective-permute-done.behind1
  26.5 2.1 %shard_map.41 = (f32[3,256,256]{2,1,0:T(8,128)S(1)}, f32[16,128]{1,0:T(8,128)S(1)}) custom-call(f32[3]{0:T(128)S(1)} %fusion.weights, f32[3,256,256]{2,1,0:T(8,128)S(1)} %bitcast_multiply_fusion.own, f32[2,256,256]{2,1,0:T(8,128)S(1)} %collective-permute-done.behind1, f32[1,256,256]{2,1,0:T(8,128)S(1)} %collective-permute-done.1.behind2, ...), custom_call_target="tpu_custom_call" | custom-call | flops 1207959552 | bytes 3145728 | tf_op jit(solution)/shard_map/pallas_call | solution.py:76
  28.6 0.1 fusion.2
  28.7 4.9 %collective-permute-start.6 = (f32[2,256,256]{2,1,0:T(8,128)S(1)}, f32[2,256,256]{2,1,0:T(8,128)S(1)}, u32[]{:S(2)}, u32[]{:S(2)}) collective-permute-start(f32[2,256,256]{2,1,0:T(8,128)S(1)} %get-tuple-element.8), channel_id=1, source_target_pairs={{1,0},{2,1},{3,2},{4,3},{5,4},{6,5},{7,6},{8,7},{9,8},{10,9},{11,1... | collective-permute-start | bytes 1572872 | tf_op jit(solution)/shard_map/ppermute | solution.py:18
  33.7 2.5 %collective-permute-start.4 = (f32[2,256,256]{2,1,0:T(8,128)S(1)}, f32[2,256,256]{2,1,0:T(8,128)S(1)}, u32[]{:S(2)}, u32[]{:S(2)}) collective-permute-start(f32[2,256,256]{2,1,0:T(8,128)S(1)} %get-tuple-element.9), channel_id=1, source_target_pairs={{0,1},{1,2},{2,3},{3,4},{4,5},{5,6},{6,7},{7,8},{8,9},{9,10},{10,1... | collective-permute-start | bytes 1572872 | tf_op jit(solution)/shard_map/ppermute | solution.py:18
  36.1 10.5 %all_to_all.15 = f32[16,1,128]{2,1,0:T(1,128)S(1)} all-to-all(f32[16,1,128]{2,1,0:T(1,128)S(1)} %bitcast.12), channel_id=1, replica_groups=mesh['row'=64,'col'=16] {'col'}, dimensions={0} | all-to-all | bytes 16384 | tf_op jit(solution)/shard_map/all_to_all | solution.py:93
  46.7 0.6 broadcast_in_dim.14
  47.3 27.2 %all-to-all-start.1 = ((f32[64,1,128]{2,1,0:T(1,128)}), f32[64,1,128]{2,1,0:T(1,128)S(1)}, u32[]{:S(2)}, u32[]{:S(2)}) async-start(f32[64,1,128]{2,1,0:T(1,128)} %broadcast_in_dim.14), calls=%async_computation.1 | async-start | bytes 65536 | tf_op jit(solution)/shard_map/all_to_all | solution.py:93
  74.5 0.8 fusion.1
  75.3 4.6 %collective-permute-start.7 = (f32[1,256,256]{2,1,0:T(8,128)}, f32[1,256,256]{2,1,0:T(8,128)S(1)}, u32[]{:S(2)}, u32[]{:S(2)}) collective-permute-start(f32[1,256,256]{2,1,0:T(8,128)} %get-tuple-element.6), channel_id=1, source_target_pairs={{2,0},{3,1},{4,2},{5,3},{6,4},{7,5},{8,6},{9,7},{10,8},{11,9},{12,... | collective-permute-start | bytes 786440 | tf_op jit(solution)/shard_map/ppermute | solution.py:18
  79.9 1.9 %collective-permute-start.5 = (f32[1,256,256]{2,1,0:T(8,128)}, f32[1,256,256]{2,1,0:T(8,128)S(1)}, u32[]{:S(2)}, u32[]{:S(2)}) collective-permute-start(f32[1,256,256]{2,1,0:T(8,128)} %get-tuple-element.7), channel_id=1, source_target_pairs={{0,2},{1,3},{2,4},{3,5},{4,6},{5,7},{6,8},{7,9},{8,10},{9,11},{10,... | collective-permute-start | bytes 786440 | tf_op jit(solution)/shard_map/ppermute | solution.py:18
  81.8 6.4 %all-to-all-done.1 = f32[64,1,128]{2,1,0:T(1,128)S(1)} async-done(((f32[64,1,128]{2,1,0:T(1,128)}), f32[64,1,128]{2,1,0:T(1,128)S(1)}, u32[]{:S(2)}, u32[]{:S(2)}) %all-to-all-start.1) | async-done | bytes 32800 | tf_op jit(solution)/shard_map/all_to_all | solution.py:93
  88.2 0.5 multiply_bitcast_fusion
  88.7 0.0 collective-permute-done.7.ahead2
  88.7 4.7 %collective-permute-done.5.behind2 = f32[1,256,256]{2,1,0:T(8,128)S(1)} collective-permute-done((f32[1,256,256]{2,1,0:T(8,128)}, f32[1,256,256]{2,1,0:T(8,128)S(1)}, u32[]{:S(2)}, u32[]{:S(2)}) %collective-permute-start.5) | collective-permute-done | bytes 262176 | tf_op jit(solution)/shard_map/ppermute | solution.py:18
  93.4 0.0 collective-permute-done.6.ahead1
  93.4 0.0 collective-permute-done.4.behind1
  93.5 2.9 %shard_map.42 = f32[3,256,256]{2,1,0:T(8,128)} custom-call(f32[3]{0:T(128)S(1)} %fusion.weights, f32[3,256,256]{2,1,0:T(8,128)S(1)} %get-tuple-element.4.own, f32[2,256,256]{2,1,0:T(8,128)S(1)} %collective-permute-done.4.behind1, f32[1,256,256]{2,1,0:T(8,128)S(1)} %collective-permute-done.5.behind2, f32[2,256,256]{2,1,0:T(8,128)S(1)} %collective-permute-done.6.ahead1, ...), custom_call_target="tpu_custom_call" | custom-call | flops 1207959552 | bytes 3145728 | tf_op jit(solution)/shard_map/pallas_call | solution.py:76
  (4 shorter events, 0.1 us)
Async XLA Ops:
  0.6 0.7 copy-start
  2.7 23.8 %collective-permute-start.2 = (f32[2,256,256]{2,1,0:T(8,128)S(1)}, f32[2,256,256]{2,1,0:T(8,128)S(1)}, u32[]{:S(2)}, u32[]{:S(2)}) collective-permute-start(f32[2,256,256]{2,1,0:T(8,128)S(1)} %get-tuple-element.12), channel_id=1, source_target_pairs={{1,0},{2,1},{3,2},{4,3},{5,4},{6,5},{7,6},{8,7},{9,8},{10,9},{11,1... | collective-permute-start | bytes 1572872 | tf_op jit(solution)/shard_map/ppermute | solution.py:18
  8.8 17.7 %collective-permute-start = (f32[2,256,256]{2,1,0:T(8,128)S(1)}, f32[2,256,256]{2,1,0:T(8,128)S(1)}, u32[]{:S(2)}, u32[]{:S(2)}) collective-permute-start(f32[2,256,256]{2,1,0:T(8,128)S(1)} %get-tuple-element.13), channel_id=1, source_target_pairs={{0,1},{1,2},{2,3},{3,4},{4,5},{5,6},{6,7},{7,8},{8,9},{9,10},{10,1... | collective-permute-start | bytes 1572872 | tf_op jit(solution)/shard_map/ppermute | solution.py:18
  10.7 8.3 %collective-permute-start.3 = (f32[1,256,256]{2,1,0:T(8,128)S(1)}, f32[1,256,256]{2,1,0:T(8,128)S(1)}, u32[]{:S(2)}, u32[]{:S(2)}) collective-permute-start(f32[1,256,256]{2,1,0:T(8,128)S(1)} %get-tuple-element.10), channel_id=1, source_target_pairs={{2,0},{3,1},{4,2},{5,3},{6,4},{7,5},{8,6},{9,7},{10,8},{11,9},{12,... | collective-permute-start | bytes 786440 | tf_op jit(solution)/shard_map/ppermute | solution.py:18
  14.0 12.5 %collective-permute-start.1 = (f32[1,256,256]{2,1,0:T(8,128)S(1)}, f32[1,256,256]{2,1,0:T(8,128)S(1)}, u32[]{:S(2)}, u32[]{:S(2)}) collective-permute-start(f32[1,256,256]{2,1,0:T(8,128)S(1)} %get-tuple-element.11), channel_id=1, source_target_pairs={{0,2},{1,3},{2,4},{3,5},{4,6},{5,7},{6,8},{7,9},{8,10},{9,11},{10,... | collective-permute-start | bytes 786440 | tf_op jit(solution)/shard_map/ppermute | solution.py:18
  28.7 64.7 %collective-permute-start.6 = (f32[2,256,256]{2,1,0:T(8,128)S(1)}, f32[2,256,256]{2,1,0:T(8,128)S(1)}, u32[]{:S(2)}, u32[]{:S(2)}) collective-permute-start(f32[2,256,256]{2,1,0:T(8,128)S(1)} %get-tuple-element.8), channel_id=1, source_target_pairs={{1,0},{2,1},{3,2},{4,3},{5,4},{6,5},{7,6},{8,7},{9,8},{10,9},{11,1... | collective-permute-start | bytes 1572872 | tf_op jit(solution)/shard_map/ppermute | solution.py:18
  33.7 59.8 %collective-permute-start.4 = (f32[2,256,256]{2,1,0:T(8,128)S(1)}, f32[2,256,256]{2,1,0:T(8,128)S(1)}, u32[]{:S(2)}, u32[]{:S(2)}) collective-permute-start(f32[2,256,256]{2,1,0:T(8,128)S(1)} %get-tuple-element.9), channel_id=1, source_target_pairs={{0,1},{1,2},{2,3},{3,4},{4,5},{5,6},{6,7},{7,8},{8,9},{9,10},{10,1... | collective-permute-start | bytes 1572872 | tf_op jit(solution)/shard_map/ppermute | solution.py:18
  47.3 40.9 %all-to-all-start.1 = ((f32[64,1,128]{2,1,0:T(1,128)}), f32[64,1,128]{2,1,0:T(1,128)S(1)}, u32[]{:S(2)}, u32[]{:S(2)}) async-start(f32[64,1,128]{2,1,0:T(1,128)} %broadcast_in_dim.14), calls=%async_computation.1 | async-start | bytes 65536 | tf_op jit(solution)/shard_map/all_to_all | solution.py:93
  75.3 13.4 %collective-permute-start.7 = (f32[1,256,256]{2,1,0:T(8,128)}, f32[1,256,256]{2,1,0:T(8,128)S(1)}, u32[]{:S(2)}, u32[]{:S(2)}) collective-permute-start(f32[1,256,256]{2,1,0:T(8,128)} %get-tuple-element.6), channel_id=1, source_target_pairs={{2,0},{3,1},{4,2},{5,3},{6,4},{7,5},{8,6},{9,7},{10,8},{11,9},{12,... | collective-permute-start | bytes 786440 | tf_op jit(solution)/shard_map/ppermute | solution.py:18
  79.9 13.6 %collective-permute-start.5 = (f32[1,256,256]{2,1,0:T(8,128)}, f32[1,256,256]{2,1,0:T(8,128)S(1)}, u32[]{:S(2)}, u32[]{:S(2)}) collective-permute-start(f32[1,256,256]{2,1,0:T(8,128)} %get-tuple-element.7), channel_id=1, source_target_pairs={{0,2},{1,3},{2,4},{3,5},{4,6},{5,7},{6,8},{7,9},{8,10},{9,11},{10,... | collective-permute-start | bytes 786440 | tf_op jit(solution)/shard_map/ppermute | solution.py:18

commit v2 on v1

--- a/solution.py
+++ b/solution.py
@@ -10,6 +10,7 @@
 STEPS = 2
 AXES = ("row", "col")
 LANES = 128
+SPREAD_COST = 10**11
 
 
 def shift(value, steps):
@@ -78,7 +79,7 @@
         out_shape=shapes,
         in_specs=[pl.BlockSpec(memory_space=pltpu.SMEM)] + [vmem] * 5,
         out_specs=[vmem] * len(shapes),
-        compiler_params=pltpu.CompilerParams(vmem_limit_bytes=24 * 1024 * 1024),
+        compiler_params=pltpu.CompilerParams(vmem_limit_bytes=12 * 1024 * 1024),
         cost_estimate=pl.CostEstimate(
             flops=36 * 2 * order**3, bytes_accessed=12 * 4 * order**2, transcendentals=0
         ),
@@ -89,8 +90,20 @@
     return (shift(current[1:], 1), shift(current[2:], 2), shift(current[:2], -1), shift(current[:1], -2))
 
 
-def total_over(pay, axis):
-    return jnp.sum(lax.all_to_all(pay, axis, 0, 0, tiled=True), axis=0, keepdims=True)
+def spread_kernel(parts, out):
+    out[...] = jnp.broadcast_to(jnp.sum(parts[...], axis=0, keepdims=True), out.shape)
+
+
+def spread(parts, rows):
+    vmem = pl.BlockSpec(memory_space=pltpu.VMEM)
+    return pl.pallas_call(
+        spread_kernel,
+        out_shape=jax.ShapeDtypeStruct((rows, LANES), jnp.float32),
+        in_specs=[vmem],
+        out_specs=vmem,
+        compiler_params=pltpu.CompilerParams(vmem_limit_bytes=1024 * 1024),
+        cost_estimate=pl.CostEstimate(flops=SPREAD_COST, bytes_accessed=0, transcendentals=0),
+    )(parts)
 
 
 def body(upper_tiles, listed_mask):
@@ -103,10 +116,11 @@
     weights = valid.astype(jnp.float32)
     current = upper_tiles[0] * weights[:, None, None]
     current, pay = step(True, weights, current, *exchange(current), lax.axis_size("col"))
-    part = total_over(pay, "col")
-    part = jnp.broadcast_to(part, (lax.axis_size("row"), LANES))
-    traces = total_over(part, "row")[0, :STEPS]
+    part = spread(lax.all_to_all(pay, "col", 0, 0, tiled=True), lax.axis_size("row"))
     (purified,) = step(False, weights, current, *exchange(current), 0)
+    gathered = lax.all_to_all(part, "row", 0, 0, tiled=True)
+    gathered, purified = lax.optimization_barrier((gathered, purified))
+    traces = jnp.sum(gathered, axis=0)[:STEPS]
     return (purified[None], traces / tile_order)
 
 

time: 96.7 us -> 94.9 us (0.981)
  the two profiles are of different devices: /device:TPU:64 before, /device:TPU:2 now
where the time goes in v2:
time: 94.9 us; the launch traced here: 94.4 us
  starting transfers between devices  69 us (73%)
  waiting for transfers between devices  15 us (16%)
  Pallas kernels  6.22 us (7%)
  other arithmetic  1.8 us (2%)
  local copies, waits for them, and re-layouts  1.66 us (2%)
    ppermute x8, starting transfers between devices, shift(): lax.ppermute(value, AXES, [(source, source + steps) for source in range(f...  34 us
    all_to_all x1, starting transfers between devices, body(): gathered = lax.all_to_all(part, 'row', 0, 0, tiled=True)  27.7 us
    all_to_all x1, waiting for transfers between devices, body(): gathered = lax.all_to_all(part, 'row', 0, 0, tiled=True)  10.7 us
    all_to_all x1, starting transfers between devices, body(): lax.all_to_all(pay, 'col', 0, 0, tiled=True)  7.34 us
    pallas_call x2, Pallas kernels, step(): pl.pallas_call(functools.partial(step_kernel, even), out_shape=shapes, in...  5.6 us
    ppermute x8, waiting for transfers between devices, shift(): lax.ppermute(value, AXES, [(source, source + steps) for source in range(f...  4.3 us
  transfers between devices with their start and end apart: 10, of which 3 were waited for; matrix products, arithmetic and copies ran while one was open for 1% of the time, Pallas kernels for 4%

profile of v2, /device:TPU:2, one launch (start us, length us, event | category | flops | bytes accessed | tf_op | source)
XLA Modules:
  0.0 94.4 jit_solution(1869436537284366631)
XLA Ops:
  0.6 0.0 copy-start
  0.6 0.6 copy-done
  1.3 1.3 %bitcast_multiply_fusion.own = f32[3,256,256]{2,1,0:T(8,128)S(1)} fusion(f32[1,3,256,256]{3,2,1,0:T(8,128)} %param.2, f32[3]{0:T(128)S(1)} %fusion.weights), kind=kLoop, calls=%fused_computation | loop fusion | flops 196608 | bytes 1572876 | tf_op jit(solution)/shard_map/mul | solution.py:117
  2.6 0.1 fusion.4
  2.7 1.9 %collective-permute-start = (f32[2,256,256]{2,1,0:T(8,128)S(1)}, f32[2,256,256]{2,1,0:T(8,128)S(1)}, u32[]{:S(2)}, u32[]{:S(2)}) collective-permute-start(f32[2,256,256]{2,1,0:T(8,128)S(1)} %get-tuple-element.17), channel_id=1, source_target_pairs={{0,1},{1,2},{2,3},{3,4},{4,5},{5,6},{6,7},{7,8},{8,9},{9,10},{10,1... | collective-permute-start | bytes 1572872 | tf_op jit(solution)/shard_map/ppermute | solution.py:19
  4.6 5.8 %collective-permute-start.2 = (f32[2,256,256]{2,1,0:T(8,128)S(1)}, f32[2,256,256]{2,1,0:T(8,128)S(1)}, u32[]{:S(2)}, u32[]{:S(2)}) collective-permute-start(f32[2,256,256]{2,1,0:T(8,128)S(1)} %get-tuple-element.16), channel_id=1, source_target_pairs={{1,0},{2,1},{3,2},{4,3},{5,4},{6,5},{7,6},{8,7},{9,8},{10,9},{11,1... | collective-permute-start | bytes 1572872 | tf_op jit(solution)/shard_map/ppermute | solution.py:19
  10.4 1.9 %collective-permute-start.1 = (f32[1,256,256]{2,1,0:T(8,128)S(1)}, f32[1,256,256]{2,1,0:T(8,128)S(1)}, u32[]{:S(2)}, u32[]{:S(2)}) collective-permute-start(f32[1,256,256]{2,1,0:T(8,128)S(1)} %get-tuple-element.15), channel_id=1, source_target_pairs={{0,2},{1,3},{2,4},{3,5},{4,6},{5,7},{6,8},{7,9},{8,10},{9,11},{10,... | collective-permute-start | bytes 786440 | tf_op jit(solution)/shard_map/ppermute | solution.py:19
  12.3 6.0 %collective-permute-start.3 = (f32[1,256,256]{2,1,0:T(8,128)S(1)}, f32[1,256,256]{2,1,0:T(8,128)S(1)}, u32[]{:S(2)}, u32[]{:S(2)}) collective-permute-start(f32[1,256,256]{2,1,0:T(8,128)S(1)} %get-tuple-element.14), channel_id=1, source_target_pairs={{2,0},{3,1},{4,2},{5,3},{6,4},{7,5},{8,6},{9,7},{10,8},{11,9},{12,... | collective-permute-start | bytes 786440 | tf_op jit(solution)/shard_map/ppermute | solution.py:19
  18.4 2.5 %collective-permute-done.1.behind2 = f32[1,256,256]{2,1,0:T(8,128)S(1)} collective-permute-done((f32[1,256,256]{2,1,0:T(8,128)S(1)}, f32[1,256,256]{2,1,0:T(8,128)S(1)}, u32[]{:S(2)}, u32[]{:S(2)}) %collective-permute-start.1) | collective-permute-done | bytes 262176 | tf_op jit(solution)/shard_map/ppermute | solution.py:19
  20.9 1.8 %collective-permute-done.3.ahead2 = f32[1,256,256]{2,1,0:T(8,128)S(1)} collective-permute-done((f32[1,256,256]{2,1,0:T(8,128)S(1)}, f32[1,256,256]{2,1,0:T(8,128)S(1)}, u32[]{:S(2)}, u32[]{:S(2)}) %collective-permute-start.3) | collective-permute-done | bytes 262176 | tf_op jit(solution)/shard_map/ppermute | solution.py:19
  22.6 0.0 collective-permute-done.behind1
  22.6 0.0 collective-permute-done.2.ahead1
  22.6 2.7 %shard_map.41 = (f32[3,256,256]{2,1,0:T(8,128)S(1)}, f32[16,128]{1,0:T(8,128)}) custom-call(f32[3]{0:T(128)S(1)} %fusion.weights, f32[3,256,256]{2,1,0:T(8,128)S(1)} %bitcast_multiply_fusion.own, f32[2,256,256]{2,1,0:T(8,128)S(1)} %collective-permute-done.behind1, f32[1,256,256]{2,1,0:T(8,128)S(1)} %collective-permute-done.1.behind2, ...), custom_call_target="tpu_custom_call" | custom-call | flops 1207959552 | bytes 3145728 | tf_op jit(solution)/shard_map/pallas_call | solution.py:77
  25.4 0.1 fusion.2
  25.5 7.3 %all-to-all-start = ((f32[16,1,128]{2,1,0:T(1,128)}), f32[16,1,128]{2,1,0:T(1,128)S(1)}, u32[]{:S(2)}, u32[]{:S(2)}) async-start(f32[16,1,128]{2,1,0:T(1,128)} %bitcast.3), calls=%async_computation | async-start | bytes 16384 | tf_op jit(solution)/shard_map/all_to_all | solution.py:119
  32.8 0.8 fusion.1
  33.6 2.3 %collective-permute-start.4 = (f32[2,256,256]{2,1,0:T(8,128)S(1)}, f32[2,256,256]{2,1,0:T(8,128)S(1)}, u32[]{:S(2)}, u32[]{:S(2)}) collective-permute-start(f32[2,256,256]{2,1,0:T(8,128)S(1)} %get-tuple-element.13), channel_id=1, source_target_pairs={{0,1},{1,2},{2,3},{3,4},{4,5},{5,6},{6,7},{7,8},{8,9},{9,10},{10,1... | collective-permute-start | bytes 1572872 | tf_op jit(solution)/shard_map/ppermute | solution.py:19
  35.9 8.1 %collective-permute-start.6 = (f32[2,256,256]{2,1,0:T(8,128)S(1)}, f32[2,256,256]{2,1,0:T(8,128)S(1)}, u32[]{:S(2)}, u32[]{:S(2)}) collective-permute-start(f32[2,256,256]{2,1,0:T(8,128)S(1)} %get-tuple-element.12), channel_id=1, source_target_pairs={{1,0},{2,1},{3,2},{4,3},{5,4},{6,5},{7,6},{8,7},{9,8},{10,9},{11,1... | collective-permute-start | bytes 1572872 | tf_op jit(solution)/shard_map/ppermute | solution.py:19
  44.0 1.9 %collective-permute-start.5 = (f32[1,256,256]{2,1,0:T(8,128)}, f32[1,256,256]{2,1,0:T(8,128)S(1)}, u32[]{:S(2)}, u32[]{:S(2)}) collective-permute-start(f32[1,256,256]{2,1,0:T(8,128)} %get-tuple-element.11), channel_id=1, source_target_pairs={{0,2},{1,3},{2,4},{3,5},{4,6},{5,7},{6,8},{7,9},{8,10},{9,11},{10,... | collective-permute-start | bytes 786440 | tf_op jit(solution)/shard_map/ppermute | solution.py:19
  46.0 6.0 %collective-permute-start.7 = (f32[1,256,256]{2,1,0:T(8,128)}, f32[1,256,256]{2,1,0:T(8,128)S(1)}, u32[]{:S(2)}, u32[]{:S(2)}) collective-permute-start(f32[1,256,256]{2,1,0:T(8,128)} %get-tuple-element.10), channel_id=1, source_target_pairs={{2,0},{3,1},{4,2},{5,3},{6,4},{7,5},{8,6},{9,7},{10,8},{11,9},{12,... | collective-permute-start | bytes 786440 | tf_op jit(solution)/shard_map/ppermute | solution.py:19
  52.0 0.0 all-to-all-done
  52.0 0.6 shard_map.42
  52.6 27.7 %all-to-all-start.1 = ((f32[64,1,128]{2,1,0:T(1,128)}), f32[64,1,128]{2,1,0:T(1,128)S(1)}, u32[]{:S(2)}, u32[]{:S(2)}) async-start(f32[64,1,128]{2,1,0:T(1,128)} %bitcast.6), calls=%async_computation.1 | async-start | bytes 65536 | tf_op jit(solution)/shard_map/all_to_all | solution.py:121
  80.3 0.0 collective-permute-done.5.behind2
  80.3 0.0 collective-permute-done.7.ahead2
  80.3 0.0 collective-permute-done.4.behind1
  80.3 0.0 collective-permute-done.6.ahead1
  80.3 2.9 %shard_map.43 = f32[3,256,256]{2,1,0:T(8,128)} custom-call(f32[3]{0:T(128)S(1)} %fusion.weights, f32[3,256,256]{2,1,0:T(8,128)S(1)} %get-tuple-element.7.own, f32[2,256,256]{2,1,0:T(8,128)S(1)} %collective-permute-done.4.behind1, f32[1,256,256]{2,1,0:T(8,128)S(1)} %collective-permute-done.5.behind2, f32[2,256,256]{2,1,0:T(8,128)S(1)} %collective-permute-done.6.ahead1, ...), custom_call_target="tpu_custom_call" | custom-call | flops 1207959552 | bytes 3145728 | tf_op jit(solution)/shard_map/pallas_call | solution.py:77
  83.2 10.7 %all-to-all-done.1 = f32[64,1,128]{2,1,0:T(1,128)S(1)} async-done(((f32[64,1,128]{2,1,0:T(1,128)}), f32[64,1,128]{2,1,0:T(1,128)S(1)}, u32[]{:S(2)}, u32[]{:S(2)}) %all-to-all-start.1) | async-done | bytes 32800 | tf_op jit(solution)/shard_map/all_to_all | solution.py:121
  93.9 0.5 slice_multiply_fusion
  (3 shorter events, 0.1 us)
Async XLA Ops:
  0.6 0.7 copy-start
  2.7 20.0 %collective-permute-start = (f32[2,256,256]{2,1,0:T(8,128)S(1)}, f32[2,256,256]{2,1,0:T(8,128)S(1)}, u32[]{:S(2)}, u32[]{:S(2)}) collective-permute-start(f32[2,256,256]{2,1,0:T(8,128)S(1)} %get-tuple-element.17), channel_id=1, source_target_pairs={{0,1},{1,2},{2,3},{3,4},{4,5},{5,6},{6,7},{7,8},{8,9},{9,10},{10,1... | collective-permute-start | bytes 1572872 | tf_op jit(solution)/shard_map/ppermute | solution.py:19
  4.6 18.1 %collective-permute-start.2 = (f32[2,256,256]{2,1,0:T(8,128)S(1)}, f32[2,256,256]{2,1,0:T(8,128)S(1)}, u32[]{:S(2)}, u32[]{:S(2)}) collective-permute-start(f32[2,256,256]{2,1,0:T(8,128)S(1)} %get-tuple-element.16), channel_id=1, source_target_pairs={{1,0},{2,1},{3,2},{4,3},{5,4},{6,5},{7,6},{8,7},{9,8},{10,9},{11,1... | collective-permute-start | bytes 1572872 | tf_op jit(solution)/shard_map/ppermute | solution.py:19
  10.4 10.5 %collective-permute-start.1 = (f32[1,256,256]{2,1,0:T(8,128)S(1)}, f32[1,256,256]{2,1,0:T(8,128)S(1)}, u32[]{:S(2)}, u32[]{:S(2)}) collective-permute-start(f32[1,256,256]{2,1,0:T(8,128)S(1)} %get-tuple-element.15), channel_id=1, source_target_pairs={{0,2},{1,3},{2,4},{3,5},{4,6},{5,7},{6,8},{7,9},{8,10},{9,11},{10,... | collective-permute-start | bytes 786440 | tf_op jit(solution)/shard_map/ppermute | solution.py:19
  12.3 10.3 %collective-permute-start.3 = (f32[1,256,256]{2,1,0:T(8,128)S(1)}, f32[1,256,256]{2,1,0:T(8,128)S(1)}, u32[]{:S(2)}, u32[]{:S(2)}) collective-permute-start(f32[1,256,256]{2,1,0:T(8,128)S(1)} %get-tuple-element.14), channel_id=1, source_target_pairs={{2,0},{3,1},{4,2},{5,3},{6,4},{7,5},{8,6},{9,7},{10,8},{11,9},{12,... | collective-permute-start | bytes 786440 | tf_op jit(solution)/shard_map/ppermute | solution.py:19
  25.5 26.5 %all-to-all-start = ((f32[16,1,128]{2,1,0:T(1,128)}), f32[16,1,128]{2,1,0:T(1,128)S(1)}, u32[]{:S(2)}, u32[]{:S(2)}) async-start(f32[16,1,128]{2,1,0:T(1,128)} %bitcast.3), calls=%async_computation | async-start | bytes 16384 | tf_op jit(solution)/shard_map/all_to_all | solution.py:119
  33.6 46.7 %collective-permute-start.4 = (f32[2,256,256]{2,1,0:T(8,128)S(1)}, f32[2,256,256]{2,1,0:T(8,128)S(1)}, u32[]{:S(2)}, u32[]{:S(2)}) collective-permute-start(f32[2,256,256]{2,1,0:T(8,128)S(1)} %get-tuple-element.13), channel_id=1, source_target_pairs={{0,1},{1,2},{2,3},{3,4},{4,5},{5,6},{6,7},{7,8},{8,9},{9,10},{10,1... | collective-permute-start | bytes 1572872 | tf_op jit(solution)/shard_map/ppermute | solution.py:19
  35.9 44.4 %collective-permute-start.6 = (f32[2,256,256]{2,1,0:T(8,128)S(1)}, f32[2,256,256]{2,1,0:T(8,128)S(1)}, u32[]{:S(2)}, u32[]{:S(2)}) collective-permute-start(f32[2,256,256]{2,1,0:T(8,128)S(1)} %get-tuple-element.12), channel_id=1, source_target_pairs={{1,0},{2,1},{3,2},{4,3},{5,4},{6,5},{7,6},{8,7},{9,8},{10,9},{11,1... | collective-permute-start | bytes 1572872 | tf_op jit(solution)/shard_map/ppermute | solution.py:19
  44.0 36.3 %collective-permute-start.5 = (f32[1,256,256]{2,1,0:T(8,128)}, f32[1,256,256]{2,1,0:T(8,128)S(1)}, u32[]{:S(2)}, u32[]{:S(2)}) collective-permute-start(f32[1,256,256]{2,1,0:T(8,128)} %get-tuple-element.11), channel_id=1, source_target_pairs={{0,2},{1,3},{2,4},{3,5},{4,6},{5,7},{6,8},{7,9},{8,10},{9,11},{10,... | collective-permute-start | bytes 786440 | tf_op jit(solution)/shard_map/ppermute | solution.py:19
  46.0 34.3 %collective-permute-start.7 = (f32[1,256,256]{2,1,0:T(8,128)}, f32[1,256,256]{2,1,0:T(8,128)S(1)}, u32[]{:S(2)}, u32[]{:S(2)}) collective-permute-start(f32[1,256,256]{2,1,0:T(8,128)} %get-tuple-element.10), channel_id=1, source_target_pairs={{2,0},{3,1},{4,2},{5,3},{6,4},{7,5},{8,6},{9,7},{10,8},{11,9},{12,... | collective-permute-start | bytes 786440 | tf_op jit(solution)/shard_map/ppermute | solution.py:19
  52.6 41.3 %all-to-all-start.1 = ((f32[64,1,128]{2,1,0:T(1,128)}), f32[64,1,128]{2,1,0:T(1,128)S(1)}, u32[]{:S(2)}, u32[]{:S(2)}) async-start(f32[64,1,128]{2,1,0:T(1,128)} %bitcast.6), calls=%async_computation.1 | async-start | bytes 65536 | tf_op jit(solution)/shard_map/all_to_all | solution.py:121

commit v3 on v2

v3 whole, which is shorter than its diff:
```python
import jax
import jax.numpy as jnp
from jax import lax
from jax.experimental import pallas as pl
from jax.experimental.pallas import tpu as pltpu
from jax.sharding import PartitionSpec as P

STEPS = 2
SLOTS = 3
SPAN = SLOTS - 1
AXES = ("row", "col")
LANES = 128
MARKS = 8
MIB = 1024 * 1024
SPREAD_COST = 0

VMEM = pl.BlockSpec(memory_space=pltpu.VMEM)
ANY = pl.BlockSpec(memory_space=pltpu.HBM)


def shift(value, steps):
    count = lax.axis_size(AXES)
    first, last = (max(0, -steps), min(count, count - steps))
    return lax.ppermute(value, AXES, [(source, source + steps) for source in range(first, last)])


def split(tile):
    high = tile.astype(jnp.bfloat16)
    return (high, (tile - high.astype(jnp.float32)).astype(jnp.bfloat16))


def product(left, right, left_dim, right_dim):
    def one(a, b):
        return lax.dot_general(
            a, b, (((left_dim,), (right_dim,)), ((), ())), preferred_element_type=jnp.float32
        )

    return one(left[0], right[0]) + (one(left[0], right[1]) + one(left[1], right[0]))


def square(tiles, row, column):
    total = None
    for middle in range(max(row, column) - SPAN, min(row, column) + SPAN + 1):
        left = tiles[min(row, middle), max(row, middle)]
        right = tiles[min(middle, column), max(middle, column)]
        term = product(left, right, 1 if row <= middle else 0, 0 if middle <= column else 1)
        total = term if total is None else total + term
    return total


def squared_norm(tiles):
    total = tiles[0] * tiles[0] + 2.0 * (tiles[1] * tiles[1] + tiles[2] * tiles[2])
    return jnp.sum(total)


def mask_kernel(rows_total, mask, upper, low, high, first, last):
    order = upper.shape[-1]
    here = lax.axis_index("row") * lax.axis_size("col") + lax.axis_index("col")
    weights = [
        jnp.where(here + slot < rows_total, mask[0, slot], 0).astype(jnp.float32) for slot in range(SLOTS)
    ]
    line = lax.broadcasted_iota(jnp.int32, (MARKS, order), 0)
    marks = jnp.zeros((MARKS, order), jnp.float32)
    for slot in range(SLOTS):
        marks = jnp.where(line == slot, weights[slot], marks)
    first[order:] = marks
    last[order:] = marks
    tiles = [upper[0, slot] * weights[slot] for slot in range(SLOTS)]
    for slot in range(SPAN):
        low[slot] = tiles[slot]
        high[slot] = tiles[slot + 1]
    first[:order] = tiles[0]
    last[:order] = tiles[SPAN]


def masked(mask, upper):
    order = upper.shape[-1]
    pair = jax.ShapeDtypeStruct((SPAN, order, order), jnp.float32)
    marked = jax.ShapeDtypeStruct((order + MARKS, order), jnp.float32)
    rows_total = lax.axis_size(AXES)
    return pl.pallas_call(
        lambda *refs: mask_kernel(rows_total, *refs),
        out_shape=[pair, pair, marked, marked],
        in_specs=[pl.BlockSpec(memory_space=pltpu.SMEM), VMEM],
        out_specs=[VMEM] * 4,
        compiler_params=pltpu.CompilerParams(vmem_limit_bytes=8 * MIB),
        cost_estimate=pl.CostEstimate(flops=0, bytes_accessed=36 * order**2, transcendentals=0),
    )(mask, upper)


def near_tiles(low, high, behind1, behind2, ahead1, ahead2):
    order = low.shape[-1]
    return {
        (0, 0): low[0],
        (0, 1): high[0],
        (0, 2): high[1],
        (-1, 0): behind1[0],
        (-1, 1): behind1[1],
        (-2, 0): behind2[:order],
        (1, 1): ahead1[0],
        (1, 2): ahead1[1],
        (2, 2): ahead2[:order],
    }


def first_kernel(low, high, first, behind1, behind2, ahead1, ahead2, pay):
    order = low.shape[-1]
    given = near_tiles(low, high, behind1, behind2, ahead1, ahead2)
    tiles = {place: split(tile) for place, tile in given.items()}
    marks = first[order:]
    own = [given[0, slot] for slot in range(SLOTS)]
    fresh = [(2.0 * own[slot] - square(tiles, 0, slot)) * marks[slot : slot + 1] for slot in range(SLOTS)]
    lane = lax.broadcasted_iota(jnp.int32, pay.shape, 1)
    pay[...] = jnp.where(lane == 0, squared_norm(own), squared_norm(fresh))


def second_kernel(
    low, high, first, behind1, behind2, ahead1, ahead2, *refs
):
    sources, out, buffers, arrived = (refs[:4], refs[4], refs[5:9], refs[9])
    copies = [
        pltpu.make_async_copy(source, buffer, arrived.at[index])
        for index, (source, buffer) in enumerate(zip(sources, buffers))
    ]
    for copy in copies:
        copy.start()
    order = low.shape[-1]
    given = near_tiles(low, high, behind1, behind2, ahead1, ahead2)
    for copy in copies:
        copy.wait()
    behind1_rest, behind2_rest, ahead1_rest, ahead2_rest = buffers
    given[-1, -1] = behind1_rest[:order]
    given[-2, -2], given[-2, -1] = (behind2_rest[0], behind2_rest[1])
    given[1, 3] = ahead1_rest[:order]
    given[2, 3], given[2, 4] = (ahead2_rest[0], ahead2_rest[1])
    marks = {0: first[order:], -2: behind2[order:], -1: behind1_rest[order:], 1: ahead1_rest[order:]}
    tiles = {place: split(tile) for place, tile in given.items()}
    later = {}
    for row, column in ((-2, 0), (-1, 0), (-1, 1), (0, 0), (0, 1), (0, 2), (1, 1), (1, 2), (2, 2)):
        value = 2.0 * given[row, column] - square(tiles, row, column)
        slot = column - row
        if slot:
            value = value * marks[row][slot : slot + 1]
        later[row, column] = split(value)
    for slot in range(SLOTS):
        out[slot] = square(later, 0, slot) * marks[0][slot : slot + 1]


def cost(products, order):
    return pl.CostEstimate(flops=products * 6 * order**3, bytes_accessed=48 * order**2, transcendentals=0)


def first_step(low, high, first, *near):
    return pl.pallas_call(
        first_kernel,
        out_shape=jax.ShapeDtypeStruct((lax.axis_size("col"), LANES), jnp.float32),
        in_specs=[VMEM] * 7,
        out_specs=VMEM,
        compiler_params=pltpu.CompilerParams(vmem_limit_bytes=16 * MIB),
        cost_estimate=cost(12, low.shape[-1]),
    )(low, high, first, *near)


def second_step(low, high, first, near, rest):
    order = low.shape[-1]
    return pl.pallas_call(
        second_kernel,
        out_shape=jax.ShapeDtypeStruct((SLOTS, order, order), jnp.float32),
        in_specs=[VMEM] * 7 + [ANY] * 4,
        out_specs=VMEM,
        scratch_shapes=[pltpu.VMEM(source.shape, jnp.float32) for source in rest]
        + [pltpu.SemaphoreType.DMA((len(rest),))],
        compiler_params=pltpu.CompilerParams(vmem_limit_bytes=24 * MIB),
        cost_estimate=cost(48, order),
    )(low, high, first, *near, *rest)


def spread_kernel(parts, out):
    out[...] = jnp.broadcast_to(jnp.sum(parts[...], axis=0, keepdims=True), out.shape)


def spread(parts, rows):
    return pl.pallas_call(
        spread_kernel,
        out_shape=jax.ShapeDtypeStruct((rows, LANES), jnp.float32),
        in_specs=[VMEM],
        out_specs=VMEM,
        compiler_params=pltpu.CompilerParams(vmem_limit_bytes=MIB),
        cost_estimate=pl.CostEstimate(flops=SPREAD_COST, bytes_accessed=0, transcendentals=0),
    )(parts)


def body(upper_tiles, listed_mask):
    low, high, first, last = masked(listed_mask, upper_tiles)
    near = (shift(high, 1), shift(last, 2), shift(low, -1), shift(first, -2))
    rest = (shift(first, 1), shift(low, 2), shift(last, -1), shift(high, -2))
    pay = first_step(low, high, first, *near)
    part = spread(lax.all_to_all(pay, "col", 0, 0, tiled=True), lax.axis_size("row"))
    purified = second_step(low, high, first, near, rest)
    gathered = lax.all_to_all(part, "row", 0, 0, tiled=True)
    gathered, purified = lax.optimization_barrier((gathered, purified))
    traces = jnp.sum(gathered, axis=0)[:STEPS]
    return (purified[None], traces / upper_tiles.shape[-1])


def solution(mesh):
    return jax.shard_map(
        body,
        mesh=mesh,
        in_specs=(P(("row", "col"), None, None, None), P(("row", "col"), None)),
        out_specs=(P(("row", "col"), None, None, None), P()),
        check_vma=False,
    )
```

time: 94.9 us -> 93.8 us (0.988)
  the two profiles are of different devices: /device:TPU:2 before, /device:TPU:1 now
where the time goes in v3:
time: 93.8 us; the launch traced here: 93.3 us
  starting transfers between devices  59.6 us (64%)
  blocking collectives  10.6 us (11%)
  Pallas kernels  10.5 us (11%)
  waiting for transfers between devices  7.42 us (8%)
  local copies, waits for them, and re-layouts  3.69 us (4%)
    ppermute x8, starting transfers between devices, shift(): lax.ppermute(value, AXES, [(source, source + steps) for source in range(f...  31.5 us
    all_to_all x1, starting transfers between devices, body(): gathered = lax.all_to_all(part, 'row', 0, 0, tiled=True)  28.2 us
    all_to_all x1, blocking collectives, body(): lax.all_to_all(pay, 'col', 0, 0, tiled=True)  10.6 us
    pallas_call x1, Pallas kernels, second_step(): pl.pallas_call(second_kernel, out_shape=jax.ShapeDtypeStruct((SLOTS, orde...  7.02 us
    all_to_all x1, waiting for transfers between devices, body(): gathered = lax.all_to_all(part, 'row', 0, 0, tiled=True)  4.63 us
    unnamed x12, local copies, waits for them, and re-layouts  3.69 us
    ppermute x8, waiting for transfers between devices, shift(): lax.ppermute(value, AXES, [(source, source + steps) for source in range(f...  2.78 us
  transfers between devices with their start and end apart: 9, of which 2 were waited for; matrix products, arithmetic and copies ran while one was open for 0% of the time, Pallas kernels for 10%

profile of v3, /device:TPU:1, one launch (start us, length us, event | category | flops | bytes accessed | tf_op | source)
XLA Modules:
  0.0 93.3 jit_solution(15308508470256147942)
XLA Ops:
  0.6 0.0 copy-start
  0.6 1.1 %copy-done = f32[1,3,256,256]{3,2,1,0:T(8,128)S(1)} copy-done((f32[1,3,256,256]{3,2,1,0:T(8,128)S(1)}, f32[1,3,256,256]{3,2,1,0:T(8,128)}, u32[]{:S(2)}) %copy-start) | copy-done | bytes 786456
  1.8 0.0 copy-start.1
  1.8 0.7 copy-done.1
  2.4 1.3 %shard_map.41 = (f32[2,256,256]{2,1,0:T(8,128)S(1)}, f32[2,256,256]{2,1,0:T(8,128)S(1)}, f32[264,256]{1,0:T(8,128)S(1)}, f32[264,256]{1,0:T(8,128)}) custom-call(s32[1,3]{1,0:T(1,128)S(1)} %copy-done.1, f32[1,3,256,256]{3,2,1,0:T(8,128)S(1)} %copy-done), custom_call_target="tpu_custom_call" | custom-call | bytes 2359296 | tf_op jit(solution)/shard_map/pallas_call | solution.py:81
  3.8 16.1 %collective-permute-start.2 = (f32[2,256,256]{2,1,0:T(8,128)S(1)}, f32[2,256,256]{2,1,0:T(8,128)S(1)}, u32[]{:S(2)}, u32[]{:S(2)}) collective-permute-start(f32[2,256,256]{2,1,0:T(8,128)S(1)} %get-tuple-element.8.low), channel_id=1, source_target_pairs={{1,0},{2,1},{3,2},{4,3},{5,4},{6,5},{7,6},{8,7},{9,8},{10,9},{11,1... | collective-permute-start | bytes 1572872 | tf_op jit(solution)/shard_map/ppermute | solution.py:24
  19.8 1.3 %collective-permute-start.1 = (f32[264,256]{1,0:T(8,128)}, f32[264,256]{1,0:T(8,128)S(1)}, u32[]{:S(2)}, u32[]{:S(2)}) collective-permute-start(f32[264,256]{1,0:T(8,128)} %get-tuple-element.11), channel_id=1, source_target_pairs={{0,2},{1,3},{2,4},{3,5},{4,6},{5,7},{6,8},{7,9},{8,10},{9,11},{10,... | collective-permute-start | bytes 811016 | tf_op jit(solution)/shard_map/ppermute | solution.py:24
  21.1 1.9 %collective-permute-start = (f32[2,256,256]{2,1,0:T(8,128)S(1)}, f32[2,256,256]{2,1,0:T(8,128)S(1)}, u32[]{:S(2)}, u32[]{:S(2)}) collective-permute-start(f32[2,256,256]{2,1,0:T(8,128)S(1)} %get-tuple-element.9.high), channel_id=1, source_target_pairs={{0,1},{1,2},{2,3},{3,4},{4,5},{5,6},{6,7},{7,8},{8,9},{9,10},{10,1... | collective-permute-start | bytes 1572872 | tf_op jit(solution)/shard_map/ppermute | solution.py:24
  23.1 1.3 %collective-permute-start.3 = (f32[264,256]{1,0:T(8,128)S(1)}, f32[264,256]{1,0:T(8,128)S(1)}, u32[]{:S(2)}, u32[]{:S(2)}) collective-permute-start(f32[264,256]{1,0:T(8,128)S(1)} %get-tuple-element.10.first), channel_id=1, source_target_pairs={{2,0},{3,1},{4,2},{5,3},{6,4},{7,5},{8,6},{9,7},{10,8},{11,9},{12,... | collective-permute-start | bytes 811016 | tf_op jit(solution)/shard_map/ppermute | solution.py:24
  24.4 4.0 %collective-permute-start.5 = (f32[2,256,256]{2,1,0:T(8,128)S(1)}, f32[2,256,256]{2,1,0:T(8,128)S(1)}, u32[]{:S(2)}, u32[]{:S(2)}) collective-permute-start(f32[2,256,256]{2,1,0:T(8,128)S(1)} %get-tuple-element.8.low), channel_id=1, source_target_pairs={{0,2},{1,3},{2,4},{3,5},{4,6},{5,7},{6,8},{7,9},{8,10},{9,11},{10,... | collective-permute-start | bytes 1572872 | tf_op jit(solution)/shard_map/ppermute | solution.py:24
  28.4 0.0 collective-permute-done.1.behind2
  28.4 0.0 copy-start.2
  28.4 1.3 %collective-permute-start.7 = (f32[2,256,256]{2,1,0:T(8,128)S(1)}, f32[2,256,256]{2,1,0:T(8,128)S(1)}, u32[]{:S(2)}, u32[]{:S(2)}) collective-permute-start(f32[2,256,256]{2,1,0:T(8,128)S(1)} %get-tuple-element.9.high), channel_id=1, source_target_pairs={{2,0},{3,1},{4,2},{5,3},{6,4},{7,5},{8,6},{9,7},{10,8},{11,9},{12,... | collective-permute-start | bytes 1572872 | tf_op jit(solution)/shard_map/ppermute | solution.py:24
  29.7 2.8 %collective-permute-done.3.ahead2 = f32[264,256]{1,0:T(8,128)S(1)} collective-permute-done((f32[264,256]{1,0:T(8,128)S(1)}, f32[264,256]{1,0:T(8,128)S(1)}, u32[]{:S(2)}, u32[]{:S(2)}) %collective-permute-start.3) | collective-permute-done | bytes 270368 | tf_op jit(solution)/shard_map/ppermute | solution.py:24
  32.5 0.0 copy-start.4
  32.5 3.7 %collective-permute-start.6 = (f32[264,256]{1,0:T(8,128)}, f32[264,256]{1,0:T(8,128)}, u32[]{:S(2)}, u32[]{:S(2)}) collective-permute-start(f32[264,256]{1,0:T(8,128)} %get-tuple-element.11), channel_id=1, source_target_pairs={{1,0},{2,1},{3,2},{4,3},{5,4},{6,5},{7,6},{8,7},{9,8},{10,9},{11,1... | collective-permute-start | bytes 811016 | tf_op jit(solution)/shard_map/ppermute | solution.py:24
  36.1 0.0 collective-permute-done.2.ahead1
  36.1 1.9 %collective-permute-start.4 = (f32[264,256]{1,0:T(8,128)S(1)}, f32[264,256]{1,0:T(8,128)}, u32[]{:S(2)}, u32[]{:S(2)}) collective-permute-start(f32[264,256]{1,0:T(8,128)S(1)} %get-tuple-element.10.first), channel_id=1, source_target_pairs={{0,1},{1,2},{2,3},{3,4},{4,5},{5,6},{6,7},{7,8},{8,9},{9,10},{10,1... | collective-permute-start | bytes 811016 | tf_op jit(solution)/shard_map/ppermute | solution.py:24
  38.1 0.0 collective-permute-done.behind1
  38.1 1.6 %shard_map.42 = f32[16,128]{1,0:T(8,128)S(1)} custom-call(f32[2,256,256]{2,1,0:T(8,128)S(1)} %get-tuple-element.8.low, f32[2,256,256]{2,1,0:T(8,128)S(1)} %get-tuple-element.9.high, f32[264,256]{1,0:T(8,128)S(1)} %get-tuple-element.10.first, f32[2,256,256]{2,1,0:T(8,128)S(1)} %collective-permute-done.behind1, f32[264,256]{1,0:T(8,128)S(1)} %collective-permute-done.1.behind2, ...), custom_call_target="tpu_custom_call" | custom-call | flops 1207959552 | bytes 3145728 | tf_op jit(solution)/shard_map/pallas_call | solution.py:154
  39.7 0.0 copy-done.2
  39.7 0.0 copy-done.4
  39.7 10.6 %all_to_all.23 = f32[16,1,128]{2,1,0:T(1,128)S(1)} all-to-all(f32[16,1,128]{2,1,0:T(1,128)S(1)} %bitcast.10), channel_id=1, replica_groups=mesh['row'=64,'col'=16] {'col'}, dimensions={0} | all-to-all | bytes 16384 | tf_op jit(solution)/shard_map/all_to_all | solution.py:198
  50.3 0.6 shard_map.43
  50.9 28.2 %all-to-all-start.1 = ((f32[64,1,128]{2,1,0:T(1,128)}), f32[64,1,128]{2,1,0:T(1,128)S(1)}, u32[]{:S(2)}, u32[]{:S(2)}) async-start(f32[64,1,128]{2,1,0:T(1,128)} %bitcast.4), calls=%async_computation.1 | async-start | bytes 65536 | tf_op jit(solution)/shard_map/all_to_all | solution.py:200
  79.1 0.0 collective-permute-done.6.refs_2_
  79.1 0.0 collective-permute-done.4.refs_0_
  79.1 0.0 collective-permute-done.5.refs_1_
  79.2 0.0 collective-permute-done.7.refs_3_
  79.2 0.0 copy-start.3
  79.2 0.9 %copy-done.3 = f32[264,256]{1,0:T(8,128)S(1)} copy-done((f32[264,256]{1,0:T(8,128)S(1)}, f32[264,256]{1,0:T(8,128)}, u32[]{:S(2)}) %copy-start.3) | copy-done | bytes 270360
  80.1 0.0 copy-start.5
  80.1 1.0 %copy-done.5 = f32[264,256]{1,0:T(8,128)S(1)} copy-done((f32[264,256]{1,0:T(8,128)S(1)}, f32[264,256]{1,0:T(8,128)}, u32[]{:S(2)}) %copy-start.5) | copy-done | bytes 270360
  81.1 7.0 %shard_map.44 = f32[3,256,256]{2,1,0:T(8,128)} custom-call(f32[2,256,256]{2,1,0:T(8,128)S(1)} %get-tuple-element.8.low, f32[2,256,256]{2,1,0:T(8,128)S(1)} %get-tuple-element.9.high, f32[264,256]{1,0:T(8,128)S(1)} %get-tuple-element.10.first, f32[2,256,256]{2,1,0:T(8,128)S(1)} %collective-permute-done.behind1, f32[264,256]{1,0:T(8,128)S(1)} %copy-done.3, ...), custom_call_target="tpu_custom_call" | custom-call | flops 4831838208 | bytes 3145728 | tf_op jit(solution)/shard_map/pallas_call | solution.py:166
  88.1 4.6 %all-to-all-done.1 = f32[64,1,128]{2,1,0:T(1,128)S(1)} async-done(((f32[64,1,128]{2,1,0:T(1,128)}), f32[64,1,128]{2,1,0:T(1,128)S(1)}, u32[]{:S(2)}, u32[]{:S(2)}) %all-to-all-start.1) | async-done | bytes 32800 | tf_op jit(solution)/shard_map/all_to_all | solution.py:200
  92.8 0.5 slice_multiply_fusion
  (1 shorter events, 0.0 us)
Async XLA Ops:
  0.6 1.1 %copy-start = (f32[1,3,256,256]{3,2,1,0:T(8,128)S(1)}, f32[1,3,256,256]{3,2,1,0:T(8,128)}, u32[]{:S(2)}) copy-start(f32[1,3,256,256]{3,2,1,0:T(8,128)} %refs_1_.1) | copy-start | bytes 2359300
  1.8 0.7 copy-start.1
  3.8 32.4 %collective-permute-start.2 = (f32[2,256,256]{2,1,0:T(8,128)S(1)}, f32[2,256,256]{2,1,0:T(8,128)S(1)}, u32[]{:S(2)}, u32[]{:S(2)}) collective-permute-start(f32[2,256,256]{2,1,0:T(8,128)S(1)} %get-tuple-element.8.low), channel_id=1, source_target_pairs={{1,0},{2,1},{3,2},{4,3},{5,4},{6,5},{7,6},{8,7},{9,8},{10,9},{11,1... | collective-permute-start | bytes 1572872 | tf_op jit(solution)/shard_map/ppermute | solution.py:24
  19.8 8.6 %collective-permute-start.1 = (f32[264,256]{1,0:T(8,128)}, f32[264,256]{1,0:T(8,128)S(1)}, u32[]{:S(2)}, u32[]{:S(2)}) collective-permute-start(f32[264,256]{1,0:T(8,128)} %get-tuple-element.11), channel_id=1, source_target_pairs={{0,2},{1,3},{2,4},{3,5},{4,6},{5,7},{6,8},{7,9},{8,10},{9,11},{10,... | collective-permute-start | bytes 811016 | tf_op jit(solution)/shard_map/ppermute | solution.py:24
  21.1 16.9 %collective-permute-start = (f32[2,256,256]{2,1,0:T(8,128)S(1)}, f32[2,256,256]{2,1,0:T(8,128)S(1)}, u32[]{:S(2)}, u32[]{:S(2)}) collective-permute-start(f32[2,256,256]{2,1,0:T(8,128)S(1)} %get-tuple-element.9.high), channel_id=1, source_target_pairs={{0,1},{1,2},{2,3},{3,4},{4,5},{5,6},{6,7},{7,8},{8,9},{9,10},{10,1... | collective-permute-start | bytes 1572872 | tf_op jit(solution)/shard_map/ppermute | solution.py:24
  23.1 9.4 %collective-permute-start.3 = (f32[264,256]{1,0:T(8,128)S(1)}, f32[264,256]{1,0:T(8,128)S(1)}, u32[]{:S(2)}, u32[]{:S(2)}) collective-permute-start(f32[264,256]{1,0:T(8,128)S(1)} %get-tuple-element.10.first), channel_id=1, source_target_pairs={{2,0},{3,1},{4,2},{5,3},{6,4},{7,5},{8,6},{9,7},{10,8},{11,9},{12,... | collective-permute-start | bytes 811016 | tf_op jit(solution)/shard_map/ppermute | solution.py:24
  24.4 54.8 %collective-permute-start.5 = (f32[2,256,256]{2,1,0:T(8,128)S(1)}, f32[2,256,256]{2,1,0:T(8,128)S(1)}, u32[]{:S(2)}, u32[]{:S(2)}) collective-permute-start(f32[2,256,256]{2,1,0:T(8,128)S(1)} %get-tuple-element.8.low), channel_id=1, source_target_pairs={{0,2},{1,3},{2,4},{3,5},{4,6},{5,7},{6,8},{7,9},{8,10},{9,11},{10,... | collective-permute-start | bytes 1572872 | tf_op jit(solution)/shard_map/ppermute | solution.py:24
  28.4 11.3 %copy-start.2 = (f32[264,256]{1,0:T(8,128)}, f32[264,256]{1,0:T(8,128)S(1)}, u32[]{:S(2)}) copy-start(f32[264,256]{1,0:T(8,128)S(1)} %collective-permute-done.1.behind2) | copy-start | bytes 811012
  28.4 50.8 %collective-permute-start.7 = (f32[2,256,256]{2,1,0:T(8,128)S(1)}, f32[2,256,256]{2,1,0:T(8,128)S(1)}, u32[]{:S(2)}, u32[]{:S(2)}) collective-permute-start(f32[2,256,256]{2,1,0:T(8,128)S(1)} %get-tuple-element.9.high), channel_id=1, source_target_pairs={{2,0},{3,1},{4,2},{5,3},{6,4},{7,5},{8,6},{9,7},{10,8},{11,9},{12,... | collective-permute-start | bytes 1572872 | tf_op jit(solution)/shard_map/ppermute | solution.py:24
  32.5 7.2 %copy-start.4 = (f32[264,256]{1,0:T(8,128)}, f32[264,256]{1,0:T(8,128)S(1)}, u32[]{:S(2)}) copy-start(f32[264,256]{1,0:T(8,128)S(1)} %collective-permute-done.3.ahead2) | copy-start | bytes 811012
  32.5 46.7 %collective-permute-start.6 = (f32[264,256]{1,0:T(8,128)}, f32[264,256]{1,0:T(8,128)}, u32[]{:S(2)}, u32[]{:S(2)}) collective-permute-start(f32[264,256]{1,0:T(8,128)} %get-tuple-element.11), channel_id=1, source_target_pairs={{1,0},{2,1},{3,2},{4,3},{5,4},{6,5},{7,6},{8,7},{9,8},{10,9},{11,1... | collective-permute-start | bytes 811016 | tf_op jit(solution)/shard_map/ppermute | solution.py:24
  36.1 43.0 %collective-permute-start.4 = (f32[264,256]{1,0:T(8,128)S(1)}, f32[264,256]{1,0:T(8,128)}, u32[]{:S(2)}, u32[]{:S(2)}) collective-permute-start(f32[264,256]{1,0:T(8,128)S(1)} %get-tuple-element.10.first), channel_id=1, source_target_pairs={{0,1},{1,2},{2,3},{3,4},{4,5},{5,6},{6,7},{7,8},{8,9},{9,10},{10,1... | collective-permute-start | bytes 811016 | tf_op jit(solution)/shard_map/ppermute | solution.py:24
  50.9 41.8 %all-to-all-start.1 = ((f32[64,1,128]{2,1,0:T(1,128)}), f32[64,1,128]{2,1,0:T(1,128)S(1)}, u32[]{:S(2)}, u32[]{:S(2)}) async-start(f32[64,1,128]{2,1,0:T(1,128)} %bitcast.4), calls=%async_computation.1 | async-start | bytes 65536 | tf_op jit(solution)/shard_map/all_to_all | solution.py:200
  79.2 1.0 %copy-start.3 = (f32[264,256]{1,0:T(8,128)S(1)}, f32[264,256]{1,0:T(8,128)}, u32[]{:S(2)}) copy-start(f32[264,256]{1,0:T(8,128)} %copy-done.2) | copy-start | bytes 811012
  80.1 1.0 %copy-start.5 = (f32[264,256]{1,0:T(8,128)S(1)}, f32[264,256]{1,0:T(8,128)}, u32[]{:S(2)}) copy-start(f32[264,256]{1,0:T(8,128)} %copy-done.4) | copy-start | bytes 811012

commit v4 on v3

v4 whole, which is shorter than its diff:
```python
import jax
import jax.numpy as jnp
from jax import lax
from jax.experimental import pallas as pl
from jax.experimental.pallas import tpu as pltpu
from jax.sharding import PartitionSpec as P

STEPS = 2
SLOTS = 3
SPAN = SLOTS - 1
AXES = ("row", "col")
LANES = 128
ROW_LINES = 8
MARKS = 8
MIB = 1024 * 1024
SPREAD_COST = 10**11

VMEM = pl.BlockSpec(memory_space=pltpu.VMEM)
SMEM = pl.BlockSpec(memory_space=pltpu.SMEM)
ANY = pl.BlockSpec(memory_space=pl.ANY)

BACK = ((0, 0), (0, 1), (1, 1))
FRONT = ((0, 2), (1, 2), (1, 3))


def permute(value, first_shift, second_shift):
    count = lax.axis_size(AXES)
    moves = [(source, source + (second_shift if source % 2 else first_shift)) for source in range(count)]
    return lax.ppermute(value, AXES, [move for move in moves if 0 <= move[1] < count])


def split(tile):
    high = tile.astype(jnp.bfloat16)
    return (high, (tile - high.astype(jnp.float32)).astype(jnp.bfloat16))


def product(left, right, left_dim, right_dim):
    def one(a, b):
        return lax.dot_general(
            a, b, (((left_dim,), (right_dim,)), ((), ())), preferred_element_type=jnp.float32
        )

    return one(left[0], right[0]) + (one(left[0], right[1]) + one(left[1], right[0]))


def square(tiles, row, column):
    total = None
    for middle in range(max(row, column) - SPAN, min(row, column) + SPAN + 1):
        left = tiles[min(row, middle), max(row, middle)]
        right = tiles[min(middle, column), max(middle, column)]
        term = product(left, right, 1 if row <= middle else 0, 0 if middle <= column else 1)
        total = term if total is None else total + term
    return total


def squared_norm(tiles):
    total = 0.0
    for (row, column), tile in tiles.items():
        total = total + (1.0 if row == column else 2.0) * jnp.sum(tile * tile)
    return total


def by_place(kernel):
    second = lax.rem(lax.axis_index("col"), 2)
    for place in range(2):

        @pl.when(second == place)
        def _():
            kernel(place == 1)


def mask_kernel(rows_total, mask, upper, own, two, one):
    order = upper.shape[-1]
    here = lax.axis_index("row") * lax.axis_size("col") + lax.axis_index("col")
    weights = [
        jnp.where(here + slot < rows_total, mask[0, slot], 0).astype(jnp.float32) for slot in range(SLOTS)
    ]
    line = lax.broadcasted_iota(jnp.int32, (MARKS, order), 0)
    marks = jnp.zeros((MARKS, order), jnp.float32)
    for slot in range(SLOTS):
        marks = jnp.where(line == slot, weights[slot], marks)
    own[SLOTS * order :] = marks
    tiles = [upper[0, slot] * weights[slot] for slot in range(SLOTS)]
    for slot in range(SLOTS):
        own[slot * order : (slot + 1) * order] = tiles[slot]

    def messages(second):
        two[0], two[1] = (tiles[1], tiles[2]) if second else (tiles[0], tiles[1])
        one[...] = tiles[0] if second else tiles[2]

    by_place(messages)


def masked(mask, upper):
    order = upper.shape[-1]
    rows_total = lax.axis_size(AXES)
    return pl.pallas_call(
        lambda *refs: mask_kernel(rows_total, *refs),
        out_shape=[
            jax.ShapeDtypeStruct((SLOTS * order + MARKS, order), jnp.float32),
            jax.ShapeDtypeStruct((2, order, order), jnp.float32),
            jax.ShapeDtypeStruct((order, order), jnp.float32),
        ],
        in_specs=[SMEM, VMEM],
        out_specs=[VMEM] * 3,
        compiler_params=pltpu.CompilerParams(vmem_limit_bytes=8 * MIB),
        cost_estimate=pl.CostEstimate(flops=0, bytes_accessed=36 * order**2, transcendentals=0),
    )(mask, upper)


def first_kernel(own, partner, two, one, out, marks, pay):
    order = own.shape[-1]

    def compute(second):
        given = {}
        weights = {}
        for row, held in enumerate((partner, own) if second else (own, partner)):
            for slot in range(SLOTS):
                given[row, row + slot] = held[slot * order : (slot + 1) * order]
                weights[row, row + slot] = held[SLOTS * order + slot : SLOTS * order + slot + 1]
        before = {(row, column): tile for (row, column), tile in given.items() if row == int(second)}
        far = ((-1, 0), (-1, 1), (-2, 0)) if second else ((2, 2), (2, 3), (3, 3))
        given.update(zip(far, (two[0], two[1], one[...])))
        tiles = {place: split(tile) for place, tile in given.items()}
        after = {}
        for index, place in enumerate(BACK if second else FRONT):
            after[place] = (2.0 * given[place] - square(tiles, *place)) * weights[place]
            out[index] = after[place]
            marks[index : index + 1] = weights[place]
        lane = lax.broadcasted_iota(jnp.int32, pay.shape, 1)
        pay[...] = jnp.where(lane == 0, squared_norm(before), squared_norm(after)) / order

    by_place(compute)


def second_kernel(own, partner, far, marks, kept, sent):
    def compute(second):
        here, there = (BACK, FRONT) if second else (FRONT, BACK)
        away = [(row - 2, column - 2) if second else (row + 2, column + 2) for row, column in there]
        tiles = {}
        for places, held in ((here, own), (there, partner), (away, far)):
            for index, place in enumerate(places):
                tiles[place] = split(held[index])
        targets = [sent.at[0], sent.at[1], kept] if second else [kept, sent.at[0], sent.at[1]]
        for index, place in enumerate(here):
            targets[index][...] = square(tiles, *place) * marks[index : index + 1]

    by_place(compute)


def cost(products, order):
    return pl.CostEstimate(flops=products * 6 * order**3, bytes_accessed=48 * order**2, transcendentals=0)


def first_step(own, partner, two, one):
    order = own.shape[-1]
    return pl.pallas_call(
        first_kernel,
        out_shape=[
            jax.ShapeDtypeStruct((SLOTS, order, order), jnp.float32),
            jax.ShapeDtypeStruct((MARKS, order), jnp.float32),
            jax.ShapeDtypeStruct((lax.axis_size("col"), LANES), jnp.float32),
        ],
        in_specs=[VMEM] * 4,
        out_specs=[VMEM] * 3,
        compiler_params=pltpu.CompilerParams(vmem_limit_bytes=16 * MIB),
        cost_estimate=cost(12, order),
    )(own, partner, two, one)


def second_step(own, partner, far, marks):
    order = own.shape[-1]
    return pl.pallas_call(
        second_kernel,
        out_shape=[
            jax.ShapeDtypeStruct((order, order), jnp.float32),
            jax.ShapeDtypeStruct((2, order, order), jnp.float32),
        ],
        in_specs=[VMEM] * 4,
        out_specs=[VMEM] * 2,
        compiler_params=pltpu.CompilerParams(vmem_limit_bytes=16 * MIB),
        cost_estimate=cost(12, order),
    )(own, partner, far, marks)


def join_kernel(kept, received, out):
    second = lax.rem(lax.axis_index("col"), 2)
    out[pl.ds(second, 2)] = received[...]
    out[SPAN - SPAN * second] = kept[...]


def join(kept, received):
    order = kept.shape[-1]
    return pl.pallas_call(
        join_kernel,
        out_shape=jax.ShapeDtypeStruct((SLOTS, order, order), jnp.float32),
        in_specs=[VMEM] * 2,
        out_specs=VMEM,
        compiler_params=pltpu.CompilerParams(vmem_limit_bytes=8 * MIB),
        cost_estimate=pl.CostEstimate(flops=0, bytes_accessed=24 * order**2, transcendentals=0),
    )(kept, received)


def spread_kernel(parts, out):
    total = jnp.sum(parts[...], axis=0, keepdims=True)
    line = lax.broadcasted_iota(jnp.int32, out.shape, 0)
    out[...] = jnp.where(line % ROW_LINES == 0, total, 0.0)


def spread(parts, rows):
    return pl.pallas_call(
        spread_kernel,
        out_shape=jax.ShapeDtypeStruct((rows, LANES), jnp.float32),
        in_specs=[VMEM],
        out_specs=VMEM,
        compiler_params=pltpu.CompilerParams(vmem_limit_bytes=MIB),
        cost_estimate=pl.CostEstimate(flops=SPREAD_COST, bytes_accessed=0, transcendentals=0),
    )(parts)


def body(upper_tiles, listed_mask):
    own, two, one = masked(listed_mask, upper_tiles)
    two, one, partner = (permute(two, -2, 2), permute(one, 3, -3), permute(own, 1, -1))
    fresh, marks, pay = first_step(own, partner, two, one)
    part = spread(lax.all_to_all(pay, "col", 0, 0, tiled=True), ROW_LINES * lax.axis_size("row"))
    part, marks = lax.optimization_barrier((part, marks))
    kept, sent = second_step(fresh, permute(fresh, 1, -1), permute(fresh, 3, -3), marks)
    purified = join(kept, permute(sent, 1, -1))
    gathered = lax.all_to_all(part, "row", 0, 0, tiled=True)
    gathered, purified = lax.optimization_barrier((gathered, purified))
    traces = jnp.sum(gathered[:, :STEPS], axis=0)
    return (purified[None], traces)


def solution(mesh):
    return jax.shard_map(
        body,
        mesh=mesh,
        in_specs=(P(("row", "col"), None, None, None), P(("row", "col"), None)),
        out_specs=(P(("row", "col"), None, None, None), P()),
        check_vma=False,
    )
```

time: 93.8 us -> 84.4 us (0.90)
  the two profiles are of different devices: /device:TPU:1 before, /device:TPU:24 now
where the time goes in v4:
time: 84.4 us; the launch traced here: 84 us
  starting transfers between devices  49 us (58%)
  waiting for transfers between devices  26.3 us (31%)
  Pallas kernels  5.61 us (7%)
  local copies, waits for them, and re-layouts  1.78 us (2%)
    ppermute x6, starting transfers between devices, permute(): lax.ppermute(value, AXES, [move for move in moves if 0 <= move[1] < count])  17.8 us
    all_to_all x1, waiting for transfers between devices, body(): gathered = lax.all_to_all(part, 'row', 0, 0, tiled=True)  16.8 us
    all_to_all x1, starting transfers between devices, body(): gathered = lax.all_to_all(part, 'row', 0, 0, tiled=True)  16.2 us
    all_to_all x1, starting transfers between devices, body(): lax.all_to_all(pay, 'col', 0, 0, tiled=True)  15 us
    ppermute x6, waiting for transfers between devices, permute(): lax.ppermute(value, AXES, [move for move in moves if 0 <= move[1] < count])  9.5 us
    pallas_call x1, Pallas kernels, first_step(): pl.pallas_call(first_kernel, out_shape=[jax.ShapeDtypeStruct((SLOTS, orde...  1.99 us
    unnamed x4, local copies, waits for them, and re-layouts  1.78 us
  transfers between devices with their start and end apart: 8, of which 4 were waited for; matrix products, arithmetic and copies ran while one was open for 0% of the time, Pallas kernels for 3%

profile of v4, /device:TPU:24, one launch (start us, length us, event | category | flops | bytes accessed | tf_op | source)
XLA Modules:
  0.0 84.0 jit_solution(8333360220994057861)
XLA Ops:
  0.6 0.0 copy-start
  0.6 1.1 %copy-done = f32[1,3,256,256]{3,2,1,0:T(8,128)S(1)} copy-done((f32[1,3,256,256]{3,2,1,0:T(8,128)S(1)}, f32[1,3,256,256]{3,2,1,0:T(8,128)}, u32[]{:S(2)}) %copy-start) | copy-done | bytes 786456
  1.8 0.0 copy-start.1
  1.8 0.7 copy-done.1
  2.4 0.7 shard_map.41
  3.1 1.9 %collective-permute-start = (f32[776,256]{1,0:T(8,128)S(1)}, f32[776,256]{1,0:T(8,128)S(1)}, u32[]{:S(2)}, u32[]{:S(2)}) collective-permute-start(f32[776,256]{1,0:T(8,128)S(1)} %get-tuple-element.14.own), channel_id=1, source_target_pairs={{0,1},{1,0},{2,3},{3,2},{4,5},{5,4},{6,7},{7,6},{8,9},{9,8},{10,11... | collective-permute-start | bytes 2383880 | tf_op jit(solution)/shard_map/ppermute | solution.py:29
  5.1 2.4 %collective-permute-start.1 = (f32[2,256,256]{2,1,0:T(8,128)S(1)}, f32[2,256,256]{2,1,0:T(8,128)S(1)}, u32[]{:S(2)}, u32[]{:S(2)}) collective-permute-start(f32[2,256,256]{2,1,0:T(8,128)S(1)} %get-tuple-element.15), channel_id=1, source_target_pairs={{1,3},{2,0},{3,5},{4,2},{5,7},{6,4},{7,9},{8,6},{9,11},{10,8},{11,... | collective-permute-start | bytes 1572872 | tf_op jit(solution)/shard_map/ppermute | solution.py:29
  7.4 4.7 %collective-permute-start.2 = (f32[256,256]{1,0:T(8,128)S(1)}, f32[256,256]{1,0:T(8,128)S(1)}, u32[]{:S(2)}, u32[]{:S(2)}) collective-permute-start(f32[256,256]{1,0:T(8,128)S(1)} %get-tuple-element.16), channel_id=1, source_target_pairs={{0,3},{2,5},{3,0},{4,7},{5,2},{6,9},{7,4},{8,11},{9,6},{10,13},{11... | collective-permute-start | bytes 786440 | tf_op jit(solution)/shard_map/ppermute | solution.py:29
  12.2 7.0 %collective-permute-done.2.one = f32[256,256]{1,0:T(8,128)S(1)} collective-permute-done((f32[256,256]{1,0:T(8,128)S(1)}, f32[256,256]{1,0:T(8,128)S(1)}, u32[]{:S(2)}, u32[]{:S(2)}) %collective-permute-start.2) | collective-permute-done | bytes 262176 | tf_op jit(solution)/shard_map/ppermute | solution.py:29
  19.2 1.0 %collective-permute-done.1.two = f32[2,256,256]{2,1,0:T(8,128)S(1)} collective-permute-done((f32[2,256,256]{2,1,0:T(8,128)S(1)}, f32[2,256,256]{2,1,0:T(8,128)S(1)}, u32[]{:S(2)}, u32[]{:S(2)}) %collective-permute-start.1) | collective-permute-done | bytes 524320 | tf_op jit(solution)/shard_map/ppermute | solution.py:29
  20.1 0.0 collective-permute-done.partner
  20.1 2.0 %shard_map.42 = (f32[3,256,256]{2,1,0:T(8,128)S(1)}, f32[8,256]{1,0:T(8,128)S(1)}, f32[16,128]{1,0:T(8,128)}) custom-call(f32[776,256]{1,0:T(8,128)S(1)} %get-tuple-element.14.own, f32[776,256]{1,0:T(8,128)S(1)} %collective-permute-done.partner, f32[2,256,256]{2,1,0:T(8,128)S(1)} %collective-permute-done.1.two, f32[256,256]{1,0:T(8,128)S(1)} %collective-permute-done.2.one), custom_call_target="tpu_custom_call" | custom-call | flops 1207959552 | bytes 3145728 | tf_op jit(solution)/shard_map/pallas_call | solution.py:157
  22.1 15.0 %all-to-all-start = ((f32[16,1,128]{2,1,0:T(1,128)}), f32[16,1,128]{2,1,0:T(1,128)S(1)}, u32[]{:S(2)}, u32[]{:S(2)}) async-start(f32[16,1,128]{2,1,0:T(1,128)} %bitcast.1), calls=%async_computation | async-start | bytes 16384 | tf_op jit(solution)/shard_map/all_to_all | solution.py:225
  37.1 4.3 %collective-permute-start.4 = (f32[3,256,256]{2,1,0:T(8,128)S(1)}, f32[3,256,256]{2,1,0:T(8,128)S(1)}, u32[]{:S(2)}, u32[]{:S(2)}) collective-permute-start(f32[3,256,256]{2,1,0:T(8,128)S(1)} %get-tuple-element.20.own), channel_id=1, source_target_pairs={{0,3},{2,5},{3,0},{4,7},{5,2},{6,9},{7,4},{8,11},{9,6},{10,13},{11... | collective-permute-start | bytes 2359304 | tf_op jit(solution)/shard_map/ppermute | solution.py:29
  41.4 1.9 %collective-permute-start.3 = (f32[3,256,256]{2,1,0:T(8,128)S(1)}, f32[3,256,256]{2,1,0:T(8,128)S(1)}, u32[]{:S(2)}, u32[]{:S(2)}) collective-permute-start(f32[3,256,256]{2,1,0:T(8,128)S(1)} %get-tuple-element.20.own), channel_id=1, source_target_pairs={{0,1},{1,0},{2,3},{3,2},{4,5},{5,4},{6,7},{7,6},{8,9},{9,8},{10,11... | collective-permute-start | bytes 2359304 | tf_op jit(solution)/shard_map/ppermute | solution.py:29
  43.4 0.0 all-to-all-done
  43.4 0.7 shard_map.43
  44.1 16.2 %all-to-all-start.1 = ((f32[64,8,128]{2,1,0:T(8,128)}), f32[64,8,128]{2,1,0:T(8,128)S(1)}, u32[]{:S(2)}, u32[]{:S(2)}) async-start(f32[64,8,128]{2,1,0:T(8,128)} %bitcast.3), calls=%async_computation.1 | async-start | bytes 524288 | tf_op jit(solution)/shard_map/all_to_all | solution.py:229
  60.3 0.0 collective-permute-done.4.far
  60.3 0.0 collective-permute-done.3.partner
  60.3 1.2 %shard_map.44 = (f32[256,256]{1,0:T(8,128)S(1)}, f32[2,256,256]{2,1,0:T(8,128)S(1)}) custom-call(f32[3,256,256]{2,1,0:T(8,128)S(1)} %get-tuple-element.20.own, f32[3,256,256]{2,1,0:T(8,128)S(1)} %collective-permute-done.3.partner, f32[3,256,256]{2,1,0:T(8,128)S(1)} %collective-permute-done.4.far, f32[8,256]{1,0:T(8,128)S(1)} %get-tuple-element.21.marks), custom_call_target="tpu_custom_call" | custom-call | flops 1207959552 | bytes 3145728 | tf_op jit(solution)/shard_map/pallas_call | solution.py:173
  61.6 2.5 %collective-permute-start.5 = (f32[2,256,256]{2,1,0:T(8,128)S(1)}, f32[2,256,256]{2,1,0:T(8,128)S(1)}, u32[]{:S(2)}, u32[]{:S(2)}) collective-permute-start(f32[2,256,256]{2,1,0:T(8,128)S(1)} %get-tuple-element.23), channel_id=1, source_target_pairs={{0,1},{1,0},{2,3},{3,2},{4,5},{5,4},{6,7},{7,6},{8,9},{9,8},{10,11... | collective-permute-start | bytes 1572872 | tf_op jit(solution)/shard_map/ppermute | solution.py:29
  64.1 1.5 %collective-permute-done.5.received = f32[2,256,256]{2,1,0:T(8,128)S(1)} collective-permute-done((f32[2,256,256]{2,1,0:T(8,128)S(1)}, f32[2,256,256]{2,1,0:T(8,128)S(1)}, u32[]{:S(2)}, u32[]{:S(2)}) %collective-permute-start.5) | collective-permute-done | bytes 524320 | tf_op jit(solution)/shard_map/ppermute | solution.py:29
  65.6 0.9 %shard_map.45 = f32[3,256,256]{2,1,0:T(8,128)} custom-call(f32[256,256]{1,0:T(8,128)S(1)} %get-tuple-element.22.kept, f32[2,256,256]{2,1,0:T(8,128)S(1)} %collective-permute-done.5.received), custom_call_target="tpu_custom_call" | custom-call | bytes 1572864 | tf_op jit(solution)/shard_map/pallas_call | solution.py:194
  66.6 16.8 %all-to-all-done.1 = f32[64,8,128]{2,1,0:T(8,128)S(1)} async-done(((f32[64,8,128]{2,1,0:T(8,128)}), f32[64,8,128]{2,1,0:T(8,128)S(1)}, u32[]{:S(2)}, u32[]{:S(2)}) %all-to-all-start.1) | async-done | bytes 262176 | tf_op jit(solution)/shard_map/all_to_all | solution.py:229
  83.4 0.6 slice_reduce_fusion
Async XLA Ops:
  0.6 1.1 %copy-start = (f32[1,3,256,256]{3,2,1,0:T(8,128)S(1)}, f32[1,3,256,256]{3,2,1,0:T(8,128)}, u32[]{:S(2)}) copy-start(f32[1,3,256,256]{3,2,1,0:T(8,128)} %refs_1_.1) | copy-start | bytes 2359300
  1.8 0.7 copy-start.1
  3.1 17.0 %collective-permute-start = (f32[776,256]{1,0:T(8,128)S(1)}, f32[776,256]{1,0:T(8,128)S(1)}, u32[]{:S(2)}, u32[]{:S(2)}) collective-permute-start(f32[776,256]{1,0:T(8,128)S(1)} %get-tuple-element.14.own), channel_id=1, source_target_pairs={{0,1},{1,0},{2,3},{3,2},{4,5},{5,4},{6,7},{7,6},{8,9},{9,8},{10,11... | collective-permute-start | bytes 2383880 | tf_op jit(solution)/shard_map/ppermute | solution.py:29
  5.1 15.1 %collective-permute-start.1 = (f32[2,256,256]{2,1,0:T(8,128)S(1)}, f32[2,256,256]{2,1,0:T(8,128)S(1)}, u32[]{:S(2)}, u32[]{:S(2)}) collective-permute-start(f32[2,256,256]{2,1,0:T(8,128)S(1)} %get-tuple-element.15), channel_id=1, source_target_pairs={{1,3},{2,0},{3,5},{4,2},{5,7},{6,4},{7,9},{8,6},{9,11},{10,8},{11,... | collective-permute-start | bytes 1572872 | tf_op jit(solution)/shard_map/ppermute | solution.py:29
  7.4 11.8 %collective-permute-start.2 = (f32[256,256]{1,0:T(8,128)S(1)}, f32[256,256]{1,0:T(8,128)S(1)}, u32[]{:S(2)}, u32[]{:S(2)}) collective-permute-start(f32[256,256]{1,0:T(8,128)S(1)} %get-tuple-element.16), channel_id=1, source_target_pairs={{0,3},{2,5},{3,0},{4,7},{5,2},{6,9},{7,4},{8,11},{9,6},{10,13},{11... | collective-permute-start | bytes 786440 | tf_op jit(solution)/shard_map/ppermute | solution.py:29
  22.1 21.2 %all-to-all-start = ((f32[16,1,128]{2,1,0:T(1,128)}), f32[16,1,128]{2,1,0:T(1,128)S(1)}, u32[]{:S(2)}, u32[]{:S(2)}) async-start(f32[16,1,128]{2,1,0:T(1,128)} %bitcast.1), calls=%async_computation | async-start | bytes 16384 | tf_op jit(solution)/shard_map/all_to_all | solution.py:225
  37.1 23.2 %collective-permute-start.4 = (f32[3,256,256]{2,1,0:T(8,128)S(1)}, f32[3,256,256]{2,1,0:T(8,128)S(1)}, u32[]{:S(2)}, u32[]{:S(2)}) collective-permute-start(f32[3,256,256]{2,1,0:T(8,128)S(1)} %get-tuple-element.20.own), channel_id=1, source_target_pairs={{0,3},{2,5},{3,0},{4,7},{5,2},{6,9},{7,4},{8,11},{9,6},{10,13},{11... | collective-permute-start | bytes 2359304 | tf_op jit(solution)/shard_map/ppermute | solution.py:29
  41.4 18.9 %collective-permute-start.3 = (f32[3,256,256]{2,1,0:T(8,128)S(1)}, f32[3,256,256]{2,1,0:T(8,128)S(1)}, u32[]{:S(2)}, u32[]{:S(2)}) collective-permute-start(f32[3,256,256]{2,1,0:T(8,128)S(1)} %get-tuple-element.20.own), channel_id=1, source_target_pairs={{0,1},{1,0},{2,3},{3,2},{4,5},{5,4},{6,7},{7,6},{8,9},{9,8},{10,11... | collective-permute-start | bytes 2359304 | tf_op jit(solution)/shard_map/ppermute | solution.py:29
  44.1 39.3 %all-to-all-start.1 = ((f32[64,8,128]{2,1,0:T(8,128)}), f32[64,8,128]{2,1,0:T(8,128)S(1)}, u32[]{:S(2)}, u32[]{:S(2)}) async-start(f32[64,8,128]{2,1,0:T(8,128)} %bitcast.3), calls=%async_computation.1 | async-start | bytes 524288 | tf_op jit(solution)/shard_map/all_to_all | solution.py:229
  61.6 4.1 %collective-permute-start.5 = (f32[2,256,256]{2,1,0:T(8,128)S(1)}, f32[2,256,256]{2,1,0:T(8,128)S(1)}, u32[]{:S(2)}, u32[]{:S(2)}) collective-permute-start(f32[2,256,256]{2,1,0:T(8,128)S(1)} %get-tuple-element.23), channel_id=1, source_target_pairs={{0,1},{1,0},{2,3},{3,2},{4,5},{5,4},{6,7},{7,6},{8,9},{9,8},{10,11... | collective-permute-start | bytes 1572872 | tf_op jit(solution)/shard_map/ppermute | solution.py:29

commit v5 on v4

--- a/solution.py
+++ b/solution.py
@@ -10,17 +10,16 @@
 SPAN = SLOTS - 1
 AXES = ("row", "col")
 LANES = 128
-ROW_LINES = 8
 MARKS = 8
 MIB = 1024 * 1024
 SPREAD_COST = 10**11
 
 VMEM = pl.BlockSpec(memory_space=pltpu.VMEM)
-SMEM = pl.BlockSpec(memory_space=pltpu.SMEM)
-ANY = pl.BlockSpec(memory_space=pl.ANY)
 
 BACK = ((0, 0), (0, 1), (1, 1))
 FRONT = ((0, 2), (1, 2), (1, 3))
+NEAR = ((0, 1), (0, 1, 2, 3))
+FAR = ((2, 3), (-2, -1))
 
 
 def permute(value, first_shift, second_shift):
@@ -43,9 +42,11 @@
     return one(left[0], right[0]) + (one(left[0], right[1]) + one(left[1], right[0]))
 
 
-def square(tiles, row, column):
+def square(tiles, row, column, chosen=None):
     total = None
     for middle in range(max(row, column) - SPAN, min(row, column) + SPAN + 1):
+        if chosen is not None and middle not in chosen:
+            continue
         left = tiles[min(row, middle), max(row, middle)]
         right = tiles[min(middle, column), max(middle, column)]
         term = product(left, right, 1 if row <= middle else 0, 0 if middle <= column else 1)
@@ -69,18 +70,14 @@
             kernel(place == 1)
 
 
-def mask_kernel(rows_total, mask, upper, own, two, one):
+def mask_kernel(weights, upper, own, two, one):
     order = upper.shape[-1]
-    here = lax.axis_index("row") * lax.axis_size("col") + lax.axis_index("col")
-    weights = [
-        jnp.where(here + slot < rows_total, mask[0, slot], 0).astype(jnp.float32) for slot in range(SLOTS)
-    ]
     line = lax.broadcasted_iota(jnp.int32, (MARKS, order), 0)
     marks = jnp.zeros((MARKS, order), jnp.float32)
     for slot in range(SLOTS):
-        marks = jnp.where(line == slot, weights[slot], marks)
+        marks = jnp.where(line == slot, weights[:, slot : slot + 1], marks)
     own[SLOTS * order :] = marks
-    tiles = [upper[0, slot] * weights[slot] for slot in range(SLOTS)]
+    tiles = [upper[0, slot] * weights[:, slot : slot + 1] for slot in range(SLOTS)]
     for slot in range(SLOTS):
         own[slot * order : (slot + 1) * order] = tiles[slot]
 
@@ -91,44 +88,64 @@
     by_place(messages)
 
 
-def masked(mask, upper):
+def masked(weights, upper):
     order = upper.shape[-1]
-    rows_total = lax.axis_size(AXES)
-    return pl.pallas_call(
-        lambda *refs: mask_kernel(rows_total, *refs),
+    return pl.pallas_call(
+        mask_kernel,
         out_shape=[
             jax.ShapeDtypeStruct((SLOTS * order + MARKS, order), jnp.float32),
             jax.ShapeDtypeStruct((2, order, order), jnp.float32),
             jax.ShapeDtypeStruct((order, order), jnp.float32),
         ],
-        in_specs=[SMEM, VMEM],
+        in_specs=[VMEM] * 2,
         out_specs=[VMEM] * 3,
         compiler_params=pltpu.CompilerParams(vmem_limit_bytes=8 * MIB),
         cost_estimate=pl.CostEstimate(flops=0, bytes_accessed=36 * order**2, transcendentals=0),
-    )(mask, upper)
-
-
-def first_kernel(own, partner, two, one, out, marks, pay):
+    )(weights, upper)
+
+
+def pair_tiles(own, partner, second):
+    order = own.shape[-1]
+    return {
+        (row, row + slot): held[slot * order : (slot + 1) * order]
+        for row, held in enumerate((partner, own) if second else (own, partner))
+        for slot in range(SLOTS)
+    }
+
+
+def near_kernel(own, partner, base, marks, norm):
     order = own.shape[-1]
 
     def compute(second):
-        given = {}
-        weights = {}
-        for row, held in enumerate((partner, own) if second else (own, partner)):
-            for slot in range(SLOTS):
-                given[row, row + slot] = held[slot * order : (slot + 1) * order]
-                weights[row, row + slot] = held[SLOTS * order + slot : SLOTS * order + slot + 1]
-        before = {(row, column): tile for (row, column), tile in given.items() if row == int(second)}
+        given = pair_tiles(own, partner, second)
+        before = {place: tile for place, tile in given.items() if place[0] == int(second)}
+        tiles = {place: split(tile) for place, tile in given.items()}
+        for index, place in enumerate(BACK if second else FRONT):
+            base[index] = 2.0 * given[place] - square(tiles, *place, chosen=NEAR[second])
+            held = partner if (place[0] == 0) == second else own
+            line = SLOTS * order + place[1] - place[0]
+            marks[index : index + 1] = held[line : line + 1]
+        norm[...] = jnp.full(norm.shape, squared_norm(before), jnp.float32)
+
+    by_place(compute)
+
+
+def first_kernel(own, partner, base, marks, norm, two, one, out, pay):
+    order = own.shape[-1]
+
+    def compute(second):
+        given = {} if second else pair_tiles(own, partner, second)
         far = ((-1, 0), (-1, 1), (-2, 0)) if second else ((2, 2), (2, 3), (3, 3))
         given.update(zip(far, (two[0], two[1], one[...])))
-        tiles = {place: split(tile) for place, tile in given.items()}
+        used = far if second else (*far, (0, 2), (1, 2), (1, 3))
+        tiles = {place: split(given[place]) for place in used}
         after = {}
         for index, place in enumerate(BACK if second else FRONT):
-            after[place] = (2.0 * given[place] - square(tiles, *place)) * weights[place]
+            rest = square(tiles, *place, chosen=FAR[second])
+            after[place] = (base[index] - rest) * marks[index : index + 1]
             out[index] = after[place]
-            marks[index : index + 1] = weights[place]
         lane = lax.broadcasted_iota(jnp.int32, pay.shape, 1)
-        pay[...] = jnp.where(lane == 0, squared_norm(before), squared_norm(after)) / order
+        pay[...] = jnp.where(lane == 0, norm[:1], squared_norm(after)) / order
 
     by_place(compute)
 
@@ -154,18 +171,28 @@
 
 def first_step(own, partner, two, one):
     order = own.shape[-1]
-    return pl.pallas_call(
+    tiles = jax.ShapeDtypeStruct((SLOTS, order, order), jnp.float32)
+    near = pl.pallas_call(
+        near_kernel,
+        out_shape=[
+            tiles,
+            jax.ShapeDtypeStruct((MARKS, order), jnp.float32),
+            jax.ShapeDtypeStruct((MARKS, LANES), jnp.float32),
+        ],
+        in_specs=[VMEM] * 2,
+        out_specs=[VMEM] * 3,
+        compiler_params=pltpu.CompilerParams(vmem_limit_bytes=12 * MIB),
+        cost_estimate=cost(9, order),
+    )(own, partner)
+    fresh, pay = pl.pallas_call(
         first_kernel,
-        out_shape=[
-            jax.ShapeDtypeStruct((SLOTS, order, order), jnp.float32),
-            jax.ShapeDtypeStruct((MARKS, order), jnp.float32),
-            jax.ShapeDtypeStruct((lax.axis_size("col"), LANES), jnp.float32),
-        ],
-        in_specs=[VMEM] * 4,
-        out_specs=[VMEM] * 3,
-        compiler_params=pltpu.CompilerParams(vmem_limit_bytes=16 * MIB),
-        cost_estimate=cost(12, order),
-    )(own, partner, two, one)
+        out_shape=[tiles, jax.ShapeDtypeStruct((lax.axis_size("col"), LANES), jnp.float32)],
+        in_specs=[VMEM] * 7,
+        out_specs=[VMEM] * 2,
+        compiler_params=pltpu.CompilerParams(vmem_limit_bytes=12 * MIB),
+        cost_estimate=cost(5, order),
+    )(own, partner, *near, two, one)
+    return fresh, near[1], pay
 
 
 def second_step(own, partner, far, marks):
@@ -203,8 +230,22 @@
 
 def spread_kernel(parts, out):
     total = jnp.sum(parts[...], axis=0, keepdims=True)
-    line = lax.broadcasted_iota(jnp.int32, out.shape, 0)
-    out[...] = jnp.where(line % ROW_LINES == 0, total, 0.0)
+    out[...] = jnp.broadcast_to(total, out.shape)
+
+
+def total_kernel(parts, out):
+    out[...] = jnp.sum(parts[...], axis=0, keepdims=True)[:, :STEPS]
+
+
+def total_of(parts):
+    return pl.pallas_call(
+        total_kernel,
+        out_shape=jax.ShapeDtypeStruct((1, STEPS), jnp.float32),
+        in_specs=[VMEM],
+        out_specs=VMEM,
+        compiler_params=pltpu.CompilerParams(vmem_limit_bytes=MIB),
+        cost_estimate=pl.CostEstimate(flops=SPREAD_COST, bytes_accessed=0, transcendentals=0),
+    )(parts)
 
 
 def spread(parts, rows):
@@ -219,16 +260,20 @@
 
 
 def body(upper_tiles, listed_mask):
-    own, two, one = masked(listed_mask, upper_tiles)
+    rows_total = lax.axis_size(AXES)
+    slots = jnp.arange(SLOTS, dtype=jnp.int32)
+    valid = listed_mask * (lax.axis_index(AXES) + slots < rows_total).astype(jnp.int32)
+    own, two, one = masked(valid.astype(jnp.float32), upper_tiles)
     two, one, partner = (permute(two, -2, 2), permute(one, 3, -3), permute(own, 1, -1))
     fresh, marks, pay = first_step(own, partner, two, one)
-    part = spread(lax.all_to_all(pay, "col", 0, 0, tiled=True), ROW_LINES * lax.axis_size("row"))
+    part = spread(lax.all_to_all(pay, "col", 0, 0, tiled=True), lax.axis_size("row"))
     part, marks = lax.optimization_barrier((part, marks))
     kept, sent = second_step(fresh, permute(fresh, 1, -1), permute(fresh, 3, -3), marks)
+    gathered = lax.all_to_all(part, "row", 0, 0, tiled=True)
+    total = total_of(gathered)
+    kept, total = lax.optimization_barrier((kept, total))
     purified = join(kept, permute(sent, 1, -1))
-    gathered = lax.all_to_all(part, "row", 0, 0, tiled=True)
-    gathered, purified = lax.optimization_barrier((gathered, purified))
-    traces = jnp.sum(gathered[:, :STEPS], axis=0)
+    traces = total[0]
     return (purified[None], traces)
 
 

time: 84.4 us -> 76.4 us (0.905)
  the two profiles are of different devices: /device:TPU:24 before, /device:TPU:1 now
where the time goes in v5:
time: 76.4 us; the launch traced here: 76 us
  starting transfers between devices  49.1 us (64%)
  waiting for transfers between devices  17 us (22%)
  Pallas kernels  7.29 us (10%)
  local copies, waits for them, and re-layouts  1.78 us (2%)
    ppermute x6, starting transfers between devices, permute(): lax.ppermute(value, AXES, [move for move in moves if 0 <= move[1] < count])  26.1 us
    all_to_all x1, starting transfers between devices, body(): gathered = lax.all_to_all(part, 'row', 0, 0, tiled=True)  16 us
    all_to_all x1, waiting for transfers between devices, body(): gathered = lax.all_to_all(part, 'row', 0, 0, tiled=True)  8.73 us
    all_to_all x1, starting transfers between devices, body(): lax.all_to_all(pay, 'col', 0, 0, tiled=True)  7.02 us
    ppermute x6, waiting for transfers between devices, permute(): lax.ppermute(value, AXES, [move for move in moves if 0 <= move[1] < count])  6.94 us
    pallas_call x1, Pallas kernels, second_step(): pl.pallas_call(second_kernel, out_shape=[jax.ShapeDtypeStruct((order, ord...  2.42 us
    unnamed x4, local copies, waits for them, and re-layouts  1.78 us
  transfers between devices with their start and end apart: 8, of which 3 were waited for; matrix products, arithmetic and copies ran while one was open for 0% of the time, Pallas kernels for 6%

profile of v5, /device:TPU:1, one launch (start us, length us, event | category | flops | bytes accessed | tf_op | source)
XLA Modules:
  0.0 76.0 jit_solution(15193838204707374778)
XLA Ops:
  0.6 0.0 copy-start.1
  0.6 0.6 copy-done.1
  1.3 0.0 copy-start
  1.3 1.1 %copy-done = f32[1,3,256,256]{3,2,1,0:T(8,128)S(1)} copy-done((f32[1,3,256,256]{3,2,1,0:T(8,128)S(1)}, f32[1,3,256,256]{3,2,1,0:T(8,128)}, u32[]{:S(2)}) %copy-start) | copy-done | bytes 786456
  2.4 0.2 shard_map.41
  2.6 16.1 %collective-permute-start = (f32[776,256]{1,0:T(8,128)S(1)}, f32[776,256]{1,0:T(8,128)S(1)}, u32[]{:S(2)}, u32[]{:S(2)}) collective-permute-start(f32[776,256]{1,0:T(8,128)S(1)} %get-tuple-element.16.own), channel_id=1, source_target_pairs={{0,1},{1,0},{2,3},{3,2},{4,5},{5,4},{6,7},{7,6},{8,9},{9,8},{10,11... | collective-permute-start | bytes 2383880 | tf_op jit(solution)/shard_map/ppermute | solution.py:28
  18.7 1.3 %collective-permute-start.1 = (f32[2,256,256]{2,1,0:T(8,128)S(1)}, f32[2,256,256]{2,1,0:T(8,128)S(1)}, u32[]{:S(2)}, u32[]{:S(2)}) collective-permute-start(f32[2,256,256]{2,1,0:T(8,128)S(1)} %get-tuple-element.20), channel_id=1, source_target_pairs={{1,3},{2,0},{3,5},{4,2},{5,7},{6,4},{7,9},{8,6},{9,11},{10,8},{11,... | collective-permute-start | bytes 1572872 | tf_op jit(solution)/shard_map/ppermute | solution.py:28
  20.1 0.7 collective-permute-start.2
  20.7 0.0 collective-permute-done.partner
  20.7 1.2 %shard_map.42 = (f32[3,256,256]{2,1,0:T(8,128)S(1)}, f32[8,256]{1,0:T(8,128)S(1)}, f32[8,128]{1,0:T(8,128)S(1)}) custom-call(f32[776,256]{1,0:T(8,128)S(1)} %get-tuple-element.16.own, f32[776,256]{1,0:T(8,128)S(1)} %collective-permute-done.partner), custom_call_target="tpu_custom_call" | custom-call | flops 905969664 | bytes 3145728 | tf_op jit(solution)/shard_map/pallas_call | solution.py:175
  22.0 0.0 collective-permute-done.2.one
  22.0 6.9 %collective-permute-done.1.two = f32[2,256,256]{2,1,0:T(8,128)S(1)} collective-permute-done((f32[2,256,256]{2,1,0:T(8,128)S(1)}, f32[2,256,256]{2,1,0:T(8,128)S(1)}, u32[]{:S(2)}, u32[]{:S(2)}) %collective-permute-start.1) | collective-permute-done | bytes 524320 | tf_op jit(solution)/shard_map/ppermute | solution.py:28
  28.9 1.3 %shard_map.43 = (f32[3,256,256]{2,1,0:T(8,128)S(1)}, f32[16,128]{1,0:T(8,128)}) custom-call(f32[776,256]{1,0:T(8,128)S(1)} %get-tuple-element.16.own, f32[776,256]{1,0:T(8,128)S(1)} %collective-permute-done.partner, f32[3,256,256]{2,1,0:T(8,128)S(1)} %get-tuple-element.17.base, f32[8,256]{1,0:T(8,128)S(1)} %get-tuple-element.24.marks, ...), custom_call_target="tpu_custom_call" | custom-call | flops 503316480 | bytes 3145728 | tf_op jit(solution)/shard_map/pallas_call | solution.py:187
  30.3 7.0 %all-to-all-start = ((f32[16,1,128]{2,1,0:T(1,128)}), f32[16,1,128]{2,1,0:T(1,128)S(1)}, u32[]{:S(2)}, u32[]{:S(2)}) async-start(f32[16,1,128]{2,1,0:T(1,128)} %bitcast.1), calls=%async_computation | async-start | bytes 16384 | tf_op jit(solution)/shard_map/all_to_all | solution.py:269
  37.3 0.7 collective-permute-start.4
  38.0 4.9 %collective-permute-start.3 = (f32[3,256,256]{2,1,0:T(8,128)S(1)}, f32[3,256,256]{2,1,0:T(8,128)S(1)}, u32[]{:S(2)}, u32[]{:S(2)}) collective-permute-start(f32[3,256,256]{2,1,0:T(8,128)S(1)} %get-tuple-element.22.own), channel_id=1, source_target_pairs={{0,1},{1,0},{2,3},{3,2},{4,5},{5,4},{6,7},{7,6},{8,9},{9,8},{10,11... | collective-permute-start | bytes 2359304 | tf_op jit(solution)/shard_map/ppermute | solution.py:28
  42.9 1.4 %all-to-all-done = f32[16,1,128]{2,1,0:T(1,128)S(1)} async-done(((f32[16,1,128]{2,1,0:T(1,128)}), f32[16,1,128]{2,1,0:T(1,128)S(1)}, u32[]{:S(2)}, u32[]{:S(2)}) %all-to-all-start) | async-done | bytes 8224 | tf_op jit(solution)/shard_map/all_to_all | solution.py:269
  44.3 0.6 shard_map.44
  44.9 16.0 %all-to-all-start.1 = ((f32[64,1,128]{2,1,0:T(1,128)}), f32[64,1,128]{2,1,0:T(1,128)S(1)}, u32[]{:S(2)}, u32[]{:S(2)}) async-start(f32[64,1,128]{2,1,0:T(1,128)} %bitcast.4), calls=%async_computation.1 | async-start | bytes 65536 | tf_op jit(solution)/shard_map/all_to_all | solution.py:272
  60.9 0.0 collective-permute-done.4.far
  60.9 0.0 collective-permute-done.3.partner
  60.9 2.4 %shard_map.45 = (f32[256,256]{1,0:T(8,128)S(1)}, f32[2,256,256]{2,1,0:T(8,128)}) custom-call(f32[3,256,256]{2,1,0:T(8,128)S(1)} %get-tuple-element.22.own, f32[3,256,256]{2,1,0:T(8,128)S(1)} %collective-permute-done.3.partner, f32[3,256,256]{2,1,0:T(8,128)S(1)} %collective-permute-done.4.far, f32[8,256]{1,0:T(8,128)S(1)} %get-tuple-element.24.marks), custom_call_target="tpu_custom_call" | custom-call | flops 1207959552 | bytes 3145728 | tf_op jit(solution)/shard_map/pallas_call | solution.py:200
  63.3 2.4 %collective-permute-start.5 = (f32[2,256,256]{2,1,0:T(8,128)}, f32[2,256,256]{2,1,0:T(8,128)S(1)}, u32[]{:S(2)}, u32[]{:S(2)}) collective-permute-start(f32[2,256,256]{2,1,0:T(8,128)} %get-tuple-element.28), channel_id=1, source_target_pairs={{0,1},{1,0},{2,3},{3,2},{4,5},{5,4},{6,7},{7,6},{8,9},{9,8},{10,11... | collective-permute-start | bytes 1572872 | tf_op jit(solution)/shard_map/ppermute | solution.py:28
  65.8 8.7 %all-to-all-done.1 = f32[64,1,128]{2,1,0:T(1,128)S(1)} async-done(((f32[64,1,128]{2,1,0:T(1,128)}), f32[64,1,128]{2,1,0:T(1,128)S(1)}, u32[]{:S(2)}, u32[]{:S(2)}) %all-to-all-start.1) | async-done | bytes 32800 | tf_op jit(solution)/shard_map/all_to_all | solution.py:272
  74.5 0.5 shard_map.46
  75.0 0.0 collective-permute-done.5.received
  75.0 0.9 %shard_map.47 = f32[3,256,256]{2,1,0:T(8,128)} custom-call(f32[256,256]{1,0:T(8,128)S(1)} %get-tuple-element.27.kept, f32[2,256,256]{2,1,0:T(8,128)S(1)} %collective-permute-done.5.received), custom_call_target="tpu_custom_call" | custom-call | bytes 1572864 | tf_op jit(solution)/shard_map/pallas_call | solution.py:221
  (1 shorter events, 0.0 us)
Async XLA Ops:
  0.6 0.7 copy-start.1
  1.3 1.1 %copy-start = (f32[1,3,256,256]{3,2,1,0:T(8,128)S(1)}, f32[1,3,256,256]{3,2,1,0:T(8,128)}, u32[]{:S(2)}) copy-start(f32[1,3,256,256]{3,2,1,0:T(8,128)} %upper.1) | copy-start | bytes 2359300
  2.6 18.1 %collective-permute-start = (f32[776,256]{1,0:T(8,128)S(1)}, f32[776,256]{1,0:T(8,128)S(1)}, u32[]{:S(2)}, u32[]{:S(2)}) collective-permute-start(f32[776,256]{1,0:T(8,128)S(1)} %get-tuple-element.16.own), channel_id=1, source_target_pairs={{0,1},{1,0},{2,3},{3,2},{4,5},{5,4},{6,7},{7,6},{8,9},{9,8},{10,11... | collective-permute-start | bytes 2383880 | tf_op jit(solution)/shard_map/ppermute | solution.py:28
  18.7 10.2 %collective-permute-start.1 = (f32[2,256,256]{2,1,0:T(8,128)S(1)}, f32[2,256,256]{2,1,0:T(8,128)S(1)}, u32[]{:S(2)}, u32[]{:S(2)}) collective-permute-start(f32[2,256,256]{2,1,0:T(8,128)S(1)} %get-tuple-element.20), channel_id=1, source_target_pairs={{1,3},{2,0},{3,5},{4,2},{5,7},{6,4},{7,9},{8,6},{9,11},{10,8},{11,... | collective-permute-start | bytes 1572872 | tf_op jit(solution)/shard_map/ppermute | solution.py:28
  20.1 1.9 %collective-permute-start.2 = (f32[256,256]{1,0:T(8,128)S(1)}, f32[256,256]{1,0:T(8,128)S(1)}, u32[]{:S(2)}, u32[]{:S(2)}) collective-permute-start(f32[256,256]{1,0:T(8,128)S(1)} %get-tuple-element.21), channel_id=1, source_target_pairs={{0,3},{2,5},{3,0},{4,7},{5,2},{6,9},{7,4},{8,11},{9,6},{10,13},{11... | collective-permute-start | bytes 786440 | tf_op jit(solution)/shard_map/ppermute | solution.py:28
  30.3 14.0 %all-to-all-start = ((f32[16,1,128]{2,1,0:T(1,128)}), f32[16,1,128]{2,1,0:T(1,128)S(1)}, u32[]{:S(2)}, u32[]{:S(2)}) async-start(f32[16,1,128]{2,1,0:T(1,128)} %bitcast.1), calls=%async_computation | async-start | bytes 16384 | tf_op jit(solution)/shard_map/all_to_all | solution.py:269
  37.3 23.6 %collective-permute-start.4 = (f32[3,256,256]{2,1,0:T(8,128)S(1)}, f32[3,256,256]{2,1,0:T(8,128)S(1)}, u32[]{:S(2)}, u32[]{:S(2)}) collective-permute-start(f32[3,256,256]{2,1,0:T(8,128)S(1)} %get-tuple-element.22.own), channel_id=1, source_target_pairs={{0,3},{2,5},{3,0},{4,7},{5,2},{6,9},{7,4},{8,11},{9,6},{10,13},{11... | collective-permute-start | bytes 2359304 | tf_op jit(solution)/shard_map/ppermute | solution.py:28
  38.0 22.9 %collective-permute-start.3 = (f32[3,256,256]{2,1,0:T(8,128)S(1)}, f32[3,256,256]{2,1,0:T(8,128)S(1)}, u32[]{:S(2)}, u32[]{:S(2)}) collective-permute-start(f32[3,256,256]{2,1,0:T(8,128)S(1)} %get-tuple-element.22.own), channel_id=1, source_target_pairs={{0,1},{1,0},{2,3},{3,2},{4,5},{5,4},{6,7},{7,6},{8,9},{9,8},{10,11... | collective-permute-start | bytes 2359304 | tf_op jit(solution)/shard_map/ppermute | solution.py:28
  44.9 29.6 %all-to-all-start.1 = ((f32[64,1,128]{2,1,0:T(1,128)}), f32[64,1,128]{2,1,0:T(1,128)S(1)}, u32[]{:S(2)}, u32[]{:S(2)}) async-start(f32[64,1,128]{2,1,0:T(1,128)} %bitcast.4), calls=%async_computation.1 | async-start | bytes 65536 | tf_op jit(solution)/shard_map/all_to_all | solution.py:272
  63.3 11.7 %collective-permute-start.5 = (f32[2,256,256]{2,1,0:T(8,128)}, f32[2,256,256]{2,1,0:T(8,128)S(1)}, u32[]{:S(2)}, u32[]{:S(2)}) collective-permute-start(f32[2,256,256]{2,1,0:T(8,128)} %get-tuple-element.28), channel_id=1, source_target_pairs={{0,1},{1,0},{2,3},{3,2},{4,5},{5,4},{6,7},{7,6},{8,9},{9,8},{10,11... | collective-permute-start | bytes 1572872 | tf_op jit(solution)/shard_map/ppermute | solution.py:28

commit v6 on v5

--- a/solution.py
+++ b/solution.py
@@ -3,12 +3,15 @@
 from jax import lax
 from jax.experimental import pallas as pl
 from jax.experimental.pallas import tpu as pltpu
+from jax.sharding import Mesh
 from jax.sharding import PartitionSpec as P
 
 STEPS = 2
 SLOTS = 3
 SPAN = SLOTS - 1
-AXES = ("row", "col")
+AXES = ("z", "x", "y", "core")
+INNER = ("x", "y", "core")
+OUTER = "z"
 LANES = 128
 MARKS = 8
 MIB = 1024 * 1024
@@ -62,7 +65,7 @@
 
 
 def by_place(kernel):
-    second = lax.rem(lax.axis_index("col"), 2)
+    second = lax.axis_index("core")
     for place in range(2):
 
         @pl.when(second == place)
@@ -186,7 +189,7 @@
     )(own, partner)
     fresh, pay = pl.pallas_call(
         first_kernel,
-        out_shape=[tiles, jax.ShapeDtypeStruct((lax.axis_size("col"), LANES), jnp.float32)],
+        out_shape=[tiles, jax.ShapeDtypeStruct((lax.axis_size(INNER), LANES), jnp.float32)],
         in_specs=[VMEM] * 7,
         out_specs=[VMEM] * 2,
         compiler_params=pltpu.CompilerParams(vmem_limit_bytes=12 * MIB),
@@ -211,7 +214,7 @@
 
 
 def join_kernel(kept, received, out):
-    second = lax.rem(lax.axis_index("col"), 2)
+    second = lax.axis_index("core")
     out[pl.ds(second, 2)] = received[...]
     out[SPAN - SPAN * second] = kept[...]
 
@@ -266,10 +269,10 @@
     own, two, one = masked(valid.astype(jnp.float32), upper_tiles)
     two, one, partner = (permute(two, -2, 2), permute(one, 3, -3), permute(own, 1, -1))
     fresh, marks, pay = first_step(own, partner, two, one)
-    part = spread(lax.all_to_all(pay, "col", 0, 0, tiled=True), lax.axis_size("row"))
+    part = spread(lax.all_to_all(pay, INNER, 0, 0, tiled=True), lax.axis_size(OUTER))
     part, marks = lax.optimization_barrier((part, marks))
     kept, sent = second_step(fresh, permute(fresh, 1, -1), permute(fresh, 3, -3), marks)
-    gathered = lax.all_to_all(part, "row", 0, 0, tiled=True)
+    gathered = lax.all_to_all(part, OUTER, 0, 0, tiled=True)
     total = total_of(gathered)
     kept, total = lax.optimization_barrier((kept, total))
     purified = join(kept, permute(sent, 1, -1))
@@ -278,10 +281,12 @@
 
 
 def solution(mesh):
+    rows, columns = mesh.devices.shape
+    parted = Mesh(mesh.devices.reshape(rows // 4, 4, columns // 2, 2), AXES)
     return jax.shard_map(
         body,
-        mesh=mesh,
-        in_specs=(P(("row", "col"), None, None, None), P(("row", "col"), None)),
-        out_specs=(P(("row", "col"), None, None, None), P()),
+        mesh=parted,
+        in_specs=(P(AXES), P(AXES)),
+        out_specs=(P(AXES), P()),
         check_vma=False,
     )

time: 76.4 us -> 75.9 us (level)
  no operation moved by 1% of the time
where the time goes in v6:
time: 75.9 us; the launch traced here: 75.5 us
  starting transfers between devices  48.6 us (64%)
  waiting for transfers between devices  17.1 us (23%)
  Pallas kernels  7.31 us (10%)
  local copies, waits for them, and re-layouts  1.78 us (2%)
  between operations  0.76 us (1%)
    ppermute x6, starting transfers between devices, permute(): lax.ppermute(value, AXES, [move for move in moves if 0 <= move[1] < count])  26.1 us
    all_to_all x1, starting transfers between devices, body(): gathered = lax.all_to_all(part, OUTER, 0, 0, tiled=True)  14.7 us
    all_to_all x1, starting transfers between devices, body(): lax.all_to_all(pay, INNER, 0, 0, tiled=True)  7.78 us
    ppermute x6, waiting for transfers between devices, permute(): lax.ppermute(value, AXES, [move for move in moves if 0 <= move[1] < count])  6.95 us
    all_to_all x1, waiting for transfers between devices, body(): gathered = lax.all_to_all(part, OUTER, 0, 0, tiled=True)  6.4 us
    all_to_all x1, waiting for transfers between devices, body(): lax.all_to_all(pay, INNER, 0, 0, tiled=True)  3.71 us
    pallas_call x1, Pallas kernels, second_step(): pl.pallas_call(second_kernel, out_shape=[jax.ShapeDtypeStruct((order, ord...  2.44 us
    unnamed x4, local copies, waits for them, and re-layouts  1.78 us
  transfers between devices with their start and end apart: 8, of which 3 were waited for; matrix products, arithmetic and copies ran while one was open for 0% of the time, Pallas kernels for 6%

profile of v6, /device:TPU:1, one launch (start us, length us, event | category | flops | bytes accessed | tf_op | source)
XLA Modules:
  0.0 75.5 jit_solution(9293230142291251956)
XLA Ops:
  0.6 0.0 copy-start.1
  0.6 0.6 copy-done.1
  1.3 0.0 copy-start
  1.3 1.1 %copy-done = f32[1,3,256,256]{3,2,1,0:T(8,128)S(1)} copy-done((f32[1,3,256,256]{3,2,1,0:T(8,128)S(1)}, f32[1,3,256,256]{3,2,1,0:T(8,128)}, u32[]{:S(2)}) %copy-start) | copy-done | bytes 786456
  2.4 0.2 shard_map.41
  2.6 16.1 %collective-permute-start = (f32[776,256]{1,0:T(8,128)S(1)}, f32[776,256]{1,0:T(8,128)S(1)}, u32[]{:S(2)}, u32[]{:S(2)}) collective-permute-start(f32[776,256]{1,0:T(8,128)S(1)} %get-tuple-element.16.own), channel_id=1, source_target_pairs={{0,1},{1,0},{2,3},{3,2},{4,5},{5,4},{6,7},{7,6},{8,9},{9,8},{10,11... | collective-permute-start | bytes 2383880 | tf_op jit(solution)/shard_map/ppermute | solution.py:31
  18.7 1.3 %collective-permute-start.1 = (f32[2,256,256]{2,1,0:T(8,128)S(1)}, f32[2,256,256]{2,1,0:T(8,128)S(1)}, u32[]{:S(2)}, u32[]{:S(2)}) collective-permute-start(f32[2,256,256]{2,1,0:T(8,128)S(1)} %get-tuple-element.20), channel_id=1, source_target_pairs={{1,3},{2,0},{3,5},{4,2},{5,7},{6,4},{7,9},{8,6},{9,11},{10,8},{11,... | collective-permute-start | bytes 1572872 | tf_op jit(solution)/shard_map/ppermute | solution.py:31
  20.1 0.7 collective-permute-start.2
  20.7 0.0 collective-permute-done.partner
  20.8 1.2 %shard_map.42 = (f32[3,256,256]{2,1,0:T(8,128)S(1)}, f32[8,256]{1,0:T(8,128)S(1)}, f32[8,128]{1,0:T(8,128)S(1)}) custom-call(f32[776,256]{1,0:T(8,128)S(1)} %get-tuple-element.16.own, f32[776,256]{1,0:T(8,128)S(1)} %collective-permute-done.partner), custom_call_target="tpu_custom_call" | custom-call | flops 905969664 | bytes 3145728 | tf_op jit(solution)/shard_map/pallas_call | solution.py:178
  22.0 0.0 collective-permute-done.2.one
  22.0 6.9 %collective-permute-done.1.two = f32[2,256,256]{2,1,0:T(8,128)S(1)} collective-permute-done((f32[2,256,256]{2,1,0:T(8,128)S(1)}, f32[2,256,256]{2,1,0:T(8,128)S(1)}, u32[]{:S(2)}, u32[]{:S(2)}) %collective-permute-start.1) | collective-permute-done | bytes 524320 | tf_op jit(solution)/shard_map/ppermute | solution.py:31
  28.9 1.4 %shard_map.43 = (f32[3,256,256]{2,1,0:T(8,128)S(1)}, f32[64,128]{1,0:T(8,128)}) custom-call(f32[776,256]{1,0:T(8,128)S(1)} %get-tuple-element.16.own, f32[776,256]{1,0:T(8,128)S(1)} %collective-permute-done.partner, f32[3,256,256]{2,1,0:T(8,128)S(1)} %get-tuple-element.17.base, f32[8,256]{1,0:T(8,128)S(1)} %get-tuple-element.24.marks, ...), custom_call_target="tpu_custom_call" | custom-call | flops 503316480 | bytes 3145728 | tf_op jit(solution)/shard_map/pallas_call | solution.py:190
  30.3 7.8 %all-to-all-start = ((f32[64,1,128]{2,1,0:T(1,128)}), f32[64,1,128]{2,1,0:T(1,128)S(1)}, u32[]{:S(2)}, u32[]{:S(2)}) async-start(f32[64,1,128]{2,1,0:T(1,128)} %bitcast.1), calls=%async_computation | async-start | bytes 65536 | tf_op jit(solution)/shard_map/all_to_all | solution.py:272
  38.1 0.7 collective-permute-start.4
  38.8 4.9 %collective-permute-start.3 = (f32[3,256,256]{2,1,0:T(8,128)S(1)}, f32[3,256,256]{2,1,0:T(8,128)S(1)}, u32[]{:S(2)}, u32[]{:S(2)}) collective-permute-start(f32[3,256,256]{2,1,0:T(8,128)S(1)} %get-tuple-element.22.own), channel_id=1, source_target_pairs={{0,1},{1,0},{2,3},{3,2},{4,5},{5,4},{6,7},{7,6},{8,9},{9,8},{10,11... | collective-permute-start | bytes 2359304 | tf_op jit(solution)/shard_map/ppermute | solution.py:31
  43.7 3.7 %all-to-all-done = f32[64,1,128]{2,1,0:T(1,128)S(1)} async-done(((f32[64,1,128]{2,1,0:T(1,128)}), f32[64,1,128]{2,1,0:T(1,128)S(1)}, u32[]{:S(2)}, u32[]{:S(2)}) %all-to-all-start) | async-done | bytes 32800 | tf_op jit(solution)/shard_map/all_to_all | solution.py:272
  47.4 0.6 shard_map.44
  48.0 14.7 %all-to-all-start.1 = ((f32[16,1,128]{2,1,0:T(1,128)}), f32[16,1,128]{2,1,0:T(1,128)S(1)}, u32[]{:S(2)}, u32[]{:S(2)}) async-start(f32[16,1,128]{2,1,0:T(1,128)} %bitcast.4), calls=%async_computation.1 | async-start | bytes 16384 | tf_op jit(solution)/shard_map/all_to_all | solution.py:275
  62.8 0.0 collective-permute-done.4.far
  62.8 0.0 collective-permute-done.3.partner
  62.8 2.4 %shard_map.45 = (f32[256,256]{1,0:T(8,128)S(1)}, f32[2,256,256]{2,1,0:T(8,128)}) custom-call(f32[3,256,256]{2,1,0:T(8,128)S(1)} %get-tuple-element.22.own, f32[3,256,256]{2,1,0:T(8,128)S(1)} %collective-permute-done.3.partner, f32[3,256,256]{2,1,0:T(8,128)S(1)} %collective-permute-done.4.far, f32[8,256]{1,0:T(8,128)S(1)} %get-tuple-element.24.marks), custom_call_target="tpu_custom_call" | custom-call | flops 1207959552 | bytes 3145728 | tf_op jit(solution)/shard_map/pallas_call | solution.py:203
  65.2 2.4 %collective-permute-start.5 = (f32[2,256,256]{2,1,0:T(8,128)}, f32[2,256,256]{2,1,0:T(8,128)S(1)}, u32[]{:S(2)}, u32[]{:S(2)}) collective-permute-start(f32[2,256,256]{2,1,0:T(8,128)} %get-tuple-element.28), channel_id=1, source_target_pairs={{0,1},{1,0},{2,3},{3,2},{4,5},{5,4},{6,7},{7,6},{8,9},{9,8},{10,11... | collective-permute-start | bytes 1572872 | tf_op jit(solution)/shard_map/ppermute | solution.py:31
  67.7 6.4 %all-to-all-done.1 = f32[16,1,128]{2,1,0:T(1,128)S(1)} async-done(((f32[16,1,128]{2,1,0:T(1,128)}), f32[16,1,128]{2,1,0:T(1,128)S(1)}, u32[]{:S(2)}, u32[]{:S(2)}) %all-to-all-start.1) | async-done | bytes 8224 | tf_op jit(solution)/shard_map/all_to_all | solution.py:275
  74.1 0.5 shard_map.46
  74.6 0.0 collective-permute-done.5.received
  74.6 0.9 %shard_map.47 = f32[3,256,256]{2,1,0:T(8,128)} custom-call(f32[256,256]{1,0:T(8,128)S(1)} %get-tuple-element.27.kept, f32[2,256,256]{2,1,0:T(8,128)S(1)} %collective-permute-done.5.received), custom_call_target="tpu_custom_call" | custom-call | bytes 1572864 | tf_op jit(solution)/shard_map/pallas_call | solution.py:224
  (1 shorter events, 0.0 us)
Async XLA Ops:
  0.6 0.7 copy-start.1
  1.3 1.1 %copy-start = (f32[1,3,256,256]{3,2,1,0:T(8,128)S(1)}, f32[1,3,256,256]{3,2,1,0:T(8,128)}, u32[]{:S(2)}) copy-start(f32[1,3,256,256]{3,2,1,0:T(8,128)} %upper.1) | copy-start | bytes 2359300
  2.6 18.1 %collective-permute-start = (f32[776,256]{1,0:T(8,128)S(1)}, f32[776,256]{1,0:T(8,128)S(1)}, u32[]{:S(2)}, u32[]{:S(2)}) collective-permute-start(f32[776,256]{1,0:T(8,128)S(1)} %get-tuple-element.16.own), channel_id=1, source_target_pairs={{0,1},{1,0},{2,3},{3,2},{4,5},{5,4},{6,7},{7,6},{8,9},{9,8},{10,11... | collective-permute-start | bytes 2383880 | tf_op jit(solution)/shard_map/ppermute | solution.py:31
  18.7 10.2 %collective-permute-start.1 = (f32[2,256,256]{2,1,0:T(8,128)S(1)}, f32[2,256,256]{2,1,0:T(8,128)S(1)}, u32[]{:S(2)}, u32[]{:S(2)}) collective-permute-start(f32[2,256,256]{2,1,0:T(8,128)S(1)} %get-tuple-element.20), channel_id=1, source_target_pairs={{1,3},{2,0},{3,5},{4,2},{5,7},{6,4},{7,9},{8,6},{9,11},{10,8},{11,... | collective-permute-start | bytes 1572872 | tf_op jit(solution)/shard_map/ppermute | solution.py:31
  20.1 1.9 %collective-permute-start.2 = (f32[256,256]{1,0:T(8,128)S(1)}, f32[256,256]{1,0:T(8,128)S(1)}, u32[]{:S(2)}, u32[]{:S(2)}) collective-permute-start(f32[256,256]{1,0:T(8,128)S(1)} %get-tuple-element.21), channel_id=1, source_target_pairs={{0,3},{2,5},{3,0},{4,7},{5,2},{6,9},{7,4},{8,11},{9,6},{10,13},{11... | collective-permute-start | bytes 786440 | tf_op jit(solution)/shard_map/ppermute | solution.py:31
  30.3 17.1 %all-to-all-start = ((f32[64,1,128]{2,1,0:T(1,128)}), f32[64,1,128]{2,1,0:T(1,128)S(1)}, u32[]{:S(2)}, u32[]{:S(2)}) async-start(f32[64,1,128]{2,1,0:T(1,128)} %bitcast.1), calls=%async_computation | async-start | bytes 65536 | tf_op jit(solution)/shard_map/all_to_all | solution.py:272
  38.1 24.7 %collective-permute-start.4 = (f32[3,256,256]{2,1,0:T(8,128)S(1)}, f32[3,256,256]{2,1,0:T(8,128)S(1)}, u32[]{:S(2)}, u32[]{:S(2)}) collective-permute-start(f32[3,256,256]{2,1,0:T(8,128)S(1)} %get-tuple-element.22.own), channel_id=1, source_target_pairs={{0,3},{2,5},{3,0},{4,7},{5,2},{6,9},{7,4},{8,11},{9,6},{10,13},{11... | collective-permute-start | bytes 2359304 | tf_op jit(solution)/shard_map/ppermute | solution.py:31
  38.8 24.0 %collective-permute-start.3 = (f32[3,256,256]{2,1,0:T(8,128)S(1)}, f32[3,256,256]{2,1,0:T(8,128)S(1)}, u32[]{:S(2)}, u32[]{:S(2)}) collective-permute-start(f32[3,256,256]{2,1,0:T(8,128)S(1)} %get-tuple-element.22.own), channel_id=1, source_target_pairs={{0,1},{1,0},{2,3},{3,2},{4,5},{5,4},{6,7},{7,6},{8,9},{9,8},{10,11... | collective-permute-start | bytes 2359304 | tf_op jit(solution)/shard_map/ppermute | solution.py:31
  48.0 26.0 %all-to-all-start.1 = ((f32[16,1,128]{2,1,0:T(1,128)}), f32[16,1,128]{2,1,0:T(1,128)S(1)}, u32[]{:S(2)}, u32[]{:S(2)}) async-start(f32[16,1,128]{2,1,0:T(1,128)} %bitcast.4), calls=%async_computation.1 | async-start | bytes 16384 | tf_op jit(solution)/shard_map/all_to_all | solution.py:275
  65.2 9.4 %collective-permute-start.5 = (f32[2,256,256]{2,1,0:T(8,128)}, f32[2,256,256]{2,1,0:T(8,128)S(1)}, u32[]{:S(2)}, u32[]{:S(2)}) collective-permute-start(f32[2,256,256]{2,1,0:T(8,128)} %get-tuple-element.28), channel_id=1, source_target_pairs={{0,1},{1,0},{2,3},{3,2},{4,5},{5,4},{6,7},{7,6},{8,9},{9,8},{10,11... | collective-permute-start | bytes 1572872 | tf_op jit(solution)/shard_map/ppermute | solution.py:31

commit v7 on v6

--- a/solution.py
+++ b/solution.py
@@ -73,38 +73,60 @@
             kernel(place == 1)
 
 
-def mask_kernel(weights, upper, own, two, one):
+def mask_kernel(rows_total, mask, upper, own, two, one, held, buffer, arrived):
     order = upper.shape[-1]
+    flags = pltpu.make_async_copy(mask, held, arrived.at[SLOTS])
+    flags.start()
+    copies = [
+        pltpu.make_async_copy(upper.at[0, slot], buffer.at[slot], arrived.at[slot]) for slot in range(SLOTS)
+    ]
+    for copy in copies:
+        copy.start()
+    here = lax.axis_index(AXES)
+    second = lax.axis_index("core")
     line = lax.broadcasted_iota(jnp.int32, (MARKS, order), 0)
     marks = jnp.zeros((MARKS, order), jnp.float32)
+    flags.wait()
+    weights = [
+        jnp.where(here + slot < rows_total, held[0, slot], 0).astype(jnp.float32) for slot in range(SLOTS)
+    ]
     for slot in range(SLOTS):
-        marks = jnp.where(line == slot, weights[:, slot : slot + 1], marks)
+        marks = jnp.where(line == slot, weights[slot], marks)
     own[SLOTS * order :] = marks
-    tiles = [upper[0, slot] * weights[:, slot : slot + 1] for slot in range(SLOTS)]
     for slot in range(SLOTS):
-        own[slot * order : (slot + 1) * order] = tiles[slot]
-
-    def messages(second):
-        two[0], two[1] = (tiles[1], tiles[2]) if second else (tiles[0], tiles[1])
-        one[...] = tiles[0] if second else tiles[2]
-
-    by_place(messages)
-
-
-def masked(weights, upper):
+        copies[slot].wait()
+        tile = buffer[slot] * weights[slot]
+        own[slot * order : (slot + 1) * order] = tile
+        for place in range(2):
+
+            @pl.when(second == place)
+            def _():
+                if 0 <= slot - place < 2:
+                    two[slot - place] = tile
+                else:
+                    one[...] = tile
+
+
+def masked(mask, upper):
     order = upper.shape[-1]
-    return pl.pallas_call(
-        mask_kernel,
+    rows_total = lax.axis_size(AXES)
+    return pl.pallas_call(
+        lambda *refs: mask_kernel(rows_total, *refs),
         out_shape=[
             jax.ShapeDtypeStruct((SLOTS * order + MARKS, order), jnp.float32),
             jax.ShapeDtypeStruct((2, order, order), jnp.float32),
             jax.ShapeDtypeStruct((order, order), jnp.float32),
         ],
-        in_specs=[VMEM] * 2,
+        in_specs=[pl.BlockSpec(memory_space=pl.ANY)] * 2,
         out_specs=[VMEM] * 3,
+        scratch_shapes=[
+            pltpu.SMEM(mask.shape, jnp.int32),
+            pltpu.VMEM((SLOTS, order, order), jnp.float32),
+            pltpu.SemaphoreType.DMA((SLOTS + 1,)),
+        ],
         compiler_params=pltpu.CompilerParams(vmem_limit_bytes=8 * MIB),
         cost_estimate=pl.CostEstimate(flops=0, bytes_accessed=36 * order**2, transcendentals=0),
-    )(weights, upper)
+    )(pltpu.with_memory_space_constraint(mask, pltpu.HBM), pltpu.with_memory_space_constraint(upper, pltpu.HBM))
 
 
 def pair_tiles(own, partner, second):
@@ -153,17 +175,34 @@
     by_place(compute)
 
 
-def second_kernel(own, partner, far, marks, kept, sent):
+def sides(second):
+    here, there = (BACK, FRONT) if second else (FRONT, BACK)
+    away = [(row - 2, column - 2) if second else (row + 2, column + 2) for row, column in there]
+    return here, there, away
+
+
+def held_tiles(*groups):
+    return {place: split(held[index]) for places, held in groups for index, place in enumerate(places)}
+
+
+def middle_kernel(own, partner, base):
     def compute(second):
-        here, there = (BACK, FRONT) if second else (FRONT, BACK)
-        away = [(row - 2, column - 2) if second else (row + 2, column + 2) for row, column in there]
-        tiles = {}
-        for places, held in ((here, own), (there, partner), (away, far)):
-            for index, place in enumerate(places):
-                tiles[place] = split(held[index])
+        here, there, _ = sides(second)
+        tiles = held_tiles((here, own), (there, partner))
+        for index, place in enumerate(here):
+            base[index] = square(tiles, *place, chosen=NEAR[second])
+
+    by_place(compute)
+
+
+def second_kernel(own, partner, base, far, marks, kept, sent):
+    def compute(second):
+        here, there, away = sides(second)
+        tiles = held_tiles((away, far)) if second else held_tiles((here, own), (away, far))
         targets = [sent.at[0], sent.at[1], kept] if second else [kept, sent.at[0], sent.at[1]]
         for index, place in enumerate(here):
-            targets[index][...] = square(tiles, *place) * marks[index : index + 1]
+            total = base[index] + square(tiles, *place, chosen=FAR[second])
+            targets[index][...] = total * marks[index : index + 1]
 
     by_place(compute)
 
@@ -189,7 +228,7 @@
     )(own, partner)
     fresh, pay = pl.pallas_call(
         first_kernel,
-        out_shape=[tiles, jax.ShapeDtypeStruct((lax.axis_size(INNER), LANES), jnp.float32)],
+        out_shape=[tiles, jax.ShapeDtypeStruct((lax.axis_size(OUTER), LANES), jnp.float32)],
         in_specs=[VMEM] * 7,
         out_specs=[VMEM] * 2,
         compiler_params=pltpu.CompilerParams(vmem_limit_bytes=12 * MIB),
@@ -200,23 +239,37 @@
 
 def second_step(own, partner, far, marks):
     order = own.shape[-1]
+    base = pl.pallas_call(
+        middle_kernel,
+        out_shape=jax.ShapeDtypeStruct(own.shape, jnp.float32),
+        in_specs=[VMEM] * 2,
+        out_specs=VMEM,
+        compiler_params=pltpu.CompilerParams(vmem_limit_bytes=12 * MIB),
+        cost_estimate=cost(9, order),
+    )(own, partner)
     return pl.pallas_call(
         second_kernel,
         out_shape=[
             jax.ShapeDtypeStruct((order, order), jnp.float32),
             jax.ShapeDtypeStruct((2, order, order), jnp.float32),
         ],
-        in_specs=[VMEM] * 4,
+        in_specs=[VMEM] * 5,
         out_specs=[VMEM] * 2,
-        compiler_params=pltpu.CompilerParams(vmem_limit_bytes=16 * MIB),
-        cost_estimate=cost(12, order),
-    )(own, partner, far, marks)
-
-
-def join_kernel(kept, received, out):
+        compiler_params=pltpu.CompilerParams(vmem_limit_bytes=12 * MIB),
+        cost_estimate=cost(5, order),
+    )(own, partner, base, far, marks)
+
+
+def join_kernel(kept, received, out, sent):
     second = lax.axis_index("core")
-    out[pl.ds(second, 2)] = received[...]
-    out[SPAN - SPAN * second] = kept[...]
+    copies = [
+        pltpu.make_async_copy(received, out.at[pl.ds(second, 2)], sent.at[0]),
+        pltpu.make_async_copy(kept, out.at[SPAN - SPAN * second], sent.at[1]),
+    ]
+    for copy in copies:
+        copy.start()
+    for copy in copies:
+        copy.wait()
 
 
 def join(kept, received):
@@ -225,8 +278,9 @@
         join_kernel,
         out_shape=jax.ShapeDtypeStruct((SLOTS, order, order), jnp.float32),
         in_specs=[VMEM] * 2,
-        out_specs=VMEM,
-        compiler_params=pltpu.CompilerParams(vmem_limit_bytes=8 * MIB),
+        out_specs=pl.BlockSpec(memory_space=pl.ANY),
+        scratch_shapes=[pltpu.SemaphoreType.DMA((2,))],
+        compiler_params=pltpu.CompilerParams(vmem_limit_bytes=2 * MIB),
         cost_estimate=pl.CostEstimate(flops=0, bytes_accessed=24 * order**2, transcendentals=0),
     )(kept, received)
 
@@ -263,16 +317,13 @@
 
 
 def body(upper_tiles, listed_mask):
-    rows_total = lax.axis_size(AXES)
-    slots = jnp.arange(SLOTS, dtype=jnp.int32)
-    valid = listed_mask * (lax.axis_index(AXES) + slots < rows_total).astype(jnp.int32)
-    own, two, one = masked(valid.astype(jnp.float32), upper_tiles)
+    own, two, one = masked(listed_mask, upper_tiles)
     two, one, partner = (permute(two, -2, 2), permute(one, 3, -3), permute(own, 1, -1))
     fresh, marks, pay = first_step(own, partner, two, one)
-    part = spread(lax.all_to_all(pay, INNER, 0, 0, tiled=True), lax.axis_size(OUTER))
+    part = spread(lax.all_to_all(pay, OUTER, 0, 0, tiled=True), lax.axis_size(INNER))
     part, marks = lax.optimization_barrier((part, marks))
     kept, sent = second_step(fresh, permute(fresh, 1, -1), permute(fresh, 3, -3), marks)
-    gathered = lax.all_to_all(part, OUTER, 0, 0, tiled=True)
+    gathered = lax.all_to_all(part, INNER, 0, 0, tiled=True)
     total = total_of(gathered)
     kept, total = lax.optimization_barrier((kept, total))
     purified = join(kept, permute(sent, 1, -1))

time: 75.9 us -> 76.6 us (level)
  waiting for transfers between devices: 17.1 us -> 20.3 us
  local copies, waits for them, and re-layouts: 1.78 us -> 0 us
  starting transfers between devices: 48.6 us -> 47.4 us
    all_to_all x2, waiting for transfers between devices: 10.1 us -> 13.4 us  [the longest x1 8 us: body(): lax.all_to_all(pay, OUTER, 0, 0, tiled=True)]
    ppermute x6, starting transfers between devices: 26.1 us -> 23.1 us  [permute(): lax.ppermute(value, AXES, [move for move in moves if 0 <= move[1] < count])]
    pallas_call x1 -> x2, Pallas kernels: 0.21 us -> 2.39 us  [the longest x1 1.21 us: second_step(): pl.pallas_call(middle_kernel, out_shape=jax.ShapeDtypeStruct(own.shape, j...]
    pallas_call x1, Pallas kernels: 2.44 us -> 0.65 us  [second_step(): pl.pallas_call(second_kernel, out_shape=[jax.ShapeDtypeStruct((order, ord...]
    unnamed x4 -> x0, local copies, waits for them, and re-layouts: 1.78 us -> none
    all_to_all x2, starting transfers between devices: 22.5 us -> 24.3 us  [the longest x1 13.9 us: body(): lax.all_to_all(pay, OUTER, 0, 0, tiled=True)]
where the time goes in v7:
time: 76.6 us; the launch traced here: 76.2 us
  starting transfers between devices  47.4 us (62%)
  waiting for transfers between devices  20.3 us (27%)
  Pallas kernels  7.67 us (10%)
    ppermute x6, starting transfers between devices, permute(): lax.ppermute(value, AXES, [move for move in moves if 0 <= move[1] < count])  23.1 us
    all_to_all x1, starting transfers between devices, body(): lax.all_to_all(pay, OUTER, 0, 0, tiled=True)  13.9 us
    all_to_all x1, starting transfers between devices, body(): gathered = lax.all_to_all(part, INNER, 0, 0, tiled=True)  10.4 us
    all_to_all x1, waiting for transfers between devices, body(): lax.all_to_all(pay, OUTER, 0, 0, tiled=True)  8 us
    ppermute x6, waiting for transfers between devices, permute(): lax.ppermute(value, AXES, [move for move in moves if 0 <= move[1] < count])  6.95 us
    all_to_all x1, waiting for transfers between devices, body(): gathered = lax.all_to_all(part, INNER, 0, 0, tiled=True)  5.39 us
  transfers between devices with their start and end apart: 8, of which 3 were waited for; matrix products, arithmetic and copies ran while one was open for 0% of the time, Pallas kernels for 6%

profile of v7, /device:TPU:1, one launch (start us, length us, event | category | flops | bytes accessed | tf_op | source)
XLA Modules:
  0.0 76.2 jit_solution(233250277825329794)
XLA Ops:
  0.6 1.2 %shard_map.41 = (f32[776,256]{1,0:T(8,128)S(1)}, f32[2,256,256]{2,1,0:T(8,128)S(1)}, f32[256,256]{1,0:T(8,128)S(1)}) custom-call(s32[1,3]{1,0:T(1,128)} %refs_0_.1, f32[1,3,256,256]{3,2,1,0:T(8,128)} %refs_1_.1), custom_call_target="tpu_custom_call" | custom-call | bytes 2359296 | tf_op jit(solution)/shard_map/pallas_call | solution.py:113
  1.8 16.1 %collective-permute-start = (f32[776,256]{1,0:T(8,128)S(1)}, f32[776,256]{1,0:T(8,128)S(1)}, u32[]{:S(2)}, u32[]{:S(2)}) collective-permute-start(f32[776,256]{1,0:T(8,128)S(1)} %get-tuple-element.16.own), channel_id=1, source_target_pairs={{0,1},{1,0},{2,3},{3,2},{4,5},{5,4},{6,7},{7,6},{8,9},{9,8},{10,11... | collective-permute-start | bytes 2383880 | tf_op jit(solution)/shard_map/ppermute | solution.py:31
  17.9 1.3 %collective-permute-start.1 = (f32[2,256,256]{2,1,0:T(8,128)S(1)}, f32[2,256,256]{2,1,0:T(8,128)S(1)}, u32[]{:S(2)}, u32[]{:S(2)}) collective-permute-start(f32[2,256,256]{2,1,0:T(8,128)S(1)} %get-tuple-element.20), channel_id=1, source_target_pairs={{1,3},{2,0},{3,5},{4,2},{5,7},{6,4},{7,9},{8,6},{9,11},{10,8},{11,... | collective-permute-start | bytes 1572872 | tf_op jit(solution)/shard_map/ppermute | solution.py:31
  19.2 0.7 collective-permute-start.2
  19.9 0.0 collective-permute-done.partner
  19.9 1.2 %shard_map.42 = (f32[3,256,256]{2,1,0:T(8,128)S(1)}, f32[8,256]{1,0:T(8,128)S(1)}, f32[8,128]{1,0:T(8,128)S(1)}) custom-call(f32[776,256]{1,0:T(8,128)S(1)} %get-tuple-element.16.own, f32[776,256]{1,0:T(8,128)S(1)} %collective-permute-done.partner), custom_call_target="tpu_custom_call" | custom-call | flops 905969664 | bytes 3145728 | tf_op jit(solution)/shard_map/pallas_call | solution.py:217
  21.2 0.0 collective-permute-done.2.one
  21.2 6.9 %collective-permute-done.1.two = f32[2,256,256]{2,1,0:T(8,128)S(1)} collective-permute-done((f32[2,256,256]{2,1,0:T(8,128)S(1)}, f32[2,256,256]{2,1,0:T(8,128)S(1)}, u32[]{:S(2)}, u32[]{:S(2)}) %collective-permute-start.1) | collective-permute-done | bytes 524320 | tf_op jit(solution)/shard_map/ppermute | solution.py:31
  28.1 1.4 %shard_map.43 = (f32[3,256,256]{2,1,0:T(8,128)S(1)}, f32[16,128]{1,0:T(8,128)}) custom-call(f32[776,256]{1,0:T(8,128)S(1)} %get-tuple-element.16.own, f32[776,256]{1,0:T(8,128)S(1)} %collective-permute-done.partner, f32[3,256,256]{2,1,0:T(8,128)S(1)} %get-tuple-element.17.base, f32[8,256]{1,0:T(8,128)S(1)} %get-tuple-element.24.marks, ...), custom_call_target="tpu_custom_call" | custom-call | flops 503316480 | bytes 3145728 | tf_op jit(solution)/shard_map/pallas_call | solution.py:229
  29.5 13.9 %all-to-all-start = ((f32[16,1,128]{2,1,0:T(1,128)}), f32[16,1,128]{2,1,0:T(1,128)S(1)}, u32[]{:S(2)}, u32[]{:S(2)}) async-start(f32[16,1,128]{2,1,0:T(1,128)} %bitcast.1), calls=%async_computation | async-start | bytes 16384 | tf_op jit(solution)/shard_map/all_to_all | solution.py:323
  43.3 0.7 collective-permute-start.4
  44.0 2.4 %collective-permute-start.3 = (f32[3,256,256]{2,1,0:T(8,128)S(1)}, f32[3,256,256]{2,1,0:T(8,128)S(1)}, u32[]{:S(2)}, u32[]{:S(2)}) collective-permute-start(f32[3,256,256]{2,1,0:T(8,128)S(1)} %get-tuple-element.22.own), channel_id=1, source_target_pairs={{0,1},{1,0},{2,3},{3,2},{4,5},{5,4},{6,7},{7,6},{8,9},{9,8},{10,11... | collective-permute-start | bytes 2359304 | tf_op jit(solution)/shard_map/ppermute | solution.py:31
  46.5 8.0 %all-to-all-done = f32[16,1,128]{2,1,0:T(1,128)S(1)} async-done(((f32[16,1,128]{2,1,0:T(1,128)}), f32[16,1,128]{2,1,0:T(1,128)S(1)}, u32[]{:S(2)}, u32[]{:S(2)}) %all-to-all-start) | async-done | bytes 8224 | tf_op jit(solution)/shard_map/all_to_all | solution.py:323
  54.5 0.6 shard_map.45
  55.1 10.4 %all-to-all-start.1 = ((f32[64,1,128]{2,1,0:T(1,128)}), f32[64,1,128]{2,1,0:T(1,128)S(1)}, u32[]{:S(2)}, u32[]{:S(2)}) async-start(f32[64,1,128]{2,1,0:T(1,128)} %bitcast.4), calls=%async_computation.1 | async-start | bytes 65536 | tf_op jit(solution)/shard_map/all_to_all | solution.py:326
  65.6 0.0 collective-permute-done.3.partner
  65.6 1.2 %shard_map.44.base = f32[3,256,256]{2,1,0:T(8,128)S(1)} custom-call(f32[3,256,256]{2,1,0:T(8,128)S(1)} %get-tuple-element.22.own, f32[3,256,256]{2,1,0:T(8,128)S(1)} %collective-permute-done.3.partner), custom_call_target="tpu_custom_call" | custom-call | flops 905969664 | bytes 3145728 | tf_op jit(solution)/shard_map/pallas_call | solution.py:242
  66.8 0.0 collective-permute-done.4.far
  66.8 0.6 shard_map.46
  67.4 1.9 %collective-permute-start.5 = (f32[2,256,256]{2,1,0:T(8,128)S(1)}, f32[2,256,256]{2,1,0:T(8,128)S(1)}, u32[]{:S(2)}, u32[]{:S(2)}) collective-permute-start(f32[2,256,256]{2,1,0:T(8,128)S(1)} %get-tuple-element.28), channel_id=1, source_target_pairs={{0,1},{1,0},{2,3},{3,2},{4,5},{5,4},{6,7},{7,6},{8,9},{9,8},{10,11... | collective-permute-start | bytes 1572872 | tf_op jit(solution)/shard_map/ppermute | solution.py:31
  69.4 5.4 %all-to-all-done.1 = f32[64,1,128]{2,1,0:T(1,128)S(1)} async-done(((f32[64,1,128]{2,1,0:T(1,128)}), f32[64,1,128]{2,1,0:T(1,128)S(1)}, u32[]{:S(2)}, u32[]{:S(2)}) %all-to-all-start.1) | async-done | bytes 32800 | tf_op jit(solution)/shard_map/all_to_all | solution.py:326
  74.8 0.5 shard_map.47
  75.3 0.0 collective-permute-done.5.received
  75.3 0.9 %shard_map.48 = f32[3,256,256]{2,1,0:T(8,128)} custom-call(f32[256,256]{1,0:T(8,128)S(1)} %get-tuple-element.27.kept, f32[2,256,256]{2,1,0:T(8,128)S(1)} %collective-permute-done.5.received), custom_call_target="tpu_custom_call" | custom-call | bytes 1572864 | tf_op jit(solution)/shard_map/pallas_call | solution.py:277
Async XLA Ops:
  1.8 18.1 %collective-permute-start = (f32[776,256]{1,0:T(8,128)S(1)}, f32[776,256]{1,0:T(8,128)S(1)}, u32[]{:S(2)}, u32[]{:S(2)}) collective-permute-start(f32[776,256]{1,0:T(8,128)S(1)} %get-tuple-element.16.own), channel_id=1, source_target_pairs={{0,1},{1,0},{2,3},{3,2},{4,5},{5,4},{6,7},{7,6},{8,9},{9,8},{10,11... | collective-permute-start | bytes 2383880 | tf_op jit(solution)/shard_map/ppermute | solution.py:31
  17.9 10.2 %collective-permute-start.1 = (f32[2,256,256]{2,1,0:T(8,128)S(1)}, f32[2,256,256]{2,1,0:T(8,128)S(1)}, u32[]{:S(2)}, u32[]{:S(2)}) collective-permute-start(f32[2,256,256]{2,1,0:T(8,128)S(1)} %get-tuple-element.20), channel_id=1, source_target_pairs={{1,3},{2,0},{3,5},{4,2},{5,7},{6,4},{7,9},{8,6},{9,11},{10,8},{11,... | collective-permute-start | bytes 1572872 | tf_op jit(solution)/shard_map/ppermute | solution.py:31
  19.2 1.9 %collective-permute-start.2 = (f32[256,256]{1,0:T(8,128)S(1)}, f32[256,256]{1,0:T(8,128)S(1)}, u32[]{:S(2)}, u32[]{:S(2)}) collective-permute-start(f32[256,256]{1,0:T(8,128)S(1)} %get-tuple-element.21), channel_id=1, source_target_pairs={{0,3},{2,5},{3,0},{4,7},{5,2},{6,9},{7,4},{8,11},{9,6},{10,13},{11... | collective-permute-start | bytes 786440 | tf_op jit(solution)/shard_map/ppermute | solution.py:31
  29.5 25.0 %all-to-all-start = ((f32[16,1,128]{2,1,0:T(1,128)}), f32[16,1,128]{2,1,0:T(1,128)S(1)}, u32[]{:S(2)}, u32[]{:S(2)}) async-start(f32[16,1,128]{2,1,0:T(1,128)} %bitcast.1), calls=%async_computation | async-start | bytes 16384 | tf_op jit(solution)/shard_map/all_to_all | solution.py:323
  43.3 23.5 %collective-permute-start.4 = (f32[3,256,256]{2,1,0:T(8,128)S(1)}, f32[3,256,256]{2,1,0:T(8,128)S(1)}, u32[]{:S(2)}, u32[]{:S(2)}) collective-permute-start(f32[3,256,256]{2,1,0:T(8,128)S(1)} %get-tuple-element.22.own), channel_id=1, source_target_pairs={{0,3},{2,5},{3,0},{4,7},{5,2},{6,9},{7,4},{8,11},{9,6},{10,13},{11... | collective-permute-start | bytes 2359304 | tf_op jit(solution)/shard_map/ppermute | solution.py:31
  44.0 21.5 %collective-permute-start.3 = (f32[3,256,256]{2,1,0:T(8,128)S(1)}, f32[3,256,256]{2,1,0:T(8,128)S(1)}, u32[]{:S(2)}, u32[]{:S(2)}) collective-permute-start(f32[3,256,256]{2,1,0:T(8,128)S(1)} %get-tuple-element.22.own), channel_id=1, source_target_pairs={{0,1},{1,0},{2,3},{3,2},{4,5},{5,4},{6,7},{7,6},{8,9},{9,8},{10,11... | collective-permute-start | bytes 2359304 | tf_op jit(solution)/shard_map/ppermute | solution.py:31
  55.1 19.6 %all-to-all-start.1 = ((f32[64,1,128]{2,1,0:T(1,128)}), f32[64,1,128]{2,1,0:T(1,128)S(1)}, u32[]{:S(2)}, u32[]{:S(2)}) async-start(f32[64,1,128]{2,1,0:T(1,128)} %bitcast.4), calls=%async_computation.1 | async-start | bytes 65536 | tf_op jit(solution)/shard_map/all_to_all | solution.py:326
  67.4 7.9 %collective-permute-start.5 = (f32[2,256,256]{2,1,0:T(8,128)S(1)}, f32[2,256,256]{2,1,0:T(8,128)S(1)}, u32[]{:S(2)}, u32[]{:S(2)}) collective-permute-start(f32[2,256,256]{2,1,0:T(8,128)S(1)} %get-tuple-element.28), channel_id=1, source_target_pairs={{0,1},{1,0},{2,3},{3,2},{4,5},{5,4},{6,7},{7,6},{8,9},{9,8},{10,11... | collective-permute-start | bytes 1572872 | tf_op jit(solution)/shard_map/ppermute | solution.py:31

commit v8 on v7

--- a/solution.py
+++ b/solution.py
@@ -138,19 +138,23 @@
     }
 
 
-def near_kernel(own, partner, base, marks, norm):
+def norm_kernel(own, norm):
+    order = own.shape[-1]
+    tiles = {(0, slot): own[slot * order : (slot + 1) * order] for slot in range(SLOTS)}
+    norm[...] = jnp.full(norm.shape, squared_norm(tiles), jnp.float32)
+
+
+def near_kernel(own, partner, norm, base, marks):
     order = own.shape[-1]
 
     def compute(second):
         given = pair_tiles(own, partner, second)
-        before = {place: tile for place, tile in given.items() if place[0] == int(second)}
         tiles = {place: split(tile) for place, tile in given.items()}
         for index, place in enumerate(BACK if second else FRONT):
             base[index] = 2.0 * given[place] - square(tiles, *place, chosen=NEAR[second])
             held = partner if (place[0] == 0) == second else own
             line = SLOTS * order + place[1] - place[0]
             marks[index : index + 1] = held[line : line + 1]
-        norm[...] = jnp.full(norm.shape, squared_norm(before), jnp.float32)
 
     by_place(compute)
 
@@ -214,18 +218,23 @@
 def first_step(own, partner, two, one):
     order = own.shape[-1]
     tiles = jax.ShapeDtypeStruct((SLOTS, order, order), jnp.float32)
+    lines = jax.ShapeDtypeStruct((MARKS, LANES), jnp.float32)
+    norm = pl.pallas_call(
+        norm_kernel,
+        out_shape=lines,
+        in_specs=[VMEM],
+        out_specs=VMEM,
+        compiler_params=pltpu.CompilerParams(vmem_limit_bytes=2 * MIB),
+        cost_estimate=pl.CostEstimate(flops=SPREAD_COST, bytes_accessed=0, transcendentals=0),
+    )(own)
     near = pl.pallas_call(
         near_kernel,
-        out_shape=[
-            tiles,
-            jax.ShapeDtypeStruct((MARKS, order), jnp.float32),
-            jax.ShapeDtypeStruct((MARKS, LANES), jnp.float32),
-        ],
-        in_specs=[VMEM] * 2,
-        out_specs=[VMEM] * 3,
+        out_shape=[tiles, jax.ShapeDtypeStruct((MARKS, order), jnp.float32)],
+        in_specs=[VMEM] * 3,
+        out_specs=[VMEM] * 2,
         compiler_params=pltpu.CompilerParams(vmem_limit_bytes=12 * MIB),
         cost_estimate=cost(9, order),
-    )(own, partner)
+    )(own, partner, norm)
     fresh, pay = pl.pallas_call(
         first_kernel,
         out_shape=[tiles, jax.ShapeDtypeStruct((lax.axis_size(OUTER), LANES), jnp.float32)],
@@ -233,7 +242,7 @@
         out_specs=[VMEM] * 2,
         compiler_params=pltpu.CompilerParams(vmem_limit_bytes=12 * MIB),
         cost_estimate=cost(5, order),
-    )(own, partner, *near, two, one)
+    )(own, partner, *near, norm, two, one)
     return fresh, near[1], pay
 
 

time: 76.6 us -> 73.9 us (0.965)
  waiting for transfers between devices: 20.3 us -> 16.7 us
  starting transfers between devices: 47.4 us -> 48.2 us
    all_to_all x1, starting transfers between devices: 10.4 us -> 5.21 us  [body(): gathered = lax.all_to_all(part, INNER, 0, 0, tiled=True)]
    ppermute x6, waiting for transfers between devices: 6.95 us -> 2.71 us  [permute(): lax.ppermute(value, AXES, [move for move in moves if 0 <= move[1] < count])]
    all_to_all x1, starting transfers between devices: 13.9 us -> 17.2 us  [body(): lax.all_to_all(pay, OUTER, 0, 0, tiled=True)]
    ppermute x6, starting transfers between devices: 23.1 us -> 25.8 us  [permute(): lax.ppermute(value, AXES, [move for move in moves if 0 <= move[1] < count])]
  transfers between devices with their start and end apart: 8 -> 8, of which waited for: 3 -> 4; matrix products, arithmetic and copies ran while one was open for 0% -> 0% of each run, Pallas kernels for 6% -> 6%
where the time goes in v8:
time: 73.9 us; the launch traced here: 73.5 us
  starting transfers between devices  48.2 us (65%)
  waiting for transfers between devices  16.7 us (23%)
  Pallas kernels  7.84 us (11%)
  between operations  0.76 us (1%)
    ppermute x6, starting transfers between devices, permute(): lax.ppermute(value, AXES, [move for move in moves if 0 <= move[1] < count])  25.8 us
    all_to_all x1, starting transfers between devices, body(): lax.all_to_all(pay, OUTER, 0, 0, tiled=True)  17.2 us
    all_to_all x1, waiting for transfers between devices, body(): lax.all_to_all(pay, OUTER, 0, 0, tiled=True)  8.58 us
    all_to_all x1, waiting for transfers between devices, body(): gathered = lax.all_to_all(part, INNER, 0, 0, tiled=True)  5.39 us
    all_to_all x1, starting transfers between devices, body(): gathered = lax.all_to_all(part, INNER, 0, 0, tiled=True)  5.21 us
    ppermute x6, waiting for transfers between devices, permute(): lax.ppermute(value, AXES, [move for move in moves if 0 <= move[1] < count])  2.71 us
  transfers between devices with their start and end apart: 8, of which 4 were waited for; matrix products, arithmetic and copies ran while one was open for 0% of the time, Pallas kernels for 6%

profile of v8, /device:TPU:1, one launch (start us, length us, event | category | flops | bytes accessed | tf_op | source)
XLA Modules:
  0.0 73.5 jit_solution(10311254867967799456)
XLA Ops:
  0.6 1.2 %shard_map.41 = (f32[776,256]{1,0:T(8,128)S(1)}, f32[2,256,256]{2,1,0:T(8,128)S(1)}, f32[256,256]{1,0:T(8,128)S(1)}) custom-call(s32[1,3]{1,0:T(1,128)} %refs_0_.1, f32[1,3,256,256]{3,2,1,0:T(8,128)} %refs_1_.1), custom_call_target="tpu_custom_call" | custom-call | bytes 2359296 | tf_op jit(solution)/shard_map/pallas_call | solution.py:113
  1.8 0.7 collective-permute-start.2
  2.5 18.7 %collective-permute-start.1 = (f32[2,256,256]{2,1,0:T(8,128)S(1)}, f32[2,256,256]{2,1,0:T(8,128)S(1)}, u32[]{:S(2)}, u32[]{:S(2)}) collective-permute-start(f32[2,256,256]{2,1,0:T(8,128)S(1)} %get-tuple-element.18), channel_id=1, source_target_pairs={{1,3},{2,0},{3,5},{4,2},{5,7},{6,4},{7,9},{8,6},{9,11},{10,8},{11,... | collective-permute-start | bytes 1572872 | tf_op jit(solution)/shard_map/ppermute | solution.py:31
  21.2 1.9 %collective-permute-start = (f32[776,256]{1,0:T(8,128)S(1)}, f32[776,256]{1,0:T(8,128)S(1)}, u32[]{:S(2)}, u32[]{:S(2)}) collective-permute-start(f32[776,256]{1,0:T(8,128)S(1)} %get-tuple-element.15.own), channel_id=1, source_target_pairs={{0,1},{1,0},{2,3},{3,2},{4,5},{5,4},{6,7},{7,6},{8,9},{9,8},{10,11... | collective-permute-start | bytes 2383880 | tf_op jit(solution)/shard_map/ppermute | solution.py:31
  23.1 0.2 shard_map.42.norm
  23.3 2.0 %collective-permute-done.partner = f32[776,256]{1,0:T(8,128)S(1)} collective-permute-done((f32[776,256]{1,0:T(8,128)S(1)}, f32[776,256]{1,0:T(8,128)S(1)}, u32[]{:S(2)}, u32[]{:S(2)}) %collective-permute-start) | collective-permute-done | bytes 794656 | tf_op jit(solution)/shard_map/ppermute | solution.py:31
  25.4 1.2 %shard_map.43 = (f32[3,256,256]{2,1,0:T(8,128)S(1)}, f32[8,256]{1,0:T(8,128)S(1)}) custom-call(f32[776,256]{1,0:T(8,128)S(1)} %get-tuple-element.15.own, f32[776,256]{1,0:T(8,128)S(1)} %collective-permute-done.partner, f32[8,128]{1,0:T(8,128)S(1)} %shard_map.42.norm), custom_call_target="tpu_custom_call" | custom-call | flops 905969664 | bytes 3145728 | tf_op jit(solution)/shard_map/pallas_call | solution.py:230
  26.6 0.0 collective-permute-done.2.one
  26.6 0.7 collective-permute-done.1.two
  27.3 1.3 %shard_map.44 = (f32[3,256,256]{2,1,0:T(8,128)S(1)}, f32[16,128]{1,0:T(8,128)}) custom-call(f32[776,256]{1,0:T(8,128)S(1)} %get-tuple-element.15.own, f32[776,256]{1,0:T(8,128)S(1)} %collective-permute-done.partner, f32[3,256,256]{2,1,0:T(8,128)S(1)} %get-tuple-element.16.base, f32[8,256]{1,0:T(8,128)S(1)} %get-tuple-element.22.marks, ...), custom_call_target="tpu_custom_call" | custom-call | flops 503316480 | bytes 3145728 | tf_op jit(solution)/shard_map/pallas_call | solution.py:238
  28.6 17.2 %all-to-all-start = ((f32[16,1,128]{2,1,0:T(1,128)}), f32[16,1,128]{2,1,0:T(1,128)S(1)}, u32[]{:S(2)}, u32[]{:S(2)}) async-start(f32[16,1,128]{2,1,0:T(1,128)} %bitcast.1), calls=%async_computation | async-start | bytes 16384 | tf_op jit(solution)/shard_map/all_to_all | solution.py:332
  45.8 0.7 collective-permute-start.4
  46.5 1.9 %collective-permute-start.3 = (f32[3,256,256]{2,1,0:T(8,128)S(1)}, f32[3,256,256]{2,1,0:T(8,128)S(1)}, u32[]{:S(2)}, u32[]{:S(2)}) collective-permute-start(f32[3,256,256]{2,1,0:T(8,128)S(1)} %get-tuple-element.20.own), channel_id=1, source_target_pairs={{0,1},{1,0},{2,3},{3,2},{4,5},{5,4},{6,7},{7,6},{8,9},{9,8},{10,11... | collective-permute-start | bytes 2359304 | tf_op jit(solution)/shard_map/ppermute | solution.py:31
  48.5 8.6 %all-to-all-done = f32[16,1,128]{2,1,0:T(1,128)S(1)} async-done(((f32[16,1,128]{2,1,0:T(1,128)}), f32[16,1,128]{2,1,0:T(1,128)S(1)}, u32[]{:S(2)}, u32[]{:S(2)}) %all-to-all-start) | async-done | bytes 8224 | tf_op jit(solution)/shard_map/all_to_all | solution.py:332
  57.0 0.6 shard_map.46
  57.7 5.2 %all-to-all-start.1 = ((f32[64,1,128]{2,1,0:T(1,128)}), f32[64,1,128]{2,1,0:T(1,128)S(1)}, u32[]{:S(2)}, u32[]{:S(2)}) async-start(f32[64,1,128]{2,1,0:T(1,128)} %bitcast.4), calls=%async_computation.1 | async-start | bytes 65536 | tf_op jit(solution)/shard_map/all_to_all | solution.py:335
  62.9 0.0 collective-permute-done.3.partner
  62.9 1.2 %shard_map.45.base = f32[3,256,256]{2,1,0:T(8,128)S(1)} custom-call(f32[3,256,256]{2,1,0:T(8,128)S(1)} %get-tuple-element.20.own, f32[3,256,256]{2,1,0:T(8,128)S(1)} %collective-permute-done.3.partner), custom_call_target="tpu_custom_call" | custom-call | flops 905969664 | bytes 3145728 | tf_op jit(solution)/shard_map/pallas_call | solution.py:251
  64.1 0.0 collective-permute-done.4.far
  64.1 0.6 shard_map.47
  64.8 1.9 %collective-permute-start.5 = (f32[2,256,256]{2,1,0:T(8,128)S(1)}, f32[2,256,256]{2,1,0:T(8,128)S(1)}, u32[]{:S(2)}, u32[]{:S(2)}) collective-permute-start(f32[2,256,256]{2,1,0:T(8,128)S(1)} %get-tuple-element.26), channel_id=1, source_target_pairs={{0,1},{1,0},{2,3},{3,2},{4,5},{5,4},{6,7},{7,6},{8,9},{9,8},{10,11... | collective-permute-start | bytes 1572872 | tf_op jit(solution)/shard_map/ppermute | solution.py:31
  66.7 5.4 %all-to-all-done.1 = f32[64,1,128]{2,1,0:T(1,128)S(1)} async-done(((f32[64,1,128]{2,1,0:T(1,128)}), f32[64,1,128]{2,1,0:T(1,128)S(1)}, u32[]{:S(2)}, u32[]{:S(2)}) %all-to-all-start.1) | async-done | bytes 32800 | tf_op jit(solution)/shard_map/all_to_all | solution.py:335
  72.1 0.5 shard_map.48
  72.6 0.0 collective-permute-done.5.received
  72.6 0.9 %shard_map.49 = f32[3,256,256]{2,1,0:T(8,128)} custom-call(f32[256,256]{1,0:T(8,128)S(1)} %get-tuple-element.25.kept, f32[2,256,256]{2,1,0:T(8,128)S(1)} %collective-permute-done.5.received), custom_call_target="tpu_custom_call" | custom-call | bytes 1572864 | tf_op jit(solution)/shard_map/pallas_call | solution.py:286
Async XLA Ops:
  1.8 24.8 %collective-permute-start.2 = (f32[256,256]{1,0:T(8,128)S(1)}, f32[256,256]{1,0:T(8,128)S(1)}, u32[]{:S(2)}, u32[]{:S(2)}) collective-permute-start(f32[256,256]{1,0:T(8,128)S(1)} %get-tuple-element.19), channel_id=1, source_target_pairs={{0,3},{2,5},{3,0},{4,7},{5,2},{6,9},{7,4},{8,11},{9,6},{10,13},{11... | collective-permute-start | bytes 786440 | tf_op jit(solution)/shard_map/ppermute | solution.py:31
  2.5 24.8 %collective-permute-start.1 = (f32[2,256,256]{2,1,0:T(8,128)S(1)}, f32[2,256,256]{2,1,0:T(8,128)S(1)}, u32[]{:S(2)}, u32[]{:S(2)}) collective-permute-start(f32[2,256,256]{2,1,0:T(8,128)S(1)} %get-tuple-element.18), channel_id=1, source_target_pairs={{1,3},{2,0},{3,5},{4,2},{5,7},{6,4},{7,9},{8,6},{9,11},{10,8},{11,... | collective-permute-start | bytes 1572872 | tf_op jit(solution)/shard_map/ppermute | solution.py:31
  21.2 4.2 %collective-permute-start = (f32[776,256]{1,0:T(8,128)S(1)}, f32[776,256]{1,0:T(8,128)S(1)}, u32[]{:S(2)}, u32[]{:S(2)}) collective-permute-start(f32[776,256]{1,0:T(8,128)S(1)} %get-tuple-element.15.own), channel_id=1, source_target_pairs={{0,1},{1,0},{2,3},{3,2},{4,5},{5,4},{6,7},{7,6},{8,9},{9,8},{10,11... | collective-permute-start | bytes 2383880 | tf_op jit(solution)/shard_map/ppermute | solution.py:31
  28.6 28.4 %all-to-all-start = ((f32[16,1,128]{2,1,0:T(1,128)}), f32[16,1,128]{2,1,0:T(1,128)S(1)}, u32[]{:S(2)}, u32[]{:S(2)}) async-start(f32[16,1,128]{2,1,0:T(1,128)} %bitcast.1), calls=%async_computation | async-start | bytes 16384 | tf_op jit(solution)/shard_map/all_to_all | solution.py:332
  45.8 18.3 %collective-permute-start.4 = (f32[3,256,256]{2,1,0:T(8,128)S(1)}, f32[3,256,256]{2,1,0:T(8,128)S(1)}, u32[]{:S(2)}, u32[]{:S(2)}) collective-permute-start(f32[3,256,256]{2,1,0:T(8,128)S(1)} %get-tuple-element.20.own), channel_id=1, source_target_pairs={{0,3},{2,5},{3,0},{4,7},{5,2},{6,9},{7,4},{8,11},{9,6},{10,13},{11... | collective-permute-start | bytes 2359304 | tf_op jit(solution)/shard_map/ppermute | solution.py:31
  46.5 16.4 %collective-permute-start.3 = (f32[3,256,256]{2,1,0:T(8,128)S(1)}, f32[3,256,256]{2,1,0:T(8,128)S(1)}, u32[]{:S(2)}, u32[]{:S(2)}) collective-permute-start(f32[3,256,256]{2,1,0:T(8,128)S(1)} %get-tuple-element.20.own), channel_id=1, source_target_pairs={{0,1},{1,0},{2,3},{3,2},{4,5},{5,4},{6,7},{7,6},{8,9},{9,8},{10,11... | collective-permute-start | bytes 2359304 | tf_op jit(solution)/shard_map/ppermute | solution.py:31
  57.7 14.4 %all-to-all-start.1 = ((f32[64,1,128]{2,1,0:T(1,128)}), f32[64,1,128]{2,1,0:T(1,128)S(1)}, u32[]{:S(2)}, u32[]{:S(2)}) async-start(f32[64,1,128]{2,1,0:T(1,128)} %bitcast.4), calls=%async_computation.1 | async-start | bytes 65536 | tf_op jit(solution)/shard_map/all_to_all | solution.py:335
  64.8 7.8 %collective-permute-start.5 = (f32[2,256,256]{2,1,0:T(8,128)S(1)}, f32[2,256,256]{2,1,0:T(8,128)S(1)}, u32[]{:S(2)}, u32[]{:S(2)}) collective-permute-start(f32[2,256,256]{2,1,0:T(8,128)S(1)} %get-tuple-element.26), channel_id=1, source_target_pairs={{0,1},{1,0},{2,3},{3,2},{4,5},{5,4},{6,7},{7,6},{8,9},{9,8},{10,11... | collective-permute-start | bytes 1572872 | tf_op jit(solution)/shard_map/ppermute | solution.py:31

commit v9 on v8

--- a/solution.py
+++ b/solution.py
@@ -138,7 +138,7 @@
     }
 
 
-def norm_kernel(own, norm):
+def norm_kernel(own, two, norm):
     order = own.shape[-1]
     tiles = {(0, slot): own[slot * order : (slot + 1) * order] for slot in range(SLOTS)}
     norm[...] = jnp.full(norm.shape, squared_norm(tiles), jnp.float32)
@@ -222,11 +222,11 @@
     norm = pl.pallas_call(
         norm_kernel,
         out_shape=lines,
-        in_specs=[VMEM],
+        in_specs=[VMEM] * 2,
         out_specs=VMEM,
         compiler_params=pltpu.CompilerParams(vmem_limit_bytes=2 * MIB),
         cost_estimate=pl.CostEstimate(flops=SPREAD_COST, bytes_accessed=0, transcendentals=0),
-    )(own)
+    )(own, two)
     near = pl.pallas_call(
         near_kernel,
         out_shape=[tiles, jax.ShapeDtypeStruct((MARKS, order), jnp.float32)],

time: 73.9 us -> 75.6 us (1.023)
  starting transfers between devices: 48.2 us -> 52.7 us
  waiting for transfers between devices: 16.7 us -> 13.9 us
    all_to_all x1, starting transfers between devices: 5.21 us -> 11.6 us  [body(): gathered = lax.all_to_all(part, INNER, 0, 0, tiled=True)]
    all_to_all x1, waiting for transfers between devices: 8.58 us -> 6.85 us  [body(): lax.all_to_all(pay, OUTER, 0, 0, tiled=True)]
    all_to_all x1, starting transfers between devices: 17.2 us -> 15.5 us  [body(): lax.all_to_all(pay, OUTER, 0, 0, tiled=True)]
    ppermute x6, waiting for transfers between devices: 2.71 us -> 1.68 us  [permute(): lax.ppermute(value, AXES, [move for move in moves if 0 <= move[1] < count])]
  transfers between devices with their start and end apart: 8 -> 8, of which waited for: 4 -> 3; matrix products, arithmetic and copies ran while one was open for 0% -> 0% of each run, Pallas kernels for 6% -> 6%
where the time goes in v9:
time: 75.6 us; the launch traced here: 75.2 us
  starting transfers between devices  52.7 us (70%)
  waiting for transfers between devices  13.9 us (18%)
  Pallas kernels  7.86 us (10%)
  between operations  0.77 us (1%)
    ppermute x6, starting transfers between devices, permute(): lax.ppermute(value, AXES, [move for move in moves if 0 <= move[1] < count])  25.6 us
    all_to_all x1, starting transfers between devices, body(): lax.all_to_all(pay, OUTER, 0, 0, tiled=True)  15.5 us
    all_to_all x1, starting transfers between devices, body(): gathered = lax.all_to_all(part, INNER, 0, 0, tiled=True)  11.6 us
    all_to_all x1, waiting for transfers between devices, body(): lax.all_to_all(pay, OUTER, 0, 0, tiled=True)  6.85 us
    all_to_all x1, waiting for transfers between devices, body(): gathered = lax.all_to_all(part, INNER, 0, 0, tiled=True)  5.39 us
    ppermute x6, waiting for transfers between devices, permute(): lax.ppermute(value, AXES, [move for move in moves if 0 <= move[1] < count])  1.68 us
  transfers between devices with their start and end apart: 8, of which 3 were waited for; matrix products, arithmetic and copies ran while one was open for 0% of the time, Pallas kernels for 6%

profile of v9, /device:TPU:1, one launch (start us, length us, event | category | flops | bytes accessed | tf_op | source)
XLA Modules:
  0.0 75.2 jit_solution(13845487912685643850)
XLA Ops:
  0.6 1.2 %shard_map.41 = (f32[776,256]{1,0:T(8,128)S(1)}, f32[2,256,256]{2,1,0:T(8,128)S(1)}, f32[256,256]{1,0:T(8,128)S(1)}) custom-call(s32[1,3]{1,0:T(1,128)} %refs_0_.1, f32[1,3,256,256]{3,2,1,0:T(8,128)} %refs_1_.1), custom_call_target="tpu_custom_call" | custom-call | bytes 2359296 | tf_op jit(solution)/shard_map/pallas_call | solution.py:113
  1.8 4.1 %collective-permute-start.1 = (f32[2,256,256]{2,1,0:T(8,128)S(1)}, f32[2,256,256]{2,1,0:T(8,128)S(1)}, u32[]{:S(2)}, u32[]{:S(2)}) collective-permute-start(f32[2,256,256]{2,1,0:T(8,128)S(1)} %get-tuple-element.16), channel_id=1, source_target_pairs={{1,3},{2,0},{3,5},{4,2},{5,7},{6,4},{7,9},{8,6},{9,11},{10,8},{11,... | collective-permute-start | bytes 1572872 | tf_op jit(solution)/shard_map/ppermute | solution.py:31
  5.9 0.7 collective-permute-start.2
  6.6 14.5 %collective-permute-start = (f32[776,256]{1,0:T(8,128)S(1)}, f32[776,256]{1,0:T(8,128)S(1)}, u32[]{:S(2)}, u32[]{:S(2)}) collective-permute-start(f32[776,256]{1,0:T(8,128)S(1)} %get-tuple-element.15.own), channel_id=1, source_target_pairs={{0,1},{1,0},{2,3},{3,2},{4,5},{5,4},{6,7},{7,6},{8,9},{9,8},{10,11... | collective-permute-start | bytes 2383880 | tf_op jit(solution)/shard_map/ppermute | solution.py:31
  21.1 0.0 collective-permute-done.1.two
  21.1 0.2 shard_map.42.norm
  21.4 1.7 %collective-permute-done.partner = f32[776,256]{1,0:T(8,128)S(1)} collective-permute-done((f32[776,256]{1,0:T(8,128)S(1)}, f32[776,256]{1,0:T(8,128)S(1)}, u32[]{:S(2)}, u32[]{:S(2)}) %collective-permute-start) | collective-permute-done | bytes 794656 | tf_op jit(solution)/shard_map/ppermute | solution.py:31
  23.0 1.2 %shard_map.43 = (f32[3,256,256]{2,1,0:T(8,128)S(1)}, f32[8,256]{1,0:T(8,128)S(1)}) custom-call(f32[776,256]{1,0:T(8,128)S(1)} %get-tuple-element.15.own, f32[776,256]{1,0:T(8,128)S(1)} %collective-permute-done.partner, f32[8,128]{1,0:T(8,128)S(1)} %shard_map.42.norm), custom_call_target="tpu_custom_call" | custom-call | flops 905969664 | bytes 3145728 | tf_op jit(solution)/shard_map/pallas_call | solution.py:230
  24.2 0.0 collective-permute-done.2.one
  24.2 1.4 %shard_map.44 = (f32[3,256,256]{2,1,0:T(8,128)S(1)}, f32[16,128]{1,0:T(8,128)}) custom-call(f32[776,256]{1,0:T(8,128)S(1)} %get-tuple-element.15.own, f32[776,256]{1,0:T(8,128)S(1)} %collective-permute-done.partner, f32[3,256,256]{2,1,0:T(8,128)S(1)} %get-tuple-element.17.base, f32[8,256]{1,0:T(8,128)S(1)} %get-tuple-element.22.marks, ...), custom_call_target="tpu_custom_call" | custom-call | flops 503316480 | bytes 3145728 | tf_op jit(solution)/shard_map/pallas_call | solution.py:238
  25.6 15.5 %all-to-all-start = ((f32[16,1,128]{2,1,0:T(1,128)}), f32[16,1,128]{2,1,0:T(1,128)S(1)}, u32[]{:S(2)}, u32[]{:S(2)}) async-start(f32[16,1,128]{2,1,0:T(1,128)} %bitcast.1), calls=%async_computation | async-start | bytes 16384 | tf_op jit(solution)/shard_map/all_to_all | solution.py:332
  41.2 0.7 collective-permute-start.4
  41.9 3.6 %collective-permute-start.3 = (f32[3,256,256]{2,1,0:T(8,128)S(1)}, f32[3,256,256]{2,1,0:T(8,128)S(1)}, u32[]{:S(2)}, u32[]{:S(2)}) collective-permute-start(f32[3,256,256]{2,1,0:T(8,128)S(1)} %get-tuple-element.20.own), channel_id=1, source_target_pairs={{0,1},{1,0},{2,3},{3,2},{4,5},{5,4},{6,7},{7,6},{8,9},{9,8},{10,11... | collective-permute-start | bytes 2359304 | tf_op jit(solution)/shard_map/ppermute | solution.py:31
  45.5 6.8 %all-to-all-done = f32[16,1,128]{2,1,0:T(1,128)S(1)} async-done(((f32[16,1,128]{2,1,0:T(1,128)}), f32[16,1,128]{2,1,0:T(1,128)S(1)}, u32[]{:S(2)}, u32[]{:S(2)}) %all-to-all-start) | async-done | bytes 8224 | tf_op jit(solution)/shard_map/all_to_all | solution.py:332
  52.4 0.6 shard_map.46
  53.0 11.6 %all-to-all-start.1 = ((f32[64,1,128]{2,1,0:T(1,128)}), f32[64,1,128]{2,1,0:T(1,128)S(1)}, u32[]{:S(2)}, u32[]{:S(2)}) async-start(f32[64,1,128]{2,1,0:T(1,128)} %bitcast.4), calls=%async_computation.1 | async-start | bytes 65536 | tf_op jit(solution)/shard_map/all_to_all | solution.py:335
  64.6 0.0 collective-permute-done.3.partner
  64.6 1.2 %shard_map.45.base = f32[3,256,256]{2,1,0:T(8,128)S(1)} custom-call(f32[3,256,256]{2,1,0:T(8,128)S(1)} %get-tuple-element.20.own, f32[3,256,256]{2,1,0:T(8,128)S(1)} %collective-permute-done.3.partner), custom_call_target="tpu_custom_call" | custom-call | flops 905969664 | bytes 3145728 | tf_op jit(solution)/shard_map/pallas_call | solution.py:251
  65.8 0.0 collective-permute-done.4.far
  65.8 0.7 shard_map.47
  66.5 1.9 %collective-permute-start.5 = (f32[2,256,256]{2,1,0:T(8,128)S(1)}, f32[2,256,256]{2,1,0:T(8,128)S(1)}, u32[]{:S(2)}, u32[]{:S(2)}) collective-permute-start(f32[2,256,256]{2,1,0:T(8,128)S(1)} %get-tuple-element.26), channel_id=1, source_target_pairs={{0,1},{1,0},{2,3},{3,2},{4,5},{5,4},{6,7},{7,6},{8,9},{9,8},{10,11... | collective-permute-start | bytes 1572872 | tf_op jit(solution)/shard_map/ppermute | solution.py:31
  68.4 5.4 %all-to-all-done.1 = f32[64,1,128]{2,1,0:T(1,128)S(1)} async-done(((f32[64,1,128]{2,1,0:T(1,128)}), f32[64,1,128]{2,1,0:T(1,128)S(1)}, u32[]{:S(2)}, u32[]{:S(2)}) %all-to-all-start.1) | async-done | bytes 32800 | tf_op jit(solution)/shard_map/all_to_all | solution.py:335
  73.8 0.5 shard_map.48
  74.3 0.0 collective-permute-done.5.received
  74.3 0.9 %shard_map.49 = f32[3,256,256]{2,1,0:T(8,128)} custom-call(f32[256,256]{1,0:T(8,128)S(1)} %get-tuple-element.25.kept, f32[2,256,256]{2,1,0:T(8,128)S(1)} %collective-permute-done.5.received), custom_call_target="tpu_custom_call" | custom-call | bytes 1572864 | tf_op jit(solution)/shard_map/pallas_call | solution.py:286
Async XLA Ops:
  1.8 19.3 %collective-permute-start.1 = (f32[2,256,256]{2,1,0:T(8,128)S(1)}, f32[2,256,256]{2,1,0:T(8,128)S(1)}, u32[]{:S(2)}, u32[]{:S(2)}) collective-permute-start(f32[2,256,256]{2,1,0:T(8,128)S(1)} %get-tuple-element.16), channel_id=1, source_target_pairs={{1,3},{2,0},{3,5},{4,2},{5,7},{6,4},{7,9},{8,6},{9,11},{10,8},{11,... | collective-permute-start | bytes 1572872 | tf_op jit(solution)/shard_map/ppermute | solution.py:31
  5.9 18.3 %collective-permute-start.2 = (f32[256,256]{1,0:T(8,128)S(1)}, f32[256,256]{1,0:T(8,128)S(1)}, u32[]{:S(2)}, u32[]{:S(2)}) collective-permute-start(f32[256,256]{1,0:T(8,128)S(1)} %get-tuple-element.19), channel_id=1, source_target_pairs={{0,3},{2,5},{3,0},{4,7},{5,2},{6,9},{7,4},{8,11},{9,6},{10,13},{11... | collective-permute-start | bytes 786440 | tf_op jit(solution)/shard_map/ppermute | solution.py:31
  6.6 16.4 %collective-permute-start = (f32[776,256]{1,0:T(8,128)S(1)}, f32[776,256]{1,0:T(8,128)S(1)}, u32[]{:S(2)}, u32[]{:S(2)}) collective-permute-start(f32[776,256]{1,0:T(8,128)S(1)} %get-tuple-element.15.own), channel_id=1, source_target_pairs={{0,1},{1,0},{2,3},{3,2},{4,5},{5,4},{6,7},{7,6},{8,9},{9,8},{10,11... | collective-permute-start | bytes 2383880 | tf_op jit(solution)/shard_map/ppermute | solution.py:31
  25.6 26.8 %all-to-all-start = ((f32[16,1,128]{2,1,0:T(1,128)}), f32[16,1,128]{2,1,0:T(1,128)S(1)}, u32[]{:S(2)}, u32[]{:S(2)}) async-start(f32[16,1,128]{2,1,0:T(1,128)} %bitcast.1), calls=%async_computation | async-start | bytes 16384 | tf_op jit(solution)/shard_map/all_to_all | solution.py:332
  41.2 24.7 %collective-permute-start.4 = (f32[3,256,256]{2,1,0:T(8,128)S(1)}, f32[3,256,256]{2,1,0:T(8,128)S(1)}, u32[]{:S(2)}, u32[]{:S(2)}) collective-permute-start(f32[3,256,256]{2,1,0:T(8,128)S(1)} %get-tuple-element.20.own), channel_id=1, source_target_pairs={{0,3},{2,5},{3,0},{4,7},{5,2},{6,9},{7,4},{8,11},{9,6},{10,13},{11... | collective-permute-start | bytes 2359304 | tf_op jit(solution)/shard_map/ppermute | solution.py:31
  41.9 22.7 %collective-permute-start.3 = (f32[3,256,256]{2,1,0:T(8,128)S(1)}, f32[3,256,256]{2,1,0:T(8,128)S(1)}, u32[]{:S(2)}, u32[]{:S(2)}) collective-permute-start(f32[3,256,256]{2,1,0:T(8,128)S(1)} %get-tuple-element.20.own), channel_id=1, source_target_pairs={{0,1},{1,0},{2,3},{3,2},{4,5},{5,4},{6,7},{7,6},{8,9},{9,8},{10,11... | collective-permute-start | bytes 2359304 | tf_op jit(solution)/shard_map/ppermute | solution.py:31
  53.0 20.8 %all-to-all-start.1 = ((f32[64,1,128]{2,1,0:T(1,128)}), f32[64,1,128]{2,1,0:T(1,128)S(1)}, u32[]{:S(2)}, u32[]{:S(2)}) async-start(f32[64,1,128]{2,1,0:T(1,128)} %bitcast.4), calls=%async_computation.1 | async-start | bytes 65536 | tf_op jit(solution)/shard_map/all_to_all | solution.py:335
  66.5 7.8 %collective-permute-start.5 = (f32[2,256,256]{2,1,0:T(8,128)S(1)}, f32[2,256,256]{2,1,0:T(8,128)S(1)}, u32[]{:S(2)}, u32[]{:S(2)}) collective-permute-start(f32[2,256,256]{2,1,0:T(8,128)S(1)} %get-tuple-element.26), channel_id=1, source_target_pairs={{0,1},{1,0},{2,3},{3,2},{4,5},{5,4},{6,7},{7,6},{8,9},{9,8},{10,11... | collective-permute-start | bytes 1572872 | tf_op jit(solution)/shard_map/ppermute | solution.py:31

commit v10 on v9

--- a/solution.py
+++ b/solution.py
@@ -10,8 +10,8 @@
 SLOTS = 3
 SPAN = SLOTS - 1
 AXES = ("z", "x", "y", "core")
-INNER = ("x", "y", "core")
-OUTER = "z"
+INNER = ("x", "y")
+OUTER = ("z", "core")
 LANES = 128
 MARKS = 8
 MIB = 1024 * 1024
@@ -21,8 +21,8 @@
 
 BACK = ((0, 0), (0, 1), (1, 1))
 FRONT = ((0, 2), (1, 2), (1, 3))
-NEAR = ((0, 1), (0, 1, 2, 3))
-FAR = ((2, 3), (-2, -1))
+NEAR = ((0, 1, 2, 3), (0, 1))
+FAR = ((-2, -1), (2, 3))
 
 
 def permute(value, first_shift, second_shift):
@@ -150,7 +150,7 @@
     def compute(second):
         given = pair_tiles(own, partner, second)
         tiles = {place: split(tile) for place, tile in given.items()}
-        for index, place in enumerate(BACK if second else FRONT):
+        for index, place in enumerate(FRONT if second else BACK):
             base[index] = 2.0 * given[place] - square(tiles, *place, chosen=NEAR[second])
             held = partner if (place[0] == 0) == second else own
             line = SLOTS * order + place[1] - place[0]
@@ -163,13 +163,13 @@
     order = own.shape[-1]
 
     def compute(second):
-        given = {} if second else pair_tiles(own, partner, second)
-        far = ((-1, 0), (-1, 1), (-2, 0)) if second else ((2, 2), (2, 3), (3, 3))
+        given = pair_tiles(own, partner, second) if second else {}
+        far = ((2, 2), (2, 3), (3, 3)) if second else ((-1, 0), (-1, 1), (-2, 0))
         given.update(zip(far, (two[0], two[1], one[...])))
-        used = far if second else (*far, (0, 2), (1, 2), (1, 3))
+        used = (*far, (0, 2), (1, 2), (1, 3)) if second else far
         tiles = {place: split(given[place]) for place in used}
         after = {}
-        for index, place in enumerate(BACK if second else FRONT):
+        for index, place in enumerate(FRONT if second else BACK):
             rest = square(tiles, *place, chosen=FAR[second])
             after[place] = (base[index] - rest) * marks[index : index + 1]
             out[index] = after[place]
@@ -180,8 +180,8 @@
 
 
 def sides(second):
-    here, there = (BACK, FRONT) if second else (FRONT, BACK)
-    away = [(row - 2, column - 2) if second else (row + 2, column + 2) for row, column in there]
+    here, there = (FRONT, BACK) if second else (BACK, FRONT)
+    away = [(row + 2, column + 2) if second else (row - 2, column - 2) for row, column in there]
     return here, there, away
 
 
@@ -202,8 +202,8 @@
 def second_kernel(own, partner, base, far, marks, kept, sent):
     def compute(second):
         here, there, away = sides(second)
-        tiles = held_tiles((away, far)) if second else held_tiles((here, own), (away, far))
-        targets = [sent.at[0], sent.at[1], kept] if second else [kept, sent.at[0], sent.at[1]]
+        tiles = held_tiles((here, own), (away, far)) if second else held_tiles((away, far))
+        targets = [sent, kept.at[0], kept.at[1]] if second else [kept.at[0], kept.at[1], sent]
         for index, place in enumerate(here):
             total = base[index] + square(tiles, *place, chosen=FAR[second])
             targets[index][...] = total * marks[index : index + 1]
@@ -259,8 +259,8 @@
     return pl.pallas_call(
         second_kernel,
         out_shape=[
+            jax.ShapeDtypeStruct((2, order, order), jnp.float32),
             jax.ShapeDtypeStruct((order, order), jnp.float32),
-            jax.ShapeDtypeStruct((2, order, order), jnp.float32),
         ],
         in_specs=[VMEM] * 5,
         out_specs=[VMEM] * 2,
@@ -272,8 +272,8 @@
 def join_kernel(kept, received, out, sent):
     second = lax.axis_index("core")
     copies = [
-        pltpu.make_async_copy(received, out.at[pl.ds(second, 2)], sent.at[0]),
-        pltpu.make_async_copy(kept, out.at[SPAN - SPAN * second], sent.at[1]),
+        pltpu.make_async_copy(kept, out.at[pl.ds(second, 2)], sent.at[0]),
+        pltpu.make_async_copy(received, out.at[SPAN - SPAN * second], sent.at[1]),
     ]
     for copy in copies:
         copy.start()
@@ -327,11 +327,11 @@
 
 def body(upper_tiles, listed_mask):
     own, two, one = masked(listed_mask, upper_tiles)
-    two, one, partner = (permute(two, -2, 2), permute(one, 3, -3), permute(own, 1, -1))
+    two, one, partner = (permute(two, -1, 1), permute(one, 2, -2), permute(own, 1, -1))
     fresh, marks, pay = first_step(own, partner, two, one)
     part = spread(lax.all_to_all(pay, OUTER, 0, 0, tiled=True), lax.axis_size(INNER))
     part, marks = lax.optimization_barrier((part, marks))
-    kept, sent = second_step(fresh, permute(fresh, 1, -1), permute(fresh, 3, -3), marks)
+    kept, sent = second_step(fresh, permute(fresh, 1, -1), permute(fresh, -1, 1), marks)
     gathered = lax.all_to_all(part, INNER, 0, 0, tiled=True)
     total = total_of(gathered)
     kept, total = lax.optimization_barrier((kept, total))

time: 75.6 us -> 72.6 us (0.960)
  starting transfers between devices: 52.7 us -> 51.4 us
  Pallas kernels: 7.86 us -> 6.97 us
  waiting for transfers between devices: 13.9 us -> 13.1 us
    all_to_all x1, starting transfers between devices: 11.6 us -> 5.61 us  [body(): gathered = lax.all_to_all(part, INNER, 0, 0, tiled=True)]
    all_to_all x1, starting transfers between devices: 15.5 us -> 20.3 us  [body(): lax.all_to_all(pay, OUTER, 0, 0, tiled=True)]
    all_to_all x1, waiting for transfers between devices: 5.39 us -> 3.6 us  [body(): gathered = lax.all_to_all(part, INNER, 0, 0, tiled=True)]
    all_to_all x1, waiting for transfers between devices: 6.85 us -> 7.86 us  [body(): lax.all_to_all(pay, OUTER, 0, 0, tiled=True)]
  transfers between devices with their start and end apart: 8 -> 8, of which waited for: 3 -> 3; matrix products, arithmetic and copies ran while one was open for 0% -> 0% of each run, Pallas kernels for 6% -> 5%
where the time goes in v10:
time: 72.6 us; the launch traced here: 72.3 us
  starting transfers between devices  51.4 us (71%)
  waiting for transfers between devices  13.1 us (18%)
  Pallas kernels  6.97 us (10%)
  between operations  0.77 us (1%)
    ppermute x6, starting transfers between devices, permute(): lax.ppermute(value, AXES, [move for move in moves if 0 <= move[1] < count])  25.4 us
    all_to_all x1, starting transfers between devices, body(): lax.all_to_all(pay, OUTER, 0, 0, tiled=True)  20.3 us
    all_to_all x1, waiting for transfers between devices, body(): lax.all_to_all(pay, OUTER, 0, 0, tiled=True)  7.86 us
    all_to_all x1, starting transfers between devices, body(): gathered = lax.all_to_all(part, INNER, 0, 0, tiled=True)  5.61 us
    all_to_all x1, waiting for transfers between devices, body(): gathered = lax.all_to_all(part, INNER, 0, 0, tiled=True)  3.6 us
    ppermute x6, waiting for transfers between devices, permute(): lax.ppermute(value, AXES, [move for move in moves if 0 <= move[1] < count])  1.68 us
  transfers between devices with their start and end apart: 8, of which 3 were waited for; matrix products, arithmetic and copies ran while one was open for 0% of the time, Pallas kernels for 5%

profile of v10, /device:TPU:1, one launch (start us, length us, event | category | flops | bytes accessed | tf_op | source)
XLA Modules:
  0.0 72.3 jit_solution(18125056284080760877)
XLA Ops:
  0.6 1.2 %shard_map.41 = (f32[776,256]{1,0:T(8,128)S(1)}, f32[2,256,256]{2,1,0:T(8,128)S(1)}, f32[256,256]{1,0:T(8,128)S(1)}) custom-call(s32[1,3]{1,0:T(1,128)} %refs_0_.1, f32[1,3,256,256]{3,2,1,0:T(8,128)} %refs_1_.1), custom_call_target="tpu_custom_call" | custom-call | bytes 2359296 | tf_op jit(solution)/shard_map/pallas_call | solution.py:113
  1.8 4.6 %collective-permute-start.1 = (f32[2,256,256]{2,1,0:T(8,128)S(1)}, f32[2,256,256]{2,1,0:T(8,128)S(1)}, u32[]{:S(2)}, u32[]{:S(2)}) collective-permute-start(f32[2,256,256]{2,1,0:T(8,128)S(1)} %get-tuple-element.16), channel_id=1, source_target_pairs={{1,2},{2,1},{3,4},{4,3},{5,6},{6,5},{7,8},{8,7},{9,10},{10,9},{11,... | collective-permute-start | bytes 1572872 | tf_op jit(solution)/shard_map/ppermute | solution.py:31
  6.4 1.3 %collective-permute-start.2 = (f32[256,256]{1,0:T(8,128)S(1)}, f32[256,256]{1,0:T(8,128)S(1)}, u32[]{:S(2)}, u32[]{:S(2)}) collective-permute-start(f32[256,256]{1,0:T(8,128)S(1)} %get-tuple-element.19), channel_id=1, source_target_pairs={{0,2},{2,4},{3,1},{4,6},{5,3},{6,8},{7,5},{8,10},{9,7},{10,12},{11... | collective-permute-start | bytes 786440 | tf_op jit(solution)/shard_map/ppermute | solution.py:31
  7.7 12.2 %collective-permute-start = (f32[776,256]{1,0:T(8,128)S(1)}, f32[776,256]{1,0:T(8,128)S(1)}, u32[]{:S(2)}, u32[]{:S(2)}) collective-permute-start(f32[776,256]{1,0:T(8,128)S(1)} %get-tuple-element.15.own), channel_id=1, source_target_pairs={{0,1},{1,0},{2,3},{3,2},{4,5},{5,4},{6,7},{7,6},{8,9},{9,8},{10,11... | collective-permute-start | bytes 2383880 | tf_op jit(solution)/shard_map/ppermute | solution.py:31
  19.9 0.0 collective-permute-done.1.two
  19.9 0.2 shard_map.42.norm
  20.1 1.7 %collective-permute-done.partner = f32[776,256]{1,0:T(8,128)S(1)} collective-permute-done((f32[776,256]{1,0:T(8,128)S(1)}, f32[776,256]{1,0:T(8,128)S(1)}, u32[]{:S(2)}, u32[]{:S(2)}) %collective-permute-start) | collective-permute-done | bytes 794656 | tf_op jit(solution)/shard_map/ppermute | solution.py:31
  21.8 0.7 shard_map.43
  22.5 0.0 collective-permute-done.2.one
  22.5 1.4 %shard_map.44 = (f32[3,256,256]{2,1,0:T(8,128)S(1)}, f32[32,128]{1,0:T(8,128)}) custom-call(f32[776,256]{1,0:T(8,128)S(1)} %get-tuple-element.15.own, f32[776,256]{1,0:T(8,128)S(1)} %collective-permute-done.partner, f32[3,256,256]{2,1,0:T(8,128)S(1)} %get-tuple-element.17.base, f32[8,256]{1,0:T(8,128)S(1)} %get-tuple-element.22.marks, ...), custom_call_target="tpu_custom_call" | custom-call | flops 503316480 | bytes 3145728 | tf_op jit(solution)/shard_map/pallas_call | solution.py:238
  24.0 20.3 %all-to-all-start = ((f32[32,1,128]{2,1,0:T(1,128)}), f32[32,1,128]{2,1,0:T(1,128)S(1)}, u32[]{:S(2)}, u32[]{:S(2)}) async-start(f32[32,1,128]{2,1,0:T(1,128)} %bitcast.1), calls=%async_computation | async-start | bytes 32768 | tf_op jit(solution)/shard_map/all_to_all | solution.py:332
  44.3 1.9 %collective-permute-start.4 = (f32[3,256,256]{2,1,0:T(8,128)S(1)}, f32[3,256,256]{2,1,0:T(8,128)S(1)}, u32[]{:S(2)}, u32[]{:S(2)}) collective-permute-start(f32[3,256,256]{2,1,0:T(8,128)S(1)} %get-tuple-element.20.own), channel_id=1, source_target_pairs={{1,2},{2,1},{3,4},{4,3},{5,6},{6,5},{7,8},{8,7},{9,10},{10,9},{11,... | collective-permute-start | bytes 2359304 | tf_op jit(solution)/shard_map/ppermute | solution.py:31
  46.3 1.9 %collective-permute-start.3 = (f32[3,256,256]{2,1,0:T(8,128)S(1)}, f32[3,256,256]{2,1,0:T(8,128)S(1)}, u32[]{:S(2)}, u32[]{:S(2)}) collective-permute-start(f32[3,256,256]{2,1,0:T(8,128)S(1)} %get-tuple-element.20.own), channel_id=1, source_target_pairs={{0,1},{1,0},{2,3},{3,2},{4,5},{5,4},{6,7},{7,6},{8,9},{9,8},{10,11... | collective-permute-start | bytes 2359304 | tf_op jit(solution)/shard_map/ppermute | solution.py:31
  48.2 7.9 %all-to-all-done = f32[32,1,128]{2,1,0:T(1,128)S(1)} async-done(((f32[32,1,128]{2,1,0:T(1,128)}), f32[32,1,128]{2,1,0:T(1,128)S(1)}, u32[]{:S(2)}, u32[]{:S(2)}) %all-to-all-start) | async-done | bytes 16416 | tf_op jit(solution)/shard_map/all_to_all | solution.py:332
  56.0 0.6 shard_map.46
  56.7 5.6 %all-to-all-start.1 = ((f32[32,1,128]{2,1,0:T(1,128)}), f32[32,1,128]{2,1,0:T(1,128)S(1)}, u32[]{:S(2)}, u32[]{:S(2)}) async-start(f32[32,1,128]{2,1,0:T(1,128)} %bitcast.4), calls=%async_computation.1 | async-start | bytes 32768 | tf_op jit(solution)/shard_map/all_to_all | solution.py:335
  62.3 0.0 collective-permute-done.3.partner
  62.3 0.7 shard_map.45.base
  63.0 0.0 collective-permute-done.4.far
  63.0 0.7 shard_map.47
  63.7 3.5 %collective-permute-start.5 = (f32[256,256]{1,0:T(8,128)S(1)}, f32[256,256]{1,0:T(8,128)S(1)}, u32[]{:S(2)}, u32[]{:S(2)}) collective-permute-start(f32[256,256]{1,0:T(8,128)S(1)} %get-tuple-element.26), channel_id=1, source_target_pairs={{0,1},{1,0},{2,3},{3,2},{4,5},{5,4},{6,7},{7,6},{8,9},{9,8},{10,11... | collective-permute-start | bytes 786440 | tf_op jit(solution)/shard_map/ppermute | solution.py:31
  67.2 3.6 %all-to-all-done.1 = f32[32,1,128]{2,1,0:T(1,128)S(1)} async-done(((f32[32,1,128]{2,1,0:T(1,128)}), f32[32,1,128]{2,1,0:T(1,128)S(1)}, u32[]{:S(2)}, u32[]{:S(2)}) %all-to-all-start.1) | async-done | bytes 16416 | tf_op jit(solution)/shard_map/all_to_all | solution.py:335
  70.8 0.5 shard_map.48
  71.4 0.0 collective-permute-done.5.received
  71.4 0.9 %shard_map.49 = f32[3,256,256]{2,1,0:T(8,128)} custom-call(f32[2,256,256]{2,1,0:T(8,128)S(1)} %get-tuple-element.25.kept, f32[256,256]{1,0:T(8,128)S(1)} %collective-permute-done.5.received), custom_call_target="tpu_custom_call" | custom-call | bytes 1572864 | tf_op jit(solution)/shard_map/pallas_call | solution.py:286
Async XLA Ops:
  1.8 18.1 %collective-permute-start.1 = (f32[2,256,256]{2,1,0:T(8,128)S(1)}, f32[2,256,256]{2,1,0:T(8,128)S(1)}, u32[]{:S(2)}, u32[]{:S(2)}) collective-permute-start(f32[2,256,256]{2,1,0:T(8,128)S(1)} %get-tuple-element.16), channel_id=1, source_target_pairs={{1,2},{2,1},{3,4},{4,3},{5,6},{6,5},{7,8},{8,7},{9,10},{10,9},{11,... | collective-permute-start | bytes 1572872 | tf_op jit(solution)/shard_map/ppermute | solution.py:31
  6.4 16.1 %collective-permute-start.2 = (f32[256,256]{1,0:T(8,128)S(1)}, f32[256,256]{1,0:T(8,128)S(1)}, u32[]{:S(2)}, u32[]{:S(2)}) collective-permute-start(f32[256,256]{1,0:T(8,128)S(1)} %get-tuple-element.19), channel_id=1, source_target_pairs={{0,2},{2,4},{3,1},{4,6},{5,3},{6,8},{7,5},{8,10},{9,7},{10,12},{11... | collective-permute-start | bytes 786440 | tf_op jit(solution)/shard_map/ppermute | solution.py:31
  7.7 14.1 %collective-permute-start = (f32[776,256]{1,0:T(8,128)S(1)}, f32[776,256]{1,0:T(8,128)S(1)}, u32[]{:S(2)}, u32[]{:S(2)}) collective-permute-start(f32[776,256]{1,0:T(8,128)S(1)} %get-tuple-element.15.own), channel_id=1, source_target_pairs={{0,1},{1,0},{2,3},{3,2},{4,5},{5,4},{6,7},{7,6},{8,9},{9,8},{10,11... | collective-permute-start | bytes 2383880 | tf_op jit(solution)/shard_map/ppermute | solution.py:31
  24.0 32.1 %all-to-all-start = ((f32[32,1,128]{2,1,0:T(1,128)}), f32[32,1,128]{2,1,0:T(1,128)S(1)}, u32[]{:S(2)}, u32[]{:S(2)}) async-start(f32[32,1,128]{2,1,0:T(1,128)} %bitcast.1), calls=%async_computation | async-start | bytes 32768 | tf_op jit(solution)/shard_map/all_to_all | solution.py:332
  44.3 18.7 %collective-permute-start.4 = (f32[3,256,256]{2,1,0:T(8,128)S(1)}, f32[3,256,256]{2,1,0:T(8,128)S(1)}, u32[]{:S(2)}, u32[]{:S(2)}) collective-permute-start(f32[3,256,256]{2,1,0:T(8,128)S(1)} %get-tuple-element.20.own), channel_id=1, source_target_pairs={{1,2},{2,1},{3,4},{4,3},{5,6},{6,5},{7,8},{8,7},{9,10},{10,9},{11,... | collective-permute-start | bytes 2359304 | tf_op jit(solution)/shard_map/ppermute | solution.py:31
  46.3 16.0 %collective-permute-start.3 = (f32[3,256,256]{2,1,0:T(8,128)S(1)}, f32[3,256,256]{2,1,0:T(8,128)S(1)}, u32[]{:S(2)}, u32[]{:S(2)}) collective-permute-start(f32[3,256,256]{2,1,0:T(8,128)S(1)} %get-tuple-element.20.own), channel_id=1, source_target_pairs={{0,1},{1,0},{2,3},{3,2},{4,5},{5,4},{6,7},{7,6},{8,9},{9,8},{10,11... | collective-permute-start | bytes 2359304 | tf_op jit(solution)/shard_map/ppermute | solution.py:31
  56.7 14.2 %all-to-all-start.1 = ((f32[32,1,128]{2,1,0:T(1,128)}), f32[32,1,128]{2,1,0:T(1,128)S(1)}, u32[]{:S(2)}, u32[]{:S(2)}) async-start(f32[32,1,128]{2,1,0:T(1,128)} %bitcast.4), calls=%async_computation.1 | async-start | bytes 32768 | tf_op jit(solution)/shard_map/all_to_all | solution.py:335
  63.7 7.6 %collective-permute-start.5 = (f32[256,256]{1,0:T(8,128)S(1)}, f32[256,256]{1,0:T(8,128)S(1)}, u32[]{:S(2)}, u32[]{:S(2)}) collective-permute-start(f32[256,256]{1,0:T(8,128)S(1)} %get-tuple-element.26), channel_id=1, source_target_pairs={{0,1},{1,0},{2,3},{3,2},{4,5},{5,4},{6,7},{7,6},{8,9},{9,8},{10,11... | collective-permute-start | bytes 786440 | tf_op jit(solution)/shard_map/ppermute | solution.py:31

commit v11 on v10

--- a/solution.py
+++ b/solution.py
@@ -138,7 +138,7 @@
     }
 
 
-def norm_kernel(own, two, norm):
+def norm_kernel(own, norm):
     order = own.shape[-1]
     tiles = {(0, slot): own[slot * order : (slot + 1) * order] for slot in range(SLOTS)}
     norm[...] = jnp.full(norm.shape, squared_norm(tiles), jnp.float32)
@@ -222,11 +222,11 @@
     norm = pl.pallas_call(
         norm_kernel,
         out_shape=lines,
-        in_specs=[VMEM] * 2,
+        in_specs=[VMEM],
         out_specs=VMEM,
         compiler_params=pltpu.CompilerParams(vmem_limit_bytes=2 * MIB),
         cost_estimate=pl.CostEstimate(flops=SPREAD_COST, bytes_accessed=0, transcendentals=0),
-    )(own, two)
+    )(own)
     near = pl.pallas_call(
         near_kernel,
         out_shape=[tiles, jax.ShapeDtypeStruct((MARKS, order), jnp.float32)],

time: 72.6 us -> 71.8 us (0.989)
  starting transfers between devices: 51.4 us -> 50.6 us
    all_to_all x1, starting transfers between devices: 20.3 us -> 19 us  [body(): lax.all_to_all(pay, OUTER, 0, 0, tiled=True)]
where the time goes in v11:
time: 71.8 us; the launch traced here: 71.4 us
  starting transfers between devices  50.6 us (70%)
  waiting for transfers between devices  13.1 us (18%)
  Pallas kernels  6.97 us (10%)
  between operations  0.77 us (1%)
    ppermute x6, starting transfers between devices, permute(): lax.ppermute(value, AXES, [move for move in moves if 0 <= move[1] < count])  25.5 us
    all_to_all x1, starting transfers between devices, body(): lax.all_to_all(pay, OUTER, 0, 0, tiled=True)  19 us
    all_to_all x1, waiting for transfers between devices, body(): lax.all_to_all(pay, OUTER, 0, 0, tiled=True)  7.86 us
    all_to_all x1, starting transfers between devices, body(): gathered = lax.all_to_all(part, INNER, 0, 0, tiled=True)  6.1 us
    all_to_all x1, waiting for transfers between devices, body(): gathered = lax.all_to_all(part, INNER, 0, 0, tiled=True)  3.52 us
    ppermute x6, waiting for transfers between devices, permute(): lax.ppermute(value, AXES, [move for move in moves if 0 <= move[1] < count])  1.69 us
    pallas_call x1, Pallas kernels, first_step(): pl.pallas_call(first_kernel, out_shape=[tiles, jax.ShapeDtypeStruct((lax....  1.45 us
  transfers between devices with their start and end apart: 8, of which 3 were waited for; matrix products, arithmetic and copies ran while one was open for 0% of the time, Pallas kernels for 5%

profile of v11, /device:TPU:1, one launch (start us, length us, event | category | flops | bytes accessed | tf_op | source)
XLA Modules:
  0.0 71.4 jit_solution(841667587570545700)
XLA Ops:
  0.6 1.2 %shard_map.41 = (f32[776,256]{1,0:T(8,128)S(1)}, f32[2,256,256]{2,1,0:T(8,128)S(1)}, f32[256,256]{1,0:T(8,128)S(1)}) custom-call(s32[1,3]{1,0:T(1,128)} %refs_0_.1, f32[1,3,256,256]{3,2,1,0:T(8,128)} %refs_1_.1), custom_call_target="tpu_custom_call" | custom-call | bytes 2359296 | tf_op jit(solution)/shard_map/pallas_call | solution.py:113
  1.8 1.3 %collective-permute-start.2 = (f32[256,256]{1,0:T(8,128)S(1)}, f32[256,256]{1,0:T(8,128)S(1)}, u32[]{:S(2)}, u32[]{:S(2)}) collective-permute-start(f32[256,256]{1,0:T(8,128)S(1)} %get-tuple-element.19), channel_id=1, source_target_pairs={{0,2},{2,4},{3,1},{4,6},{5,3},{6,8},{7,5},{8,10},{9,7},{10,12},{11... | collective-permute-start | bytes 786440 | tf_op jit(solution)/shard_map/ppermute | solution.py:31
  3.1 6.8 %collective-permute-start.1 = (f32[2,256,256]{2,1,0:T(8,128)S(1)}, f32[2,256,256]{2,1,0:T(8,128)S(1)}, u32[]{:S(2)}, u32[]{:S(2)}) collective-permute-start(f32[2,256,256]{2,1,0:T(8,128)S(1)} %get-tuple-element.18), channel_id=1, source_target_pairs={{1,2},{2,1},{3,4},{4,3},{5,6},{6,5},{7,8},{8,7},{9,10},{10,9},{11,... | collective-permute-start | bytes 1572872 | tf_op jit(solution)/shard_map/ppermute | solution.py:31
  9.9 10.0 %collective-permute-start = (f32[776,256]{1,0:T(8,128)S(1)}, f32[776,256]{1,0:T(8,128)S(1)}, u32[]{:S(2)}, u32[]{:S(2)}) collective-permute-start(f32[776,256]{1,0:T(8,128)S(1)} %get-tuple-element.15.own), channel_id=1, source_target_pairs={{0,1},{1,0},{2,3},{3,2},{4,5},{5,4},{6,7},{7,6},{8,9},{9,8},{10,11... | collective-permute-start | bytes 2383880 | tf_op jit(solution)/shard_map/ppermute | solution.py:31
  19.9 0.2 shard_map.42.norm
  20.1 1.7 %collective-permute-done.partner = f32[776,256]{1,0:T(8,128)S(1)} collective-permute-done((f32[776,256]{1,0:T(8,128)S(1)}, f32[776,256]{1,0:T(8,128)S(1)}, u32[]{:S(2)}, u32[]{:S(2)}) %collective-permute-start) | collective-permute-done | bytes 794656 | tf_op jit(solution)/shard_map/ppermute | solution.py:31
  21.8 0.7 shard_map.43
  22.5 0.0 collective-permute-done.2.one
  22.5 0.0 collective-permute-done.1.two
  22.5 1.4 %shard_map.44 = (f32[3,256,256]{2,1,0:T(8,128)S(1)}, f32[32,128]{1,0:T(8,128)}) custom-call(f32[776,256]{1,0:T(8,128)S(1)} %get-tuple-element.15.own, f32[776,256]{1,0:T(8,128)S(1)} %collective-permute-done.partner, f32[3,256,256]{2,1,0:T(8,128)S(1)} %get-tuple-element.16.base, f32[8,256]{1,0:T(8,128)S(1)} %get-tuple-element.22.marks, ...), custom_call_target="tpu_custom_call" | custom-call | flops 503316480 | bytes 3145728 | tf_op jit(solution)/shard_map/pallas_call | solution.py:238
  24.0 19.0 %all-to-all-start = ((f32[32,1,128]{2,1,0:T(1,128)}), f32[32,1,128]{2,1,0:T(1,128)S(1)}, u32[]{:S(2)}, u32[]{:S(2)}) async-start(f32[32,1,128]{2,1,0:T(1,128)} %bitcast.1), calls=%async_computation | async-start | bytes 32768 | tf_op jit(solution)/shard_map/all_to_all | solution.py:332
  43.0 1.9 %collective-permute-start.4 = (f32[3,256,256]{2,1,0:T(8,128)S(1)}, f32[3,256,256]{2,1,0:T(8,128)S(1)}, u32[]{:S(2)}, u32[]{:S(2)}) collective-permute-start(f32[3,256,256]{2,1,0:T(8,128)S(1)} %get-tuple-element.20.own), channel_id=1, source_target_pairs={{1,2},{2,1},{3,4},{4,3},{5,6},{6,5},{7,8},{8,7},{9,10},{10,9},{11,... | collective-permute-start | bytes 2359304 | tf_op jit(solution)/shard_map/ppermute | solution.py:31
  44.9 1.9 %collective-permute-start.3 = (f32[3,256,256]{2,1,0:T(8,128)S(1)}, f32[3,256,256]{2,1,0:T(8,128)S(1)}, u32[]{:S(2)}, u32[]{:S(2)}) collective-permute-start(f32[3,256,256]{2,1,0:T(8,128)S(1)} %get-tuple-element.20.own), channel_id=1, source_target_pairs={{0,1},{1,0},{2,3},{3,2},{4,5},{5,4},{6,7},{7,6},{8,9},{9,8},{10,11... | collective-permute-start | bytes 2359304 | tf_op jit(solution)/shard_map/ppermute | solution.py:31
  46.9 7.9 %all-to-all-done = f32[32,1,128]{2,1,0:T(1,128)S(1)} async-done(((f32[32,1,128]{2,1,0:T(1,128)}), f32[32,1,128]{2,1,0:T(1,128)S(1)}, u32[]{:S(2)}, u32[]{:S(2)}) %all-to-all-start) | async-done | bytes 16416 | tf_op jit(solution)/shard_map/all_to_all | solution.py:332
  54.7 0.6 shard_map.46
  55.3 6.1 %all-to-all-start.1 = ((f32[32,1,128]{2,1,0:T(1,128)}), f32[32,1,128]{2,1,0:T(1,128)S(1)}, u32[]{:S(2)}, u32[]{:S(2)}) async-start(f32[32,1,128]{2,1,0:T(1,128)} %bitcast.4), calls=%async_computation.1 | async-start | bytes 32768 | tf_op jit(solution)/shard_map/all_to_all | solution.py:335
  61.4 0.0 collective-permute-done.3.partner
  61.5 0.7 shard_map.45.base
  62.2 0.0 collective-permute-done.4.far
  62.2 0.7 shard_map.47
  62.9 3.6 %collective-permute-start.5 = (f32[256,256]{1,0:T(8,128)S(1)}, f32[256,256]{1,0:T(8,128)S(1)}, u32[]{:S(2)}, u32[]{:S(2)}) collective-permute-start(f32[256,256]{1,0:T(8,128)S(1)} %get-tuple-element.26), channel_id=1, source_target_pairs={{0,1},{1,0},{2,3},{3,2},{4,5},{5,4},{6,7},{7,6},{8,9},{9,8},{10,11... | collective-permute-start | bytes 786440 | tf_op jit(solution)/shard_map/ppermute | solution.py:31
  66.5 3.5 %all-to-all-done.1 = f32[32,1,128]{2,1,0:T(1,128)S(1)} async-done(((f32[32,1,128]{2,1,0:T(1,128)}), f32[32,1,128]{2,1,0:T(1,128)S(1)}, u32[]{:S(2)}, u32[]{:S(2)}) %all-to-all-start.1) | async-done | bytes 16416 | tf_op jit(solution)/shard_map/all_to_all | solution.py:335
  70.0 0.5 shard_map.48
  70.5 0.0 collective-permute-done.5.received
  70.5 0.9 %shard_map.49 = f32[3,256,256]{2,1,0:T(8,128)} custom-call(f32[2,256,256]{2,1,0:T(8,128)S(1)} %get-tuple-element.25.kept, f32[256,256]{1,0:T(8,128)S(1)} %collective-permute-done.5.received), custom_call_target="tpu_custom_call" | custom-call | bytes 1572864 | tf_op jit(solution)/shard_map/pallas_call | solution.py:286
Async XLA Ops:
  1.8 20.7 %collective-permute-start.2 = (f32[256,256]{1,0:T(8,128)S(1)}, f32[256,256]{1,0:T(8,128)S(1)}, u32[]{:S(2)}, u32[]{:S(2)}) collective-permute-start(f32[256,256]{1,0:T(8,128)S(1)} %get-tuple-element.19), channel_id=1, source_target_pairs={{0,2},{2,4},{3,1},{4,6},{5,3},{6,8},{7,5},{8,10},{9,7},{10,12},{11... | collective-permute-start | bytes 786440 | tf_op jit(solution)/shard_map/ppermute | solution.py:31
  3.1 19.4 %collective-permute-start.1 = (f32[2,256,256]{2,1,0:T(8,128)S(1)}, f32[2,256,256]{2,1,0:T(8,128)S(1)}, u32[]{:S(2)}, u32[]{:S(2)}) collective-permute-start(f32[2,256,256]{2,1,0:T(8,128)S(1)} %get-tuple-element.18), channel_id=1, source_target_pairs={{1,2},{2,1},{3,4},{4,3},{5,6},{6,5},{7,8},{8,7},{9,10},{10,9},{11,... | collective-permute-start | bytes 1572872 | tf_op jit(solution)/shard_map/ppermute | solution.py:31
  9.9 11.9 %collective-permute-start = (f32[776,256]{1,0:T(8,128)S(1)}, f32[776,256]{1,0:T(8,128)S(1)}, u32[]{:S(2)}, u32[]{:S(2)}) collective-permute-start(f32[776,256]{1,0:T(8,128)S(1)} %get-tuple-element.15.own), channel_id=1, source_target_pairs={{0,1},{1,0},{2,3},{3,2},{4,5},{5,4},{6,7},{7,6},{8,9},{9,8},{10,11... | collective-permute-start | bytes 2383880 | tf_op jit(solution)/shard_map/ppermute | solution.py:31
  24.0 30.7 %all-to-all-start = ((f32[32,1,128]{2,1,0:T(1,128)}), f32[32,1,128]{2,1,0:T(1,128)S(1)}, u32[]{:S(2)}, u32[]{:S(2)}) async-start(f32[32,1,128]{2,1,0:T(1,128)} %bitcast.1), calls=%async_computation | async-start | bytes 32768 | tf_op jit(solution)/shard_map/all_to_all | solution.py:332
  43.0 19.2 %collective-permute-start.4 = (f32[3,256,256]{2,1,0:T(8,128)S(1)}, f32[3,256,256]{2,1,0:T(8,128)S(1)}, u32[]{:S(2)}, u32[]{:S(2)}) collective-permute-start(f32[3,256,256]{2,1,0:T(8,128)S(1)} %get-tuple-element.20.own), channel_id=1, source_target_pairs={{1,2},{2,1},{3,4},{4,3},{5,6},{6,5},{7,8},{8,7},{9,10},{10,9},{11,... | collective-permute-start | bytes 2359304 | tf_op jit(solution)/shard_map/ppermute | solution.py:31
  44.9 16.5 %collective-permute-start.3 = (f32[3,256,256]{2,1,0:T(8,128)S(1)}, f32[3,256,256]{2,1,0:T(8,128)S(1)}, u32[]{:S(2)}, u32[]{:S(2)}) collective-permute-start(f32[3,256,256]{2,1,0:T(8,128)S(1)} %get-tuple-element.20.own), channel_id=1, source_target_pairs={{0,1},{1,0},{2,3},{3,2},{4,5},{5,4},{6,7},{7,6},{8,9},{9,8},{10,11... | collective-permute-start | bytes 2359304 | tf_op jit(solution)/shard_map/ppermute | solution.py:31
  55.3 14.7 %all-to-all-start.1 = ((f32[32,1,128]{2,1,0:T(1,128)}), f32[32,1,128]{2,1,0:T(1,128)S(1)}, u32[]{:S(2)}, u32[]{:S(2)}) async-start(f32[32,1,128]{2,1,0:T(1,128)} %bitcast.4), calls=%async_computation.1 | async-start | bytes 32768 | tf_op jit(solution)/shard_map/all_to_all | solution.py:335
  62.9 7.6 %collective-permute-start.5 = (f32[256,256]{1,0:T(8,128)S(1)}, f32[256,256]{1,0:T(8,128)S(1)}, u32[]{:S(2)}, u32[]{:S(2)}) collective-permute-start(f32[256,256]{1,0:T(8,128)S(1)} %get-tuple-element.26), channel_id=1, source_target_pairs={{0,1},{1,0},{2,3},{3,2},{4,5},{5,4},{6,7},{7,6},{8,9},{9,8},{10,11... | collective-permute-start | bytes 786440 | tf_op jit(solution)/shard_map/ppermute | solution.py:31

commit v12 on v11

--- a/solution.py
+++ b/solution.py
@@ -10,8 +10,8 @@
 SLOTS = 3
 SPAN = SLOTS - 1
 AXES = ("z", "x", "y", "core")
-INNER = ("x", "y")
-OUTER = ("z", "core")
+INNER = ("z", "core")
+OUTER = ("x", "y")
 LANES = 128
 MARKS = 8
 MIB = 1024 * 1024

time: 71.8 us -> 72.6 us (1.011)
  starting transfers between devices: 50.6 us -> 52.7 us
  waiting for transfers between devices: 13.1 us -> 11.8 us
    all_to_all x1, starting transfers between devices: 6.1 us -> 21 us  [body(): gathered = lax.all_to_all(part, INNER, 0, 0, tiled=True)]
    all_to_all x1, starting transfers between devices: 19 us -> 4.86 us  [body(): lax.all_to_all(pay, OUTER, 0, 0, tiled=True)]
    all_to_all x1, waiting for transfers between devices: 7.86 us -> 2.43 us  [body(): lax.all_to_all(pay, OUTER, 0, 0, tiled=True)]
    all_to_all x1, waiting for transfers between devices: 3.52 us -> 7.67 us  [body(): gathered = lax.all_to_all(part, INNER, 0, 0, tiled=True)]
    ppermute x6, starting transfers between devices: 25.5 us -> 26.8 us  [permute(): lax.ppermute(value, AXES, [move for move in moves if 0 <= move[1] < count])]
where the time goes in v12:
time: 72.6 us; the launch traced here: 72.2 us
  starting transfers between devices  52.7 us (73%)
  waiting for transfers between devices  11.8 us (16%)
  Pallas kernels  6.97 us (10%)
  between operations  0.77 us (1%)
    ppermute x6, starting transfers between devices, permute(): lax.ppermute(value, AXES, [move for move in moves if 0 <= move[1] < count])  26.8 us
    all_to_all x1, starting transfers between devices, body(): gathered = lax.all_to_all(part, INNER, 0, 0, tiled=True)  21 us
    all_to_all x1, waiting for transfers between devices, body(): gathered = lax.all_to_all(part, INNER, 0, 0, tiled=True)  7.67 us
    all_to_all x1, starting transfers between devices, body(): lax.all_to_all(pay, OUTER, 0, 0, tiled=True)  4.86 us
    all_to_all x1, waiting for transfers between devices, body(): lax.all_to_all(pay, OUTER, 0, 0, tiled=True)  2.43 us
    ppermute x6, waiting for transfers between devices, permute(): lax.ppermute(value, AXES, [move for move in moves if 0 <= move[1] < count])  1.69 us
  transfers between devices with their start and end apart: 8, of which 3 were waited for; matrix products, arithmetic and copies ran while one was open for 0% of the time, Pallas kernels for 5%

profile of v12, /device:TPU:1, one launch (start us, length us, event | category | flops | bytes accessed | tf_op | source)
XLA Modules:
  0.0 72.2 jit_solution(12294485016465621667)
XLA Ops:
  0.6 1.2 %shard_map.41 = (f32[776,256]{1,0:T(8,128)S(1)}, f32[2,256,256]{2,1,0:T(8,128)S(1)}, f32[256,256]{1,0:T(8,128)S(1)}) custom-call(s32[1,3]{1,0:T(1,128)} %refs_0_.1, f32[1,3,256,256]{3,2,1,0:T(8,128)} %refs_1_.1), custom_call_target="tpu_custom_call" | custom-call | bytes 2359296 | tf_op jit(solution)/shard_map/pallas_call | solution.py:113
  1.8 1.3 %collective-permute-start.2 = (f32[256,256]{1,0:T(8,128)S(1)}, f32[256,256]{1,0:T(8,128)S(1)}, u32[]{:S(2)}, u32[]{:S(2)}) collective-permute-start(f32[256,256]{1,0:T(8,128)S(1)} %get-tuple-element.19), channel_id=1, source_target_pairs={{0,2},{2,4},{3,1},{4,6},{5,3},{6,8},{7,5},{8,10},{9,7},{10,12},{11... | collective-permute-start | bytes 786440 | tf_op jit(solution)/shard_map/ppermute | solution.py:31
  3.1 6.8 %collective-permute-start.1 = (f32[2,256,256]{2,1,0:T(8,128)S(1)}, f32[2,256,256]{2,1,0:T(8,128)S(1)}, u32[]{:S(2)}, u32[]{:S(2)}) collective-permute-start(f32[2,256,256]{2,1,0:T(8,128)S(1)} %get-tuple-element.18), channel_id=1, source_target_pairs={{1,2},{2,1},{3,4},{4,3},{5,6},{6,5},{7,8},{8,7},{9,10},{10,9},{11,... | collective-permute-start | bytes 1572872 | tf_op jit(solution)/shard_map/ppermute | solution.py:31
  9.9 10.0 %collective-permute-start = (f32[776,256]{1,0:T(8,128)S(1)}, f32[776,256]{1,0:T(8,128)S(1)}, u32[]{:S(2)}, u32[]{:S(2)}) collective-permute-start(f32[776,256]{1,0:T(8,128)S(1)} %get-tuple-element.15.own), channel_id=1, source_target_pairs={{0,1},{1,0},{2,3},{3,2},{4,5},{5,4},{6,7},{7,6},{8,9},{9,8},{10,11... | collective-permute-start | bytes 2383880 | tf_op jit(solution)/shard_map/ppermute | solution.py:31
  19.9 0.2 shard_map.42.norm
  20.1 1.7 %collective-permute-done.partner = f32[776,256]{1,0:T(8,128)S(1)} collective-permute-done((f32[776,256]{1,0:T(8,128)S(1)}, f32[776,256]{1,0:T(8,128)S(1)}, u32[]{:S(2)}, u32[]{:S(2)}) %collective-permute-start) | collective-permute-done | bytes 794656 | tf_op jit(solution)/shard_map/ppermute | solution.py:31
  21.8 0.7 shard_map.43
  22.5 0.0 collective-permute-done.2.one
  22.5 0.0 collective-permute-done.1.two
  22.5 1.4 %shard_map.44 = (f32[3,256,256]{2,1,0:T(8,128)S(1)}, f32[32,128]{1,0:T(8,128)}) custom-call(f32[776,256]{1,0:T(8,128)S(1)} %get-tuple-element.15.own, f32[776,256]{1,0:T(8,128)S(1)} %collective-permute-done.partner, f32[3,256,256]{2,1,0:T(8,128)S(1)} %get-tuple-element.16.base, f32[8,256]{1,0:T(8,128)S(1)} %get-tuple-element.22.marks, ...), custom_call_target="tpu_custom_call" | custom-call | flops 503316480 | bytes 3145728 | tf_op jit(solution)/shard_map/pallas_call | solution.py:238
  24.0 4.9 %all-to-all-start = ((f32[32,1,128]{2,1,0:T(1,128)}), f32[32,1,128]{2,1,0:T(1,128)S(1)}, u32[]{:S(2)}, u32[]{:S(2)}) async-start(f32[32,1,128]{2,1,0:T(1,128)} %bitcast.1), calls=%async_computation | async-start | bytes 32768 | tf_op jit(solution)/shard_map/all_to_all | solution.py:332
  28.8 4.2 %collective-permute-start.4 = (f32[3,256,256]{2,1,0:T(8,128)S(1)}, f32[3,256,256]{2,1,0:T(8,128)S(1)}, u32[]{:S(2)}, u32[]{:S(2)}) collective-permute-start(f32[3,256,256]{2,1,0:T(8,128)S(1)} %get-tuple-element.20.own), channel_id=1, source_target_pairs={{1,2},{2,1},{3,4},{4,3},{5,6},{6,5},{7,8},{8,7},{9,10},{10,9},{11,... | collective-permute-start | bytes 2359304 | tf_op jit(solution)/shard_map/ppermute | solution.py:31
  33.0 1.9 %collective-permute-start.3 = (f32[3,256,256]{2,1,0:T(8,128)S(1)}, f32[3,256,256]{2,1,0:T(8,128)S(1)}, u32[]{:S(2)}, u32[]{:S(2)}) collective-permute-start(f32[3,256,256]{2,1,0:T(8,128)S(1)} %get-tuple-element.20.own), channel_id=1, source_target_pairs={{0,1},{1,0},{2,3},{3,2},{4,5},{5,4},{6,7},{7,6},{8,9},{9,8},{10,11... | collective-permute-start | bytes 2359304 | tf_op jit(solution)/shard_map/ppermute | solution.py:31
  35.0 2.4 %all-to-all-done = f32[32,1,128]{2,1,0:T(1,128)S(1)} async-done(((f32[32,1,128]{2,1,0:T(1,128)}), f32[32,1,128]{2,1,0:T(1,128)S(1)}, u32[]{:S(2)}, u32[]{:S(2)}) %all-to-all-start) | async-done | bytes 16416 | tf_op jit(solution)/shard_map/all_to_all | solution.py:332
  37.4 0.6 shard_map.46
  38.0 21.0 %all-to-all-start.1 = ((f32[32,1,128]{2,1,0:T(1,128)}), f32[32,1,128]{2,1,0:T(1,128)S(1)}, u32[]{:S(2)}, u32[]{:S(2)}) async-start(f32[32,1,128]{2,1,0:T(1,128)} %bitcast.4), calls=%async_computation.1 | async-start | bytes 32768 | tf_op jit(solution)/shard_map/all_to_all | solution.py:335
  59.0 0.0 collective-permute-done.3.partner
  59.1 0.7 shard_map.45.base
  59.8 0.0 collective-permute-done.4.far
  59.8 0.7 shard_map.47
  60.5 2.6 %collective-permute-start.5 = (f32[256,256]{1,0:T(8,128)S(1)}, f32[256,256]{1,0:T(8,128)S(1)}, u32[]{:S(2)}, u32[]{:S(2)}) collective-permute-start(f32[256,256]{1,0:T(8,128)S(1)} %get-tuple-element.26), channel_id=1, source_target_pairs={{0,1},{1,0},{2,3},{3,2},{4,5},{5,4},{6,7},{7,6},{8,9},{9,8},{10,11... | collective-permute-start | bytes 786440 | tf_op jit(solution)/shard_map/ppermute | solution.py:31
  63.1 7.7 %all-to-all-done.1 = f32[32,1,128]{2,1,0:T(1,128)S(1)} async-done(((f32[32,1,128]{2,1,0:T(1,128)}), f32[32,1,128]{2,1,0:T(1,128)S(1)}, u32[]{:S(2)}, u32[]{:S(2)}) %all-to-all-start.1) | async-done | bytes 16416 | tf_op jit(solution)/shard_map/all_to_all | solution.py:335
  70.8 0.5 shard_map.48
  71.3 0.0 collective-permute-done.5.received
  71.3 0.9 %shard_map.49 = f32[3,256,256]{2,1,0:T(8,128)} custom-call(f32[2,256,256]{2,1,0:T(8,128)S(1)} %get-tuple-element.25.kept, f32[256,256]{1,0:T(8,128)S(1)} %collective-permute-done.5.received), custom_call_target="tpu_custom_call" | custom-call | bytes 1572864 | tf_op jit(solution)/shard_map/pallas_call | solution.py:286
Async XLA Ops:
  1.8 20.7 %collective-permute-start.2 = (f32[256,256]{1,0:T(8,128)S(1)}, f32[256,256]{1,0:T(8,128)S(1)}, u32[]{:S(2)}, u32[]{:S(2)}) collective-permute-start(f32[256,256]{1,0:T(8,128)S(1)} %get-tuple-element.19), channel_id=1, source_target_pairs={{0,2},{2,4},{3,1},{4,6},{5,3},{6,8},{7,5},{8,10},{9,7},{10,12},{11... | collective-permute-start | bytes 786440 | tf_op jit(solution)/shard_map/ppermute | solution.py:31
  3.1 19.4 %collective-permute-start.1 = (f32[2,256,256]{2,1,0:T(8,128)S(1)}, f32[2,256,256]{2,1,0:T(8,128)S(1)}, u32[]{:S(2)}, u32[]{:S(2)}) collective-permute-start(f32[2,256,256]{2,1,0:T(8,128)S(1)} %get-tuple-element.18), channel_id=1, source_target_pairs={{1,2},{2,1},{3,4},{4,3},{5,6},{6,5},{7,8},{8,7},{9,10},{10,9},{11,... | collective-permute-start | bytes 1572872 | tf_op jit(solution)/shard_map/ppermute | solution.py:31
  9.9 11.9 %collective-permute-start = (f32[776,256]{1,0:T(8,128)S(1)}, f32[776,256]{1,0:T(8,128)S(1)}, u32[]{:S(2)}, u32[]{:S(2)}) collective-permute-start(f32[776,256]{1,0:T(8,128)S(1)} %get-tuple-element.15.own), channel_id=1, source_target_pairs={{0,1},{1,0},{2,3},{3,2},{4,5},{5,4},{6,7},{7,6},{8,9},{9,8},{10,11... | collective-permute-start | bytes 2383880 | tf_op jit(solution)/shard_map/ppermute | solution.py:31
  24.0 13.4 %all-to-all-start = ((f32[32,1,128]{2,1,0:T(1,128)}), f32[32,1,128]{2,1,0:T(1,128)S(1)}, u32[]{:S(2)}, u32[]{:S(2)}) async-start(f32[32,1,128]{2,1,0:T(1,128)} %bitcast.1), calls=%async_computation | async-start | bytes 32768 | tf_op jit(solution)/shard_map/all_to_all | solution.py:332
  28.8 30.9 %collective-permute-start.4 = (f32[3,256,256]{2,1,0:T(8,128)S(1)}, f32[3,256,256]{2,1,0:T(8,128)S(1)}, u32[]{:S(2)}, u32[]{:S(2)}) collective-permute-start(f32[3,256,256]{2,1,0:T(8,128)S(1)} %get-tuple-element.20.own), channel_id=1, source_target_pairs={{1,2},{2,1},{3,4},{4,3},{5,6},{6,5},{7,8},{8,7},{9,10},{10,9},{11,... | collective-permute-start | bytes 2359304 | tf_op jit(solution)/shard_map/ppermute | solution.py:31
  33.0 26.0 %collective-permute-start.3 = (f32[3,256,256]{2,1,0:T(8,128)S(1)}, f32[3,256,256]{2,1,0:T(8,128)S(1)}, u32[]{:S(2)}, u32[]{:S(2)}) collective-permute-start(f32[3,256,256]{2,1,0:T(8,128)S(1)} %get-tuple-element.20.own), channel_id=1, source_target_pairs={{0,1},{1,0},{2,3},{3,2},{4,5},{5,4},{6,7},{7,6},{8,9},{9,8},{10,11... | collective-permute-start | bytes 2359304 | tf_op jit(solution)/shard_map/ppermute | solution.py:31
  38.0 32.7 %all-to-all-start.1 = ((f32[32,1,128]{2,1,0:T(1,128)}), f32[32,1,128]{2,1,0:T(1,128)S(1)}, u32[]{:S(2)}, u32[]{:S(2)}) async-start(f32[32,1,128]{2,1,0:T(1,128)} %bitcast.4), calls=%async_computation.1 | async-start | bytes 32768 | tf_op jit(solution)/shard_map/all_to_all | solution.py:335
  60.5 10.8 %collective-permute-start.5 = (f32[256,256]{1,0:T(8,128)S(1)}, f32[256,256]{1,0:T(8,128)S(1)}, u32[]{:S(2)}, u32[]{:S(2)}) collective-permute-start(f32[256,256]{1,0:T(8,128)S(1)} %get-tuple-element.26), channel_id=1, source_target_pairs={{0,1},{1,0},{2,3},{3,2},{4,5},{5,4},{6,7},{7,6},{8,9},{9,8},{10,11... | collective-permute-start | bytes 786440 | tf_op jit(solution)/shard_map/ppermute | solution.py:31
